TPU v7x, 256 devices: a whole 4x4x8 slice. The times are simulated.
256 devices in a mesh: seg: 64 (over y, z, core), ch: 4 (over x).
Axes of the slice: x: 4, y: 4, z: 8, core: 2. Of those that a mesh axis runs over, the one named last changes fastest.
Arguments:
- voxels: bfloat16 [65536, 256], P('seg'), may hold values from -6 to 6
- neighbours: int32 [27, 65536], P(None, 'seg'), may hold values from -1 to 65535, as said below
- send_perm: int32 [64, 1024], P('seg'), may hold values from 0 to 1023, each once within a row
- send_counts: int32 [64, 64], replicated, may hold values from 0 to 32, as said below
- conv_weight: bfloat16 [27, 256, 256], P(None, None, 'ch'), may hold values from -0.078125 to 0.078125
- qkv_first: bfloat16 [256, 3, 256], P(None, None, 'ch'), may hold values from -3 to 3
- out_first: bfloat16 [256, 256], replicated, may hold values from -0.375 to 0.375
- qkv_second: bfloat16 [256, 3, 256], P(None, None, 'ch'), may hold values from -3 to 3
- out_second: bfloat16 [256, 256], replicated, may hold values from -0.375 to 0.375
Outputs:
- encoded: bfloat16 [65536, 256], P('seg', 'ch')
Inputs may be any that keep to these rules, and one draw needn't show every extreme that they name: `neighbours`: -1 marks an absent neighbour; any other entry is a voxel within 128 positions of the entry's own voxel along the z-order curve, and the middle offset is the voxel itself. `send_counts`: each row sums to 1024; some Hilbert segment receives exactly 32 voxels from every z-order segment.
All inputs are finite; a program needn't handle non-finite values.
Results may differ from a plain program's by a relative error of at most 0.02.
Values may be sent and summed in bfloat16 or wider, within the bound.
No kernel may reach another device: no remote copies, remote signals or barrier semaphores. Data moves between devices by JAX's collectives and lax.ppermute only.
A program may use at most 64 MiB of HBM per device.

v0:
```python
import jax
import jax.numpy as jnp
from jax import lax
from jax.sharding import PartitionSpec as P

HD = 16
PATCH = 1024
KOFF = 27
HALO = 128


NORM_EPS = 1e-05
MASKED_SCORE = -1e30


def extended(cells, sides, width):
    for axis, dim in sides:
        count = lax.axis_size(axis)
        ends = count - 1
        head = lax.slice_in_dim(cells, 0, width, axis=dim)
        tail = lax.slice_in_dim(cells, cells.shape[dim] - width, cells.shape[dim], axis=dim)
        cells = jnp.concatenate(
            [
                lax.ppermute(tail, axis, [(i, (i + 1) % count) for i in range(ends)]),
                cells,
                lax.ppermute(head, axis, [((i + 1) % count, i) for i in range(ends)]),
            ],
            axis=dim,
        )
    return cells


def layer_norm(rows_in):
    values32 = rows_in.astype(jnp.float32)
    centre = values32 - jnp.mean(values32, axis=-1, keepdims=True)
    spread = jnp.mean(centre * centre, axis=-1, keepdims=True)
    return (centre * lax.rsqrt(spread + NORM_EPS)).astype(jnp.bfloat16)


def project(normed, weight):
    width_in, stacked, local_cols = weight.shape
    product = jnp.dot(
        normed, weight.reshape(width_in, stacked * local_cols), preferred_element_type=jnp.float32
    )
    return product.astype(jnp.bfloat16).reshape(normed.shape[0], stacked, local_cols // HD, HD)


def patch_attention(qkv_rows, key_live):
    count_rows, stacked, head_count, head_dim = qkv_rows.shape
    query_rows = min(512, PATCH)
    score_scale = head_dim ** (-0.5)
    grouped = qkv_rows.reshape(count_rows // PATCH, PATCH, stacked, head_count, head_dim)
    masks = key_live.reshape(count_rows // PATCH, PATCH)

    def one_patch(packed_item):
        patch_rows, live_keys = packed_item
        key_rows = patch_rows[:, 1]
        value_rows = patch_rows[:, 2]
        query_blocks = patch_rows[:, 0].reshape(
            PATCH // query_rows, query_rows, head_count, head_dim
        )

        def one_block(query_block):
            scores = (
                jnp.einsum(
                    "qhd,khd->hqk", query_block, key_rows, preferred_element_type=jnp.float32
                )
                * score_scale
            )
            scores = jnp.where(live_keys[None, None, :], scores, MASKED_SCORE)
            peak = jnp.max(scores, axis=2, keepdims=True)
            powered = jnp.exp(scores - peak)
            normaliser = jnp.sum(powered, axis=2)
            blended = jnp.einsum(
                "hqk,khd->qhd",
                powered.astype(jnp.bfloat16),
                value_rows,
                preferred_element_type=jnp.float32,
            )
            return (blended / jnp.transpose(normaliser)[:, :, None]).astype(jnp.bfloat16)

        return lax.map(one_block, query_blocks).reshape(PATCH, head_count * head_dim)

    return lax.map(one_patch, (grouped, masks)).reshape(count_rows, head_count * head_dim)


def local(
    voxels,
    neighbours,
    send_perm,
    send_counts,
    conv_weight,
    qkv_first,
    out_first,
    qkv_second,
    out_second,
):
    seg_index = lax.axis_index("seg")
    seg_count = lax.axis_size("seg")
    ch_index = lax.axis_index("ch")
    rows_dev, channels = voxels.shape
    quarter = conv_weight.shape[2]
    bucket_rows = 2 * rows_dev // seg_count
    total_slots = seg_count * bucket_rows
    padded = extended(voxels, (("seg", 0),), HALO)
    first_row = seg_index * rows_dev - HALO
    padded_rows = rows_dev + 2 * HALO

    def conv_step(kernel_index, running):
        target = neighbours[kernel_index]
        local_row = jnp.clip(target - first_row, 0, padded_rows - 1)
        picked = jnp.take(padded, local_row, axis=0)
        picked = jnp.where((target >= 0)[:, None], picked, jnp.zeros((), jnp.bfloat16))
        return running + jnp.dot(
            picked, conv_weight[kernel_index], preferred_element_type=jnp.float32
        )

    conv_sum = lax.fori_loop(0, KOFF, conv_step, jnp.zeros((rows_dev, quarter), jnp.float32))
    own_cols = lax.dynamic_slice_in_dim(voxels, ch_index * quarter, quarter, 1)
    mixed_a_part = (own_cols.astype(jnp.float32) + conv_sum).astype(jnp.bfloat16)
    mixed_a = lax.all_gather(mixed_a_part, "ch", axis=1, tiled=True)
    qkv_a = project(layer_norm(mixed_a), qkv_first)
    heads_a = patch_attention(qkv_a, jnp.ones((rows_dev,), bool))
    out_rows = lax.dynamic_slice_in_dim(out_first, ch_index * quarter, quarter, 0)
    partial_one = jnp.dot(heads_a, out_rows, preferred_element_type=jnp.float32)
    attn_one = lax.psum(partial_one.astype(jnp.bfloat16), "ch").astype(jnp.float32)
    mixed_b = (mixed_a.astype(jnp.float32) + attn_one).astype(jnp.bfloat16)
    mixed_b_part = lax.dynamic_slice_in_dim(mixed_b, ch_index * quarter, quarter, 1)
    counts_row = lax.dynamic_index_in_dim(send_counts, seg_index, 0, keepdims=False)
    send_off = jnp.cumsum(counts_row) - counts_row
    send_end = send_off + counts_row
    send_order = send_perm[0]
    bucket_pos = send_off[:, None] + jnp.arange(bucket_rows, dtype=jnp.int32)[None, :]
    send_rows = send_order[jnp.clip(bucket_pos, 0, rows_dev - 1)].reshape(-1)
    counts_col = lax.dynamic_index_in_dim(send_counts, seg_index, 1, keepdims=False)
    recv_off = jnp.cumsum(counts_col) - counts_col
    recv_end = recv_off + counts_col
    slots = jnp.arange(total_slots, dtype=jnp.int32)
    source = jnp.minimum(
        jnp.sum((recv_end[None, :] <= slots[:, None]).astype(jnp.int32), axis=1), seg_count - 1
    )
    within = jnp.clip(slots - recv_off[source], 0, bucket_rows - 1)
    flat_from = source * bucket_rows + within
    live_keys = slots < jnp.sum(counts_col)
    qkv_b = project(layer_norm(mixed_b), qkv_second)
    head_local = qkv_b.shape[2]
    outgoing = jnp.take(qkv_b.reshape(rows_dev, 3 * quarter), send_rows, axis=0).reshape(
        seg_count, bucket_rows, 3 * quarter
    )
    arrived = lax.all_to_all(outgoing, "seg", split_axis=0, concat_axis=0, tiled=True).reshape(
        total_slots, 3 * quarter
    )
    compact = jnp.take(arrived, flat_from, axis=0).reshape(total_slots, 3, head_local, HD)
    heads_owner = patch_attention(compact, live_keys)
    bucket_from = jnp.clip(
        recv_off[:, None] + jnp.arange(bucket_rows, dtype=jnp.int32)[None, :], 0, total_slots - 1
    ).reshape(-1)
    going_home = jnp.take(heads_owner, bucket_from, axis=0).reshape(seg_count, bucket_rows, quarter)
    returned = lax.all_to_all(going_home, "seg", split_axis=0, concat_axis=0, tiled=True).reshape(
        total_slots, quarter
    )
    inverse = (
        jnp.zeros((rows_dev,), jnp.int32).at[send_order].set(jnp.arange(rows_dev, dtype=jnp.int32))
    )
    owner_of = jnp.minimum(
        jnp.sum((send_end[None, :] <= inverse[:, None]).astype(jnp.int32), axis=1), seg_count - 1
    )
    home_from = owner_of * bucket_rows + jnp.clip(inverse - send_off[owner_of], 0, bucket_rows - 1)
    heads_b = jnp.take(returned, home_from, axis=0)
    out_rows_two = lax.dynamic_slice_in_dim(out_second, ch_index * quarter, quarter, 0)
    partial_two = jnp.dot(heads_b, out_rows_two, preferred_element_type=jnp.float32)
    attn_two = lax.psum_scatter(
        partial_two.astype(jnp.bfloat16), "ch", scatter_dimension=1, tiled=True
    ).astype(jnp.float32)
    return (mixed_b_part.astype(jnp.float32) + attn_two).astype(jnp.bfloat16)


def solution(mesh):
    placed = (
        P("seg", None),
        P(None, "seg"),
        P("seg", None),
        P(),
        P(None, None, "ch"),
        P(None, None, "ch"),
        P(),
        P(None, None, "ch"),
        P(),
    )
    return jax.shard_map(
        local, mesh=mesh, in_specs=placed, out_specs=P("seg", "ch"), check_vma=False
    )
```

profile of v0, /device:TPU:8, one launch (start us, length us, event | category | flops | bytes accessed | tf_op | source)
XLA Modules:
  0.0 519.8 jit_solution(14209222011439790130)
XLA Ops:
  7.5 7.1 %collective-permute-start.1 = (bf16[128,256]{1,0:T(8,128)(2,1)S(1)}, bf16[128,256]{1,0:T(8,128)(2,1)S(1)}, u32[]{:S(2)}, u32[]{:S(2)}) collective-permute-start(bf16[128,256]{1,0:T(8,128)(2,1)S(1)} %get-tuple-element.486), channel_id=1, source_target_pairs={{4,0},{8,4},{12,8},{16,12},{20,16},{24,20},{28,24},{32,28},{36,32}... | collective-permute-start | bytes 196616 | tf_op jit(solution)/shard_map/ppermute | solution.py:26
  14.6 1.9 collective-permute-start
  28.0 8.6 %gather_fusion.1 = s32[2048]{0:T(1024)S(1)} fusion(s32[1024]{0:T(1024)S(1)} %bitcast.276, s32[2048]{0:T(1024)S(1)} %broadcast_clamp_fusion.4), kind=kCustom, calls=%fused_computation.1 | custom fusion | bytes 24576 | tf_op jit(solution)/shard_map/gather | solution.py:134
  36.7 4.4 compare_select_fusion.9
  42.6 35.6 %select_select_fusion = s32[2048]{0:T(1024)S(1)} fusion(pred[2048]{0:T(1024)(128)(4,1)S(1)} %get-tuple-element.368, pred[2048]{0:T(1024)(128)(4,1)S(1)} %get-tuple-element.367, pred[2048]{0:T(1024)(128)(4,1)S(1)} %get-tuple-element.366, pred[2048]{0:T(1024)(128)(4,1)S(1)} %get-tuple-element.365, pred[2048]{0:T(1024)(128)(4,1)S(1)} %get-tuple-element.364, ...), kind=kLoop, calls=%fused_computation.244 | loop fusion | flops 116736 | bytes 133348 | tf_op jit(solution)/shard_map/gather | solution.py:142
  78.4 4.3 scatter_custom_fusion
  82.8 4.9 compare_select_fusion.18
  90.1 184.9 %while.55 = (s32[]{:T(128)}, f32[1024,64]{0,1:T(8,128)S(1)}, s32[27,1024]{1,0:T(8,128)}, s32[]{:T(128)}, bf16[1280,256]{1,0:T(8,128)(2,1)S(1)}, /*index=5*/bf16[27,256,64]{1,2,0:T(8,128)(2,1)}, s32[]{:T(128)}, s32[]{:T(128)}) while((s32[]{:T(128)}, f32[1024,64]{0,1:T(8,128)S(1)}, s32[27,1024]{1,0:T(8,128)}, s32[]{:T(128)}, ...), condition=%wide.region_1.2_spmd.clone, body=%wide.region_0.1_spmd.clone.sunk | while | flops 34223104 | bytes 2166903 | solution.py:118
  90.9 3.9 gather_fusion
  97.7 3.9 gather_fusion
  104.6 3.9 gather_fusion
  111.4 3.9 gather_fusion
  118.3 3.9 gather_fusion
  125.1 3.9 gather_fusion
  132.0 3.9 gather_fusion
  138.8 3.9 gather_fusion
  145.7 3.9 gather_fusion
  152.5 3.9 gather_fusion
  159.4 3.9 gather_fusion
  166.2 3.9 gather_fusion
  173.0 3.9 gather_fusion
  179.9 3.9 gather_fusion
  186.7 3.9 gather_fusion
  193.6 3.9 gather_fusion
  200.4 3.9 gather_fusion
  207.3 3.9 gather_fusion
  214.1 3.9 gather_fusion
  221.0 3.9 gather_fusion
  227.8 3.9 gather_fusion
  234.7 3.9 gather_fusion
  241.5 3.9 gather_fusion
  248.4 3.9 gather_fusion
  255.2 3.9 gather_fusion
  262.0 3.9 gather_fusion
  268.9 3.9 gather_fusion
  275.0 13.3 %all_gather.3 = bf16[1024,256]{0,1:T(8,128)(2,1)S(1)} all-gather(bf16[1024,64]{0,1:T(8,128)(2,1)S(1)} %add_convert_fusion.1), channel_id=1, replica_groups=mesh['seg'=64,'ch'=4] {'ch'}, dimensions={1}, use_global_device_ids=true | all-gather | bytes 655360 | tf_op jit(solution)/shard_map/all_gather | solution.py:121
  289.0 9.8 %while.52 = (s32[]{:T(128)}, bf16[2,512,4,16]{1,3,2,0:T(8,128)(2,1)S(1)}, bf16[2,512,4,16]{1,3,2,0:T(8,128)(2,1)S(1)}, bf16[1024,4,16]{0,2,1:T(8,128)(2,1)S(1)}, bf16[1024,4,16]{0,2,1:T(8,128)(2,1)S(1)}, /*index=5*/s32[]{:T(128)}) while((s32[]{:T(128)}, bf16[2,512,4,16]{1,3,2,0:T(8,128)(2,1)S(1)}, bf16[2,512,4,16]{1,3,2,0:T(8,128)(2,1)S(1)}, ...), condition=%wide.region_7.8_spmd, body=%wide.region_4.7_spmd.sunk | while | flops 151056384 | bytes 25600084 | solution.py:82
  290.5 1.8 fusion.125
  292.3 1.7 fusion.126
  295.3 1.8 fusion.125
  297.2 1.7 fusion.126
  301.0 45.8 %all-reduce.2.cloned.1.call-done = bf16[1024,256]{0,1:T(8,128)(2,1)} async-done(((bf16[1024,256]{0,1:T(8,128)(2,1)}), bf16[1024,256]{0,1:T(8,128)(2,1)}) %all-reduce.2.cloned.1.call-update) | async-done | bytes 524304 | tf_op jit(solution)/shard_map/psum | solution.py:126
  349.4 7.5 %gather_fusion.2 = bf16[2048,192]{1,0:T(8,128)(2,1)S(1)} fusion(bf16[1024,192]{1,0:T(8,128)(2,1)S(1)} %copy.62, s32[2048]{0:T(1024)S(1)} %broadcast_clamp_fusion.3), kind=kCustom, calls=%fused_computation.2 | custom fusion | bytes 1581056 | tf_op jit(solution)/shard_map/jit(_take)/gather | solution.py:147
  358.1 10.6 %all-to-all-start = ((bf16[64,32,192]{2,1,0:T(8,128)(2,1)}), bf16[64,32,192]{2,1,0:T(8,128)(2,1)S(1)}, u32[]{:S(2)}, u32[]{:S(2)}) async-start(bf16[64,32,192]{2,1,0:T(8,128)(2,1)} %broadcast_select_fusion.1), calls=%async_computation | async-start | bytes 2097152 | tf_op jit(solution)/shard_map/all_to_all | solution.py:150
  369.4 26.2 %all-to-all-done = bf16[64,32,192]{2,1,0:T(8,128)(2,1)S(1)} async-done(((bf16[64,32,192]{2,1,0:T(8,128)(2,1)}), bf16[64,32,192]{2,1,0:T(8,128)(2,1)S(1)}, u32[]{:S(2)}, u32[]{:S(2)}) %all-to-all-start) | async-done | bytes 786464 | tf_op jit(solution)/shard_map/all_to_all | solution.py:150
  395.6 7.5 %gather_fusion.3 = bf16[2048,192]{1,0:T(8,128)(2,1)S(1)} fusion(bf16[2048,192]{1,0:T(8,128)(2,1)S(1)} %bitcast.277, s32[2048]{0:T(1024)S(1)} %broadcast_clamp_fusion.2), kind=kCustom, calls=%fused_computation.3 | custom fusion | bytes 1581056 | tf_op jit(solution)/shard_map/jit(_take)/gather | solution.py:153
  405.5 22.2 %while.54 = (s32[]{:T(128)}, bf16[2,1024,64]{1,2,0:T(8,128)(2,1)S(1)}, bf16[2,1024,3,4,16]{1,4,3,2,0:T(8,128)(2,1)S(1)}, pred[2,1024]{1,0:T(4,128)(4,1)S(1)}, s32[]{:T(128)}, /*index=5*/s32[]{:T(128)}, s32[]{:T(128)}) while((s32[]{:T(128)}, bf16[2,1024,64]{1,2,0:T(8,128)(2,1)S(1)}, bf16[2,1024,3,4,16]{1,4,3,2,0:T(8,128)(2,1)S(1)}, ...), condition=%wide.region_22.23_spmd, body=%wide.region_17.22_spmd.sunk | while | flops 157347840 | bytes 28488956 | solution.py:84
  405.8 10.6 %while.56 = (s32[]{:T(128)}, bf16[2,512,4,16]{1,3,2,0:T(8,128)(2,1)S(1)}, pred[1024]{0:T(1024)(128)(4,1)S(1)}, bf16[2,512,4,16]{1,3,2,0:T(8,128)(2,1)S(1)}, bf16...) while((s32[]{:T(128)}, bf16[2,512,4,16]{1,3,2,0:T(8,128)(2,1)S(1)}, ...), condition=%wide.region_21.21_spmd, body=%wide.region_18.20_spmd.sunk | while | flops 157347840 | bytes 25603164 | solution.py:82
  407.2 2.0 fusion.133
  409.2 1.9 fusion.134
  412.5 2.0 fusion.133
  414.5 1.9 fusion.134
  416.9 10.6 %while.56 = (s32[]{:T(128)}, bf16[2,512,4,16]{1,3,2,0:T(8,128)(2,1)S(1)}, pred[1024]{0:T(1024)(128)(4,1)S(1)}, bf16[2,512,4,16]{1,3,2,0:T(8,128)(2,1)S(1)}, bf16...) while((s32[]{:T(128)}, bf16[2,512,4,16]{1,3,2,0:T(8,128)(2,1)S(1)}, ...), condition=%wide.region_21.21_spmd, body=%wide.region_18.20_spmd.sunk | while | flops 157347840 | bytes 25603164 | solution.py:82
  418.3 2.0 fusion.133
  420.3 1.9 fusion.134
  423.6 2.0 fusion.133
  425.6 1.9 fusion.134
  428.1 6.2 %gather_fusion.4 = bf16[2048,64]{1,0:T(8,128)(2,1)S(1)} fusion(bf16[2048,64]{1,0:T(8,128)(2,1)S(1)} %bitcast.278, s32[2048]{0:T(1024)S(1)} %copy-done.11), kind=kCustom, calls=%fused_computation.4 | custom fusion | bytes 532480 | tf_op jit(solution)/shard_map/jit(_take)/gather | solution.py:158
  435.6 7.8 %all-to-all-start.1 = ((bf16[64,2,1024]{2,1,0:T(2,128)(2,1)}), bf16[64,2,1024]{2,1,0:T(2,128)(2,1)S(1)}, u32[]{:S(2)}, u32[]{:S(2)}) async-start(bf16[64,2,1024]{2,1,0:T(2,128)(2,1)} %reshape.1017), calls=%async_computation.1 | async-start | bytes 524288 | tf_op jit(solution)/shard_map/all_to_all | solution.py:159
  444.6 36.5 %compare_and_fusion.4 = (pred[1024]{0:T(1024)(128)(4,1)S(1)}, s32[1024]{0:T(1024)S(1)}) fusion(s32[1024]{0:T(1024)S(1)} %copy-done.7, pred[1024]{0:T(1024)(128)(4,1)} %get-tuple-element.425, pred[1024]{0:T(1024)(128)(4,1)} %get-tuple-element.424, pred[1024]{0:T(1024)(128)(4,1)} %get-tuple-element.423, pred[1024]{0:T(1024)(128)(4,1)} %get-tuple-element.422, ...), kind=kLoop, calls=%fused_computation.258 | loop fusion | flops 69632 | bytes 76004 | tf_op jit(solution)/shard_map/jit(_take)/and | solution.py:169
  481.4 3.2 gather_fusion.5
  484.7 2.0 fusion.66
  486.7 24.6 %reduce-scatter.4.cloned.1.call-done = bf16[64,1024]{1,0:T(8,128)(2,1)} async-done(((bf16[256,1024]{1,0:T(8,128)(2,1)}), bf16[64,1024]{1,0:T(8,128)(2,1)}) %reduce-scatter.4.cloned.1.call-update) | async-done | bytes 131088
  511.3 1.7 add_convert_fusion
  (342 shorter events, 114.8 us)
Async XLA Ops:
  6.5 292.5 %copy-start = (bf16[256,256]{1,0:T(8,128)(2,1)S(1)}, bf16[256,256]{1,0:T(8,128)(2,1)}, u32[]{:S(2)}) copy-start(bf16[256,256]{1,0:T(8,128)(2,1)} %param.23) | copy-start | bytes 393220
  6.5 21.5 %copy-start.1 = (s32[1,1024]{1,0:T(1,128)S(1)}, s32[1,1024]{1,0:T(1,128)}, u32[]{:S(2)}) copy-start(s32[1,1024]{1,0:T(1,128)} %param.19) | copy-start | bytes 12292
  6.5 340.2 %all-reduce.2.cloned.1.call-start = ((), (), s32[]{:S(2)}) async-start(), calls=%async_computation.3 | async-start | bytes 1048576 | tf_op jit(solution)/shard_map/psum | solution.py:126
  7.5 82.5 %collective-permute-start.1 = (bf16[128,256]{1,0:T(8,128)(2,1)S(1)}, bf16[128,256]{1,0:T(8,128)(2,1)S(1)}, u32[]{:S(2)}, u32[]{:S(2)}) collective-permute-start(bf16[128,256]{1,0:T(8,128)(2,1)S(1)} %get-tuple-element.486), channel_id=1, source_target_pairs={{4,0},{8,4},{12,8},{16,12},{20,16},{24,20},{28,24},{32,28},{36,32}... | collective-permute-start | bytes 196616 | tf_op jit(solution)/shard_map/ppermute | solution.py:26
  14.6 75.4 %collective-permute-start = (bf16[128,256]{1,0:T(8,128)(2,1)S(1)}, bf16[128,256]{1,0:T(8,128)(2,1)S(1)}, u32[]{:S(2)}, u32[]{:S(2)}) collective-permute-start(bf16[128,256]{1,0:T(8,128)(2,1)S(1)} %get-tuple-element.485), channel_id=1, source_target_pairs={{0,4},{4,8},{8,12},{12,16},{16,20},{20,24},{24,28},{28,32},{32,36}... | collective-permute-start | bytes 196616 | tf_op jit(solution)/shard_map/ppermute | solution.py:24
  24.5 64.7 %copy-start.3 = (s32[64]{0:T(128)}, s32[64]{0:T(128)S(1)}, u32[]{:S(2)}) copy-start(s32[64]{0:T(128)S(1)} %bitcast_subtract_fusion) | copy-start | bytes 772
  28.0 62.0 %copy-start.5 = (bf16[1024,256]{1,0:T(8,128)(2,1)S(1)}, bf16[1024,256]{1,0:T(8,128)(2,1)}, u32[]{:S(2)}) copy-start(bf16[1024,256]{1,0:T(8,128)(2,1)} %param.17) | copy-start | bytes 1572868
  82.7 7.3 %copy-start.6 = (s32[1024]{0:T(1024)}, s32[1024]{0:T(1024)S(1)}, u32[]{:S(2)}) copy-start(s32[1024]{0:T(1024)S(1)} %scatter_custom_fusion) | copy-start | bytes 12292
  82.8 7.2 %copy-start.8 = (s32[1024]{0:T(1024)}, s32[1024]{0:T(1024)S(1)}, u32[]{:S(2)}) copy-start(s32[1024]{0:T(1024)S(1)} %convert_reduce_fusion.3) | copy-start | bytes 12292
  90.0 198.5 %copy-start.47 = (bf16[256,3,64]{0,2,1:T(8,128)(2,1)S(1)}, bf16[256,3,64]{0,2,1:T(8,128)(2,1)}, u32[]{:S(2)}) copy-start(bf16[256,3,64]{0,2,1:T(8,128)(2,1)} %param.22) | copy-start | bytes 294916
  289.0 59.8 %copy-start.48 = (bf16[256,3,64]{0,2,1:T(8,128)(2,1)S(1)}, bf16[256,3,64]{0,2,1:T(8,128)(2,1)}, u32[]{:S(2)}) copy-start(bf16[256,3,64]{0,2,1:T(8,128)(2,1)} %param.24) | copy-start | bytes 294916
  348.0 0.8 copy-start.2
  358.1 37.5 %all-to-all-start = ((bf16[64,32,192]{2,1,0:T(8,128)(2,1)}), bf16[64,32,192]{2,1,0:T(8,128)(2,1)S(1)}, u32[]{:S(2)}, u32[]{:S(2)}) async-start(bf16[64,32,192]{2,1,0:T(8,128)(2,1)} %broadcast_select_fusion.1), calls=%async_computation | async-start | bytes 2097152 | tf_op jit(solution)/shard_map/all_to_all | solution.py:150
  405.1 22.9 %copy-start.11 = (s32[2048]{0:T(1024)S(1)}, s32[2048]{0:T(1024)}, u32[]{:S(2)}) copy-start(s32[2048]{0:T(1024)} %broadcast_clamp_fusion.1) | copy-start | bytes 24580
  405.1 29.1 %copy-start.10 = (pred[64,32]{1,0:T(8,128)(4,1)S(1)}, pred[64,32]{1,0:T(8,128)(4,1)}, u32[]{:S(2)}) copy-start(pred[64,32]{1,0:T(8,128)(4,1)} %compare_and_fusion.2) | copy-start | bytes 6148
  405.1 38.3 %copy-start.4 = (s32[64]{0:T(128)S(1)}, s32[64]{0:T(128)}, u32[]{:S(2)}) copy-start(s32[64]{0:T(128)} %copy-done.3) | copy-start | bytes 772
  405.2 39.0 %copy-start.7 = (s32[1024]{0:T(1024)S(1)}, s32[1024]{0:T(1024)}, u32[]{:S(2)}) copy-start(s32[1024]{0:T(1024)} %copy-done.6) | copy-start | bytes 12292
  405.2 39.0 %copy-start.9 = (s32[1024]{0:T(1024)S(1)}, s32[1024]{0:T(1024)}, u32[]{:S(2)}) copy-start(s32[1024]{0:T(1024)} %copy-done.8) | copy-start | bytes 12292
  405.2 39.0 %copy-start.12 = (s32[1024,1]{0,1:T(1,128)S(1)}, s32[1024,1]{0,1:T(1,128)}, u32[]{:S(2)}) copy-start(s32[1024,1]{0,1:T(1,128)} %get-tuple-element.472) | copy-start | bytes 12292
  405.2 39.0 %copy-start.13 = (pred[1024]{0:T(1024)(128)(4,1)S(1)}, pred[1024]{0:T(1024)(128)(4,1)}, u32[]{:S(2)}) copy-start(pred[1024]{0:T(1024)(128)(4,1)} %get-tuple-element.369) | copy-start | bytes 3076
  405.2 39.0 %copy-start.14 = (pred[1024]{0:T(1024)(128)(4,1)S(1)}, pred[1024]{0:T(1024)(128)(4,1)}, u32[]{:S(2)}) copy-start(pred[1024]{0:T(1024)(128)(4,1)} %get-tuple-element.370) | copy-start | bytes 3076
  405.2 39.0 %copy-start.15 = (pred[1024]{0:T(1024)(128)(4,1)S(1)}, pred[1024]{0:T(1024)(128)(4,1)}, u32[]{:S(2)}) copy-start(pred[1024]{0:T(1024)(128)(4,1)} %get-tuple-element.371) | copy-start | bytes 3076
  405.2 39.0 %copy-start.16 = (pred[1024]{0:T(1024)(128)(4,1)S(1)}, pred[1024]{0:T(1024)(128)(4,1)}, u32[]{:S(2)}) copy-start(pred[1024]{0:T(1024)(128)(4,1)} %get-tuple-element.372) | copy-start | bytes 3076
  405.2 39.0 %copy-start.17 = (pred[1024]{0:T(1024)(128)(4,1)S(1)}, pred[1024]{0:T(1024)(128)(4,1)}, u32[]{:S(2)}) copy-start(pred[1024]{0:T(1024)(128)(4,1)} %get-tuple-element.373) | copy-start | bytes 3076
  405.2 39.0 %copy-start.18 = (pred[1024]{0:T(1024)(128)(4,1)S(1)}, pred[1024]{0:T(1024)(128)(4,1)}, u32[]{:S(2)}) copy-start(pred[1024]{0:T(1024)(128)(4,1)} %get-tuple-element.374) | copy-start | bytes 3076
  405.2 39.0 %copy-start.19 = (pred[1024]{0:T(1024)(128)(4,1)S(1)}, pred[1024]{0:T(1024)(128)(4,1)}, u32[]{:S(2)}) copy-start(pred[1024]{0:T(1024)(128)(4,1)} %get-tuple-element.375) | copy-start | bytes 3076
  405.3 39.0 %copy-start.20 = (pred[1024]{0:T(1024)(128)(4,1)S(1)}, pred[1024]{0:T(1024)(128)(4,1)}, u32[]{:S(2)}) copy-start(pred[1024]{0:T(1024)(128)(4,1)} %get-tuple-element.376) | copy-start | bytes 3076
  405.3 39.0 %copy-start.21 = (pred[1024]{0:T(1024)(128)(4,1)S(1)}, pred[1024]{0:T(1024)(128)(4,1)}, u32[]{:S(2)}) copy-start(pred[1024]{0:T(1024)(128)(4,1)} %get-tuple-element.377) | copy-start | bytes 3076
  405.3 39.0 %copy-start.22 = (pred[1024]{0:T(1024)(128)(4,1)S(1)}, pred[1024]{0:T(1024)(128)(4,1)}, u32[]{:S(2)}) copy-start(pred[1024]{0:T(1024)(128)(4,1)} %get-tuple-element.378) | copy-start | bytes 3076
  405.3 39.0 %copy-start.23 = (pred[1024]{0:T(1024)(128)(4,1)S(1)}, pred[1024]{0:T(1024)(128)(4,1)}, u32[]{:S(2)}) copy-start(pred[1024]{0:T(1024)(128)(4,1)} %get-tuple-element.379) | copy-start | bytes 3076
  405.3 39.0 %copy-start.24 = (pred[1024]{0:T(1024)(128)(4,1)S(1)}, pred[1024]{0:T(1024)(128)(4,1)}, u32[]{:S(2)}) copy-start(pred[1024]{0:T(1024)(128)(4,1)} %get-tuple-element.380) | copy-start | bytes 3076
  405.3 39.0 %copy-start.25 = (pred[1024]{0:T(1024)(128)(4,1)S(1)}, pred[1024]{0:T(1024)(128)(4,1)}, u32[]{:S(2)}) copy-start(pred[1024]{0:T(1024)(128)(4,1)} %get-tuple-element.381) | copy-start | bytes 3076
  405.3 39.0 %copy-start.26 = (pred[1024]{0:T(1024)(128)(4,1)S(1)}, pred[1024]{0:T(1024)(128)(4,1)}, u32[]{:S(2)}) copy-start(pred[1024]{0:T(1024)(128)(4,1)} %get-tuple-element.382) | copy-start | bytes 3076
  405.3 39.0 %copy-start.27 = (pred[1024]{0:T(1024)(128)(4,1)S(1)}, pred[1024]{0:T(1024)(128)(4,1)}, u32[]{:S(2)}) copy-start(pred[1024]{0:T(1024)(128)(4,1)} %get-tuple-element.383) | copy-start | bytes 3076
  405.3 39.0 %copy-start.28 = (pred[1024]{0:T(1024)(128)(4,1)S(1)}, pred[1024]{0:T(1024)(128)(4,1)}, u32[]{:S(2)}) copy-start(pred[1024]{0:T(1024)(128)(4,1)} %get-tuple-element.384) | copy-start | bytes 3076
  405.3 39.0 %copy-start.29 = (pred[1024]{0:T(1024)(128)(4,1)S(1)}, pred[1024]{0:T(1024)(128)(4,1)}, u32[]{:S(2)}) copy-start(pred[1024]{0:T(1024)(128)(4,1)} %get-tuple-element.385) | copy-start | bytes 3076
  405.4 39.0 %copy-start.30 = (pred[1024]{0:T(1024)(128)(4,1)S(1)}, pred[1024]{0:T(1024)(128)(4,1)}, u32[]{:S(2)}) copy-start(pred[1024]{0:T(1024)(128)(4,1)} %get-tuple-element.386) | copy-start | bytes 3076
  405.4 39.0 %copy-start.31 = (pred[1024]{0:T(1024)(128)(4,1)S(1)}, pred[1024]{0:T(1024)(128)(4,1)}, u32[]{:S(2)}) copy-start(pred[1024]{0:T(1024)(128)(4,1)} %get-tuple-element.387) | copy-start | bytes 3076
  405.4 39.0 %copy-start.32 = (pred[1024]{0:T(1024)(128)(4,1)S(1)}, pred[1024]{0:T(1024)(128)(4,1)}, u32[]{:S(2)}) copy-start(pred[1024]{0:T(1024)(128)(4,1)} %get-tuple-element.388) | copy-start | bytes 3076
  405.4 39.0 %copy-start.33 = (pred[1024]{0:T(1024)(128)(4,1)S(1)}, pred[1024]{0:T(1024)(128)(4,1)}, u32[]{:S(2)}) copy-start(pred[1024]{0:T(1024)(128)(4,1)} %get-tuple-element.389) | copy-start | bytes 3076
  405.4 39.0 %copy-start.34 = (pred[1024]{0:T(1024)(128)(4,1)S(1)}, pred[1024]{0:T(1024)(128)(4,1)}, u32[]{:S(2)}) copy-start(pred[1024]{0:T(1024)(128)(4,1)} %get-tuple-element.390) | copy-start | bytes 3076
  405.4 39.0 %copy-start.35 = (pred[1024]{0:T(1024)(128)(4,1)S(1)}, pred[1024]{0:T(1024)(128)(4,1)}, u32[]{:S(2)}) copy-start(pred[1024]{0:T(1024)(128)(4,1)} %get-tuple-element.391) | copy-start | bytes 3076
  405.4 39.0 %copy-start.36 = (pred[1024]{0:T(1024)(128)(4,1)S(1)}, pred[1024]{0:T(1024)(128)(4,1)}, u32[]{:S(2)}) copy-start(pred[1024]{0:T(1024)(128)(4,1)} %get-tuple-element.392) | copy-start | bytes 3076
  405.4 39.0 %copy-start.37 = (pred[1024]{0:T(1024)(128)(4,1)S(1)}, pred[1024]{0:T(1024)(128)(4,1)}, u32[]{:S(2)}) copy-start(pred[1024]{0:T(1024)(128)(4,1)} %get-tuple-element.393) | copy-start | bytes 3076
  405.4 39.0 %copy-start.38 = (pred[1024]{0:T(1024)(128)(4,1)S(1)}, pred[1024]{0:T(1024)(128)(4,1)}, u32[]{:S(2)}) copy-start(pred[1024]{0:T(1024)(128)(4,1)} %get-tuple-element.394) | copy-start | bytes 3076
  405.4 39.0 %copy-start.39 = (pred[1024]{0:T(1024)(128)(4,1)S(1)}, pred[1024]{0:T(1024)(128)(4,1)}, u32[]{:S(2)}) copy-start(pred[1024]{0:T(1024)(128)(4,1)} %get-tuple-element.395) | copy-start | bytes 3076
  405.5 39.0 %copy-start.40 = (pred[1024]{0:T(1024)(128)(4,1)S(1)}, pred[1024]{0:T(1024)(128)(4,1)}, u32[]{:S(2)}) copy-start(pred[1024]{0:T(1024)(128)(4,1)} %get-tuple-element.396) | copy-start | bytes 3076
  405.5 39.0 %copy-start.41 = (pred[1024]{0:T(1024)(128)(4,1)S(1)}, pred[1024]{0:T(1024)(128)(4,1)}, u32[]{:S(2)}) copy-start(pred[1024]{0:T(1024)(128)(4,1)} %get-tuple-element.397) | copy-start | bytes 3076
  405.5 39.0 %copy-start.42 = (pred[1024]{0:T(1024)(128)(4,1)S(1)}, pred[1024]{0:T(1024)(128)(4,1)}, u32[]{:S(2)}) copy-start(pred[1024]{0:T(1024)(128)(4,1)} %get-tuple-element.398) | copy-start | bytes 3076
  405.5 39.0 %copy-start.43 = (pred[1024]{0:T(1024)(128)(4,1)S(1)}, pred[1024]{0:T(1024)(128)(4,1)}, u32[]{:S(2)}) copy-start(pred[1024]{0:T(1024)(128)(4,1)} %get-tuple-element.399) | copy-start | bytes 3076
  405.5 39.0 %copy-start.44 = (pred[1024]{0:T(1024)(128)(4,1)S(1)}, pred[1024]{0:T(1024)(128)(4,1)}, u32[]{:S(2)}) copy-start(pred[1024]{0:T(1024)(128)(4,1)} %get-tuple-element.400) | copy-start | bytes 3076
  405.5 39.0 %copy-start.45 = (pred[1024]{0:T(1024)(128)(4,1)S(1)}, pred[1024]{0:T(1024)(128)(4,1)}, u32[]{:S(2)}) copy-start(pred[1024]{0:T(1024)(128)(4,1)} %get-tuple-element.401) | copy-start | bytes 3076
  405.5 39.0 %copy-start.46 = (pred[1024]{0:T(1024)(128)(4,1)S(1)}, pred[1024]{0:T(1024)(128)(4,1)}, u32[]{:S(2)}) copy-start(pred[1024]{0:T(1024)(128)(4,1)} %get-tuple-element.402) | copy-start | bytes 3076
  435.6 45.5 %all-to-all-start.1 = ((bf16[64,2,1024]{2,1,0:T(2,128)(2,1)}), bf16[64,2,1024]{2,1,0:T(2,128)(2,1)S(1)}, u32[]{:S(2)}, u32[]{:S(2)}) async-start(bf16[64,2,1024]{2,1,0:T(2,128)(2,1)} %reshape.1017), calls=%async_computation.1 | async-start | bytes 524288 | tf_op jit(solution)/shard_map/all_to_all | solution.py:159
  443.4 67.9 %reduce-scatter.4.cloned.1.call-start = ((), (), s32[]{:S(2)}) async-start(), calls=%async_computation.4 | async-start | bytes 655360
Sparse Core Ops, SparseCore 0:
  300.3 46.3 all-reduce.1
  486.8 24.4 reduce-scatter.3
where the time goes:
time: 527 us; the launch traced here: 520 us
  local copies, waits for them, and re-layouts  158 us (30%)
  other arithmetic  150 us (28%)
  waiting for transfers between devices  96.7 us (18%)
  matrix products  57.5 us (11%)
  starting transfers between devices  27.4 us (5%)
  between operations  14.6 us (3%)
  blocking collectives  13.3 us (3%)
    gather x27, local copies, waits for them, and re-layouts, conv_step(): picked = jnp.take(padded, local_row, axis=0)  106 us
    psum x1, waiting for transfers between devices, local(): lax.psum(partial_one.astype(jnp.bfloat16), 'ch').astype(jnp.float32)  45.8 us
    gather x3, other arithmetic, local(): within = jnp.clip(slots - recv_off[source], 0, bucket_rows - 1)  41.5 us
    and x1, other arithmetic, local(): heads_b = jnp.take(returned, home_from, axis=0)  36.5 us
    dot_general x27, matrix products, conv_step(): jnp.dot(picked, conv_weight[kernel_index], preferred_element_type=jnp.flo...  34.4 us
    all_to_all x1, waiting for transfers between devices, local(): lax.all_to_all(outgoing, 'seg', split_axis=0, concat_axis=0, tiled=True)  26.2 us
    unnamed x3, waiting for transfers between devices  24.6 us
    ge x27, other arithmetic, conv_step(): target >= 0  21.3 us
  transfers between devices with their start and end apart: 6, of which 3 were waited for; matrix products, arithmetic and copies ran while one was open for 22% of the time, Pallas kernels for 0%

commit v1 on v0

v1 whole, which is shorter than its diff:
```python
import jax
import jax.numpy as jnp
import numpy as np
from jax import lax
from jax.experimental import pallas as pl
from jax.experimental.pallas import tpu as pltpu
from jax.sharding import PartitionSpec as P

BF = jnp.bfloat16
F32 = jnp.float32
I32 = jnp.int32
HALO = 128
KOFF = 27
EPS = 1e-05
DEAD = -1e30
EXP_SCALE = float(16 ** (-0.5) * np.log2(np.e))
NT = (((1,), (1,)), ((), ()))
TN = (((0,), (0,)), ((), ()))
VM = pl.BlockSpec(memory_space=pltpu.VMEM)
SM = pl.BlockSpec(memory_space=pltpu.SMEM)
PARAMS = pltpu.CompilerParams(vmem_limit_bytes=50 << 20)


def iota(shape, dim):
    return lax.broadcasted_iota(I32, shape, dim)


def one_where(cond):
    return jnp.where(cond, 1.0, 0.0)


def norm_columns(x):
    centre = x - jnp.mean(x, axis=0, keepdims=True)
    spread = jnp.mean(centre * centre, axis=0, keepdims=True)
    return (centre * lax.rsqrt(spread + EPS)).astype(BF)


def place(pieces, ch, full_ref):
    size = pieces[0].shape[0]
    for j, piece in enumerate(pieces):
        owner = (ch + j) & 3
        full_ref[pl.ds(pl.multiple_of(owner * size, size), size), :] = piece[...]


def conv_kernel(ids, prev_ref, own_ref, next_ref, nb_ref, w_ref, out_ref, y_ref, acc_ref, nbs_ref):
    base = ids[0] * 1024 - HALO
    ch = ids[1]
    for b in range(8):
        nbs_ref[b * 32 : b * 32 + KOFF, :] = nb_ref[:, b * 128 : (b + 1) * 128]
    chosen = one_where(iota((64, 256), 1) == iota((64, 256), 0) + ch * 64).astype(BF)
    acc_ref[...] = lax.dot_general(chosen, own_ref[...], NT, preferred_element_type=F32)

    def transform(k, slot):
        w = w_ref[k]
        y_ref[slot, :, 0:128] = lax.dot_general(w, prev_ref[...], NT, preferred_element_type=F32)
        for j in range(4):
            y_ref[slot, :, 128 + j * 256 : 384 + j * 256] = lax.dot_general(
                w, own_ref[j * 256 : (j + 1) * 256], NT, preferred_element_type=F32
            )
        y_ref[slot, :, 1152:1280] = lax.dot_general(
            w, next_ref[...], NT, preferred_element_type=F32
        )

    def collect(k, slot):
        for b in range(8):
            r = nbs_ref[pl.ds(b * 32 + k, 8, stride=0), :] - (base + b * 128)
            there = nbs_ref[pl.ds(b * 32 + k, 8, stride=0), :] >= 0
            lane = r & 127
            first = r < 128
            second = r < 256
            for g in range(8):
                t = [
                    jnp.take_along_axis(
                        y_ref[slot, g * 8 : g * 8 + 8, (b + j) * 128 : (b + j + 1) * 128],
                        lane,
                        axis=1,
                        mode="promise_in_bounds",
                    )
                    for j in range(3)
                ]
                v = jnp.where(first, t[0], jnp.where(second, t[1], t[2]))
                acc_ref[g * 8 : g * 8 + 8, b * 128 : (b + 1) * 128] += jnp.where(there, v, 0.0)

    transform(0, 0)

    def body(i, carry):
        transform(2 * i + 1, 1)
        collect(2 * i, 0)
        transform(2 * i + 2, 0)
        collect(2 * i + 1, 1)
        return carry

    lax.fori_loop(0, KOFF // 2, body, 0)
    collect(KOFF - 1, 0)
    out_ref[...] = acc_ref[...].astype(BF)


def conv(ids, prev, own, nxt, nb, w):
    return pl.pallas_call(
        conv_kernel,
        name="conv",
        out_shape=jax.ShapeDtypeStruct((64, 1024), BF),
        in_specs=[SM] + [VM] * 5,
        out_specs=VM,
        scratch_shapes=[
            pltpu.VMEM((2, 64, 1280), F32),
            pltpu.VMEM((64, 1024), F32),
            pltpu.VMEM((256, 128), I32),
        ],
        compiler_params=PARAMS,
    )(ids, prev, own, nxt, nb, w)


def stage_heads(qkv, bias, q_ref, k_ref, v_ref):
    rows = qkv.shape[1]
    qkv16 = qkv.astype(BF)
    ones = jnp.ones((16, rows), BF)
    q_ref[...] = jnp.concatenate([qkv16[0:64], ones, jnp.zeros((48, rows), BF)], 0).T
    values = jnp.concatenate([qkv16[128:192], jnp.ones((64, rows), BF)], 0).T
    owner = (iota((1, 128), 1) & 63) >> 4
    k_ref[...] = jnp.zeros(k_ref.shape, BF)
    for h in range(4):
        k_ref[h, h * 16 : (h + 1) * 16, :] = qkv16[64 + h * 16 : 80 + h * 16]
        if bias is not None:
            k_ref[h, 64:80, :] = bias
        v_ref[h] = jnp.where(owner == h, values, jnp.zeros_like(values))


def attend(q_ref, k_ref, v_ref, patch, qb, block):
    start = patch * 1024
    if not isinstance(start, int):
        start = pl.multiple_of(start, 1024)
    rows = pl.ds(start + qb * block, block)
    keys = pl.ds(start, 1024)
    q = q_ref[rows, :]
    total = None
    for h in range(4):
        s = jnp.dot(q, k_ref[h, :, keys], preferred_element_type=F32)
        peak = jnp.max(s, axis=1, keepdims=True)
        p = jnp.exp2((s - peak) * EXP_SCALE).astype(BF)
        o = jnp.dot(p, v_ref[h, keys, :], preferred_element_type=F32)
        total = o if total is None else total + o
    return total / pltpu.roll(total, 64, 1)


def first_kernel(ids, x0, x1, x2, x3, w_ref, out_ref, full_ref, q_ref, k_ref, v_ref):
    place((x0, x1, x2, x3), ids[1], full_ref)
    normed = norm_columns(full_ref[...].astype(F32))
    qkv = jnp.dot(w_ref[...], normed, preferred_element_type=F32)
    stage_heads(qkv, None, q_ref, k_ref, v_ref)
    for qb in range(4):
        o = attend(q_ref, k_ref, v_ref, 0, qb, 256)
        out_ref[:, qb * 256 : (qb + 1) * 256] = o.T[:64].astype(BF)


def first(ids, pieces, w):
    return pl.pallas_call(
        first_kernel,
        name="first",
        out_shape=jax.ShapeDtypeStruct((64, 1024), BF),
        in_specs=[SM] + [VM] * 5,
        out_specs=VM,
        scratch_shapes=[
            pltpu.VMEM((256, 1024), BF),
            pltpu.VMEM((1024, 128), BF),
            pltpu.VMEM((4, 128, 1024), BF),
            pltpu.VMEM((4, 1024, 128), BF),
        ],
        compiler_params=PARAMS,
    )(ids, *pieces, w)


def pick_kernel(
    ids, x0, x1, x2, x3, h0, h1, h2, h3, wo_ref, perm_ref, counts_ref, send_ref, mine_ref, full_ref, heads_ref
):
    seg = ids[0]
    ch = ids[1]
    place((x0, x1, x2, x3), ch, full_ref)
    place((h0, h1, h2, h3), ch, heads_ref)
    mixed = full_ref[...].astype(F32) + lax.dot_general(
        wo_ref[...], heads_ref[...], TN, preferred_element_type=F32
    )
    mixed16 = mixed.astype(BF)
    full_ref[...] = mixed16
    mine_ref[...] = full_ref[pl.ds(pl.multiple_of(ch * 64, 64), 64), :]
    normed = norm_columns(mixed16.astype(F32))
    counts = counts_ref[...].astype(F32)
    row = jnp.sum(jnp.where(iota((64, 64), 0) == seg, counts, 0.0), axis=0, keepdims=True)
    slot = iota((512, 64), 0)
    before = jnp.where(iota((512, 64), 1) < (slot >> 3), row, 0.0)
    position = jnp.sum(before, axis=1, keepdims=True).astype(I32)
    position = position + ch * 8 + (iota((512, 1), 0) & 7)
    perm = perm_ref[...].astype(F32)
    hit = iota((512, 1024), 1) == position
    source = jnp.sum(jnp.where(hit, perm, 0.0), axis=1, keepdims=True).astype(I32)
    chosen = one_where(iota((512, 1024), 1) == source).astype(BF)
    rows = lax.dot_general(chosen, normed, NT, preferred_element_type=F32)
    send_ref[...] = rows.astype(BF).reshape(64, 8, 256)


def pick(ids, mixed, heads, wo, perm, counts):
    return pl.pallas_call(
        pick_kernel,
        name="pick",
        out_shape=(
            jax.ShapeDtypeStruct((64, 8, 256), BF),
            jax.ShapeDtypeStruct((64, 1024), BF),
        ),
        in_specs=[SM] + [VM] * 11,
        out_specs=(VM, VM),
        scratch_shapes=[pltpu.VMEM((256, 1024), BF), pltpu.VMEM((256, 1024), BF)],
        compiler_params=PARAMS,
    )(ids, *mixed, *heads, wo, perm, counts)


def second_kernel(
    ids, counts_sm, a0, a1, a2, a3, w_ref, out_ref, lo_ref, hi_ref, q_ref, k_ref, v_ref, o_ref
):
    seg = ids[0]
    ch = ids[1]
    lo_ref[...] = jnp.zeros(lo_ref.shape, F32)
    hi_ref[...] = jnp.zeros(hi_ref.shape, F32)

    def compact(s, off):
        tiles = [piece[s].astype(F32) for piece in (a0, a1, a2, a3)]
        for j, tile in enumerate(tiles):
            dst = pl.ds(off + ((ch + j) & 3) * 8, 8)
            lo_ref[dst, :] = tile[:, :128]
            hi_ref[dst, :] = tile[:, 128:]
        return off + counts_sm[s, seg]

    live = lax.fori_loop(0, 64, compact, 0)
    rows = jnp.concatenate([lo_ref[0:2048, :], hi_ref[0:2048, :]], 1).astype(BF)
    qkv = lax.dot_general(w_ref[...], rows, NT, preferred_element_type=F32)
    dead = (iota((16, 2048), 1) >= live) & (iota((16, 2048), 0) == 0)
    bias = jnp.where(dead, DEAD, 0.0).astype(BF)
    stage_heads(qkv, bias, q_ref, k_ref, v_ref)
    o_ref[2048:2080, :] = jnp.zeros((32, 128), F32)

    def block(i, carry):
        o = attend(q_ref, k_ref, v_ref, i >> 2, i & 3, 256)
        both = jnp.where(iota((1, 128), 1) < 64, o, pltpu.roll(o, 64, 1))
        o_ref[pl.ds(pl.multiple_of(i * 256, 256), 256), :] = both
        return carry

    lax.fori_loop(0, 8, block, 0)
    low = iota((16, 128), 1) < 64

    def give(s, off):
        top = o_ref[pl.ds(off, 16), :]
        end = o_ref[pl.ds(off + 16, 16), :]
        out_ref[s] = jnp.where(low, top, end).astype(BF)
        return off + counts_sm[s, seg]

    lax.fori_loop(0, 64, give, 0)


def second(ids, counts, arrived, w):
    return pl.pallas_call(
        second_kernel,
        name="second",
        out_shape=jax.ShapeDtypeStruct((64, 16, 128), BF),
        in_specs=[SM, SM] + [VM] * 5,
        out_specs=VM,
        scratch_shapes=[
            pltpu.VMEM((2080, 128), F32),
            pltpu.VMEM((2080, 128), F32),
            pltpu.VMEM((2048, 128), BF),
            pltpu.VMEM((4, 128, 2048), BF),
            pltpu.VMEM((4, 2048, 128), BF),
            pltpu.VMEM((2080, 128), F32),
        ],
        compiler_params=PARAMS,
    )(ids, counts, *arrived, w)


def home_kernel(ids, counts_sm, back_ref, perm_ref, out_ref, sorted_ref):
    seg = ids[0]

    def put(t, off):
        tile = back_ref[t].astype(F32)
        sorted_ref[pl.ds(off, 16), :] = tile
        sorted_ref[pl.ds(off + 16, 16), :] = pltpu.roll(tile, 64, 1)
        return off + counts_sm[seg, t]

    lax.fori_loop(0, 64, put, 0)
    chosen = one_where(iota((1024, 1024), 0) == perm_ref[...]).astype(BF)
    rows = jnp.dot(chosen, sorted_ref[0:1024, :].astype(BF), preferred_element_type=F32)
    out_ref[...] = rows.T[:64].astype(BF)


def home(ids, counts, back, perm):
    return pl.pallas_call(
        home_kernel,
        name="home",
        out_shape=jax.ShapeDtypeStruct((64, 1024), BF),
        in_specs=[SM, SM, VM, VM],
        out_specs=VM,
        scratch_shapes=[pltpu.VMEM((1056, 128), F32)],
        compiler_params=PARAMS,
    )(ids, counts, back, perm)


def last_kernel(ids, mine_ref, h0, h1, h2, h3, wo_ref, out_ref, heads_ref, all_ref):
    ch = ids[1]
    place((h0, h1, h2, h3), ch, heads_ref)
    all_ref[...] = lax.dot_general(
        wo_ref[...], heads_ref[...], TN, preferred_element_type=F32
    )
    own = all_ref[pl.ds(pl.multiple_of(ch * 64, 64), 64), :]
    out_ref[...] = (mine_ref[...].astype(F32) + own).astype(BF)


def last(ids, mine, heads, wo):
    return pl.pallas_call(
        last_kernel,
        name="last",
        out_shape=jax.ShapeDtypeStruct((64, 1024), BF),
        in_specs=[SM] + [VM] * 6,
        out_specs=VM,
        scratch_shapes=[pltpu.VMEM((256, 1024), BF), pltpu.VMEM((256, 1024), F32)],
        compiler_params=PARAMS,
    )(ids, mine, *heads, wo)


def spread(piece):
    def moved(step):
        return lax.ppermute(piece, "ch", [((i + step) % 4, i) for i in range(4)])

    return piece, moved(1), moved(2), moved(3)


def local(
    voxels, neighbours, send_perm, send_counts, conv_weight, qkv_first, out_first, qkv_second, out_second
):
    seg_count = lax.axis_size("seg")
    ids = jnp.stack([lax.axis_index("seg"), lax.axis_index("ch")]).astype(I32)
    up = [(i, i + 1) for i in range(seg_count - 1)]
    down = [(i + 1, i) for i in range(seg_count - 1)]
    prev = lax.ppermute(voxels[-HALO:], "seg", up)
    nxt = lax.ppermute(voxels[:HALO], "seg", down)
    conv_w = jnp.swapaxes(conv_weight, 1, 2)
    w_first = jnp.transpose(qkv_first, (1, 2, 0)).reshape(192, 256)
    w_second = jnp.transpose(qkv_second, (1, 2, 0)).reshape(192, 256)
    mixed_a = spread(conv(ids, prev, voxels, nxt, neighbours, conv_w))
    heads_a = spread(first(ids, mixed_a, w_first))
    outgoing, mine = pick(ids, mixed_a, heads_a, out_first, send_perm, send_counts)
    arrived = lax.all_to_all(outgoing, "seg", split_axis=0, concat_axis=0, tiled=True)
    going = second(ids, send_counts, spread(arrived), w_second)
    back = lax.all_to_all(going, "seg", split_axis=0, concat_axis=0, tiled=True)
    heads_b = spread(home(ids, send_counts, back, send_perm))
    return jnp.swapaxes(last(ids, mine, heads_b, out_second), 0, 1)


def solution(mesh):
    placed = (
        P("seg", None),
        P(None, "seg"),
        P("seg", None),
        P(),
        P(None, None, "ch"),
        P(None, None, "ch"),
        P(),
        P(None, None, "ch"),
        P(),
    )
    return jax.shard_map(
        local, mesh=mesh, in_specs=placed, out_specs=P("seg", "ch"), check_vma=False
    )
```

time: 527 us -> 147 us (0.28); the launches traced: 520 us -> 146 us
  local copies, waits for them, and re-layouts: 158 us -> 3.15 us
  other arithmetic: 150 us -> 0.08 us
  waiting for transfers between devices: 96.7 us -> 29.8 us
  matrix products: 57.5 us -> 0 us
  Pallas kernels: 0 us -> 46.9 us
  blocking collectives: 13.3 us -> 36.1 us
  between operations: 14.6 us -> 0.1 us
    gather x44 -> x0, local copies, waits for them, and re-layouts: 146 us -> none  [the longest x27 106 us: conv_step(): picked = jnp.take(padded, local_row, axis=0)]
    dot_general x43 -> x0, matrix products: 57.5 us -> none  [the longest x27 34.4 us: conv_step(): jnp.dot(picked, conv_weight[kernel_index], preferred_element_type=jnp.flo...]
    gather x37 -> x0, other arithmetic: 48.6 us -> none  [the longest x3 41.5 us: local(): within = jnp.clip(slots - recv_off[source], 0, bucket_rows - 1)]
    pallas_call x0 -> x6, Pallas kernels: none -> 46.9 us  [the longest x1 19.5 us: second(): pl.pallas_call(second_kernel, name='second', out_shape=jax.ShapeDtypeStru...]
    psum x1 -> x0, waiting for transfers between devices: 45.8 us -> none  [local(): lax.psum(partial_one.astype(jnp.bfloat16), 'ch').astype(jnp.float32)]
    and x31 -> x0, other arithmetic: 37.4 us -> none  [the longest x1 36.5 us: local(): heads_b = jnp.take(returned, home_from, axis=0)]
    all_to_all x0 -> x2, blocking collectives: none -> 36.1 us  [the longest x1 18.5 us: local(): lax.all_to_all(outgoing, 'seg', split_axis=0, concat_axis=0, tiled=True)]
    ppermute x2 -> x14, waiting for transfers between devices: 0.01 us -> 29.8 us  [the longest x12 24.1 us: moved(): return lax.ppermute(piece, 'ch', [((i + step) % 4, i) for i in range(4)])]
  transfers between devices with their start and end apart: 6 -> 14, of which waited for: 3 -> 11; matrix products, arithmetic and copies ran while one was open for 22% -> 0% of each run, Pallas kernels for 0% -> 0%
where the time goes in v1:
time: 147 us; the launch traced here: 146 us
  Pallas kernels  46.9 us (32%)
  blocking collectives  36.1 us (25%)
  waiting for transfers between devices  29.8 us (20%)
  starting transfers between devices  29.6 us (20%)
  local copies, waits for them, and re-layouts  3.15 us (2%)
    ppermute x12, waiting for transfers between devices, moved(): return lax.ppermute(piece, 'ch', [((i + step) % 4, i) for i in range(4)])  24.1 us
    ppermute x12, starting transfers between devices, moved(): return lax.ppermute(piece, 'ch', [((i + step) % 4, i) for i in range(4)])  20.6 us
    pallas_call x1, Pallas kernels, second(): pl.pallas_call(second_kernel, name='second', out_shape=jax.ShapeDtypeStru...  19.5 us
    all_to_all x1, blocking collectives, local(): lax.all_to_all(outgoing, 'seg', split_axis=0, concat_axis=0, tiled=True)  18.5 us
    all_to_all x1, blocking collectives, local(): back = lax.all_to_all(going, 'seg', split_axis=0, concat_axis=0, tiled=True)  17.6 us
    pallas_call x1, Pallas kernels, conv(): pl.pallas_call(conv_kernel, name='conv', out_shape=jax.ShapeDtypeStruct((...  9.04 us
    pallas_call x1, Pallas kernels, first(): pl.pallas_call(first_kernel, name='first', out_shape=jax.ShapeDtypeStruct...  8.41 us
    ppermute x1, starting transfers between devices, local(): nxt = lax.ppermute(voxels[:HALO], 'seg', down)  7.09 us
  transfers between devices with their start and end apart: 14, of which 11 were waited for; matrix products, arithmetic and copies ran while one was open for 0% of the time, Pallas kernels for 0%

profile of v1, /device:TPU:8, one launch (start us, length us, event | category | flops | bytes accessed | tf_op | source)
XLA Modules:
  0.0 145.7 jit_solution(17762003726764429908)
XLA Ops:
  0.0 0.0 copy-start.5
  0.0 0.9 fusion
  0.9 7.1 %collective-permute-start.1 = (bf16[128,256]{1,0:T(8,128)(2,1)S(1)}, bf16[128,256]{1,0:T(8,128)(2,1)S(1)}, u32[]{:S(2)}, u32[]{:S(2)}) collective-permute-start(bf16[128,256]{1,0:T(8,128)(2,1)S(1)} %get-tuple-element.9), channel_id=1, source_target_pairs={{4,0},{8,4},{12,8},{16,12},{20,16},{24,20},{28,24},{32,28},{36,32}... | collective-permute-start | bytes 196616 | tf_op jit(solution)/shard_map/ppermute | solution.py:341
  8.0 1.9 %collective-permute-start = (bf16[128,256]{1,0:T(8,128)(2,1)S(1)}, bf16[128,256]{1,0:T(8,128)(2,1)S(1)}, u32[]{:S(2)}, u32[]{:S(2)}) collective-permute-start(bf16[128,256]{1,0:T(8,128)(2,1)S(1)} %get-tuple-element.10), channel_id=1, source_target_pairs={{0,4},{4,8},{8,12},{12,16},{16,20},{20,24},{24,28},{28,32},{32,36}... | collective-permute-start | bytes 196616 | tf_op jit(solution)/shard_map/ppermute | solution.py:340
  10.0 0.1 pad_add_fusion.ids
  10.0 0.0 collective-permute-done.1.next_ref
  10.0 5.7 %collective-permute-done.prev_ref = bf16[128,256]{1,0:T(8,128)(2,1)S(1)} collective-permute-done((bf16[128,256]{1,0:T(8,128)(2,1)S(1)}, bf16[128,256]{1,0:T(8,128)(2,1)S(1)}, u32[]{:S(2)}, u32[]{:S(2)}) %collective-permute-start) | collective-permute-done | bytes 65568 | tf_op jit(solution)/shard_map/ppermute | solution.py:340
  15.7 0.0 copy-done.5
  15.7 0.0 copy-start
  15.7 1.2 copy-done
  16.9 0.0 copy-start.1
  16.9 1.0 copy-done.1
  17.9 0.0 copy-start.6
  17.9 9.0 %conv.1.x0 = bf16[64,1024]{1,0:T(8,128)(2,1)S(1)} custom-call(s32[2]{0:T(128)S(1)} %pad_add_fusion.ids, bf16[128,256]{1,0:T(8,128)(2,1)S(1)} %collective-permute-done.prev_ref, bf16[1024,256]{1,0:T(8,128)(2,1)S(1)} %copy-done.1, bf16[128,256]{1,0:T(8,128)(2,1)S(1)} %collective-permute-done.1.next_ref, s32[27,1024]{1,0:T(8,128)S(1)} %copy-done.5, ...), custom_call_target="tpu_custom_call" | custom-call | tf_op jit(solution)/shard_map/conv/pallas_call | solution.py:99
  27.0 1.6 %collective-permute-start.4 = (bf16[64,1024]{1,0:T(8,128)(2,1)S(1)}, bf16[64,1024]{1,0:T(8,128)(2,1)S(1)}, u32[]{:S(2)}, u32[]{:S(2)}) collective-permute-start(bf16[64,1024]{1,0:T(8,128)(2,1)S(1)} %conv.1.x0), channel_id=1, source_target_pairs={{3,0},{0,1},{1,2},{2,3},{7,4},{4,5},{5,6},{6,7},{11,8},{8,9},{9,10... | collective-permute-start | bytes 393224 | tf_op jit(solution)/shard_map/ppermute | solution.py:328
  28.5 2.7 %collective-permute-start.3 = (bf16[64,1024]{1,0:T(8,128)(2,1)S(1)}, bf16[64,1024]{1,0:T(8,128)(2,1)S(1)}, u32[]{:S(2)}, u32[]{:S(2)}) collective-permute-start(bf16[64,1024]{1,0:T(8,128)(2,1)S(1)} %conv.1.x0), channel_id=1, source_target_pairs={{2,0},{3,1},{0,2},{1,3},{6,4},{7,5},{4,6},{5,7},{10,8},{11,9},{8,1... | collective-permute-start | bytes 393224 | tf_op jit(solution)/shard_map/ppermute | solution.py:328
  31.3 1.4 collective-permute-start.2
  32.7 0.5 collective-permute-done.4.x3
  33.2 2.4 %collective-permute-done.3.x2 = bf16[64,1024]{1,0:T(8,128)(2,1)S(1)} collective-permute-done((bf16[64,1024]{1,0:T(8,128)(2,1)S(1)}, bf16[64,1024]{1,0:T(8,128)(2,1)S(1)}, u32[]{:S(2)}, u32[]{:S(2)}) %collective-permute-start.3) | collective-permute-done | bytes 131104 | tf_op jit(solution)/shard_map/ppermute | solution.py:328
  35.6 0.6 collective-permute-done.2.x1
  36.2 0.0 copy-done.6
  36.3 0.0 copy-start.2
  36.3 0.0 copy-start.3
  36.3 0.0 copy-start.8
  36.3 8.4 %first.1.h0 = bf16[64,1024]{1,0:T(8,128)(2,1)S(1)} custom-call(s32[2]{0:T(128)S(1)} %pad_add_fusion.ids, bf16[64,1024]{1,0:T(8,128)(2,1)S(1)} %conv.1.x0, bf16[64,1024]{1,0:T(8,128)(2,1)S(1)} %collective-permute-done.2.x1, bf16[64,1024]{1,0:T(8,128)(2,1)S(1)} %collective-permute-done.3.x2, bf16[64,1024]{1,0:T(8,128)(2,1)S(1)} %collective-permute-done.4.x3, ...), custom_call_target="tpu_custom_call" | custom-call | tf_op jit(solution)/shard_map/first/pallas_call | solution.py:157
  44.7 1.4 collective-permute-start.7
  46.0 2.8 %collective-permute-start.6 = (bf16[64,1024]{1,0:T(8,128)(2,1)S(1)}, bf16[64,1024]{1,0:T(8,128)(2,1)S(1)}, u32[]{:S(2)}, u32[]{:S(2)}) collective-permute-start(bf16[64,1024]{1,0:T(8,128)(2,1)S(1)} %first.1.h0), channel_id=1, source_target_pairs={{2,0},{3,1},{0,2},{1,3},{6,4},{7,5},{4,6},{5,7},{10,8},{11,9},{8,1... | collective-permute-start | bytes 393224 | tf_op jit(solution)/shard_map/ppermute | solution.py:328
  48.9 0.8 collective-permute-start.5
  49.7 1.2 collective-permute-done.7.h3
  50.9 2.3 %collective-permute-done.6.h2 = bf16[64,1024]{1,0:T(8,128)(2,1)S(1)} collective-permute-done((bf16[64,1024]{1,0:T(8,128)(2,1)S(1)}, bf16[64,1024]{1,0:T(8,128)(2,1)S(1)}, u32[]{:S(2)}, u32[]{:S(2)}) %collective-permute-start.6) | collective-permute-done | bytes 131104 | tf_op jit(solution)/shard_map/ppermute | solution.py:328
  53.2 0.6 collective-permute-done.5.h1
  53.8 0.0 copy-done.2
  53.8 0.0 copy-done.3
  53.8 0.0 copy-done.8
  53.8 1.9 %pick.1 = (bf16[64,8,256]{2,1,0:T(8,128)(2,1)S(1)}, bf16[64,1024]{1,0:T(8,128)(2,1)S(1)}) custom-call(s32[2]{0:T(128)S(1)} %pad_add_fusion.ids, bf16[64,1024]{1,0:T(8,128)(2,1)S(1)} %conv.1.x0, bf16[64,1024]{1,0:T(8,128)(2,1)S(1)} %collective-permute-done.2.x1, bf16[64,1024]{1,0:T(8,128)(2,1)S(1)} %collective-permute-done.3.x2, ...), custom_call_target="tpu_custom_call" | custom-call | tf_op jit(solution)/shard_map/pick/pallas_call | solution.py:202
  55.8 0.0 copy-start.7
  55.8 18.5 %all_to_all.10.a0 = bf16[64,8,256]{2,1,0:T(8,128)(2,1)S(1)} all-to-all(bf16[64,8,256]{2,1,0:T(8,128)(2,1)S(1)} %get-tuple-element.8), channel_id=1, replica_groups=mesh['seg'=64,'ch'=4] {'seg'}, dimensions={0} | all-to-all | bytes 524288 | tf_op jit(solution)/shard_map/all_to_all | solution.py:348
  74.2 1.7 %collective-permute-start.10 = (bf16[64,8,256]{2,1,0:T(8,128)(2,1)S(1)}, bf16[64,8,256]{2,1,0:T(8,128)(2,1)S(1)}, u32[]{:S(2)}, u32[]{:S(2)}) collective-permute-start(bf16[64,8,256]{2,1,0:T(8,128)(2,1)S(1)} %all_to_all.10.a0), channel_id=1, source_target_pairs={{3,0},{0,1},{1,2},{2,3},{7,4},{4,5},{5,6},{6,7},{11,8},{8,9},{9,10... | collective-permute-start | bytes 786440 | tf_op jit(solution)/shard_map/ppermute | solution.py:328
  76.0 2.4 %collective-permute-start.9 = (bf16[64,8,256]{2,1,0:T(8,128)(2,1)S(1)}, bf16[64,8,256]{2,1,0:T(8,128)(2,1)S(1)}, u32[]{:S(2)}, u32[]{:S(2)}) collective-permute-start(bf16[64,8,256]{2,1,0:T(8,128)(2,1)S(1)} %all_to_all.10.a0), channel_id=1, source_target_pairs={{2,0},{3,1},{0,2},{1,3},{6,4},{7,5},{4,6},{5,7},{10,8},{11,9},{8,1... | collective-permute-start | bytes 786440 | tf_op jit(solution)/shard_map/ppermute | solution.py:328
  78.4 0.9 collective-permute-start.8
  79.3 4.5 %collective-permute-done.10.a3 = bf16[64,8,256]{2,1,0:T(8,128)(2,1)S(1)} collective-permute-done((bf16[64,8,256]{2,1,0:T(8,128)(2,1)S(1)}, bf16[64,8,256]{2,1,0:T(8,128)(2,1)S(1)}, u32[]{:S(2)}, u32[]{:S(2)}) %collective-permute-start.10) | collective-permute-done | bytes 262176 | tf_op jit(solution)/shard_map/ppermute | solution.py:328
  83.8 6.5 %collective-permute-done.9.a2 = bf16[64,8,256]{2,1,0:T(8,128)(2,1)S(1)} collective-permute-done((bf16[64,8,256]{2,1,0:T(8,128)(2,1)S(1)}, bf16[64,8,256]{2,1,0:T(8,128)(2,1)S(1)}, u32[]{:S(2)}, u32[]{:S(2)}) %collective-permute-start.9) | collective-permute-done | bytes 262176 | tf_op jit(solution)/shard_map/ppermute | solution.py:328
  90.3 0.0 collective-permute-done.8.a1
  90.3 0.0 copy-done.7
  90.3 19.5 %second.1 = bf16[64,16,128]{2,1,0:T(8,128)(2,1)S(1)} custom-call(s32[2]{0:T(128)S(1)} %pad_add_fusion.ids, s32[64,64]{1,0:T(8,128)S(1)} %copy-done.2, bf16[64,8,256]{2,1,0:T(8,128)(2,1)S(1)} %all_to_all.10.a0, bf16[64,8,256]{2,1,0:T(8,128)(2,1)S(1)} %collective-permute-done.8.a1, bf16[64,8,256]{2,1,0:T(8,128)(2,1)S(1)} %collective-permute-done.9.a2, ...), custom_call_target="tpu_custom_call" | custom-call | tf_op jit(solution)/shard_map/second/pallas_call | solution.py:259
  109.9 17.6 %all_to_all.11.back_ref = bf16[64,16,128]{2,1,0:T(8,128)(2,1)S(1)} all-to-all(bf16[64,16,128]{2,1,0:T(8,128)(2,1)S(1)} %second.1), channel_id=1, replica_groups=mesh['seg'=64,'ch'=4] {'seg'}, dimensions={0} | all-to-all | bytes 524288 | tf_op jit(solution)/shard_map/all_to_all | solution.py:350
  127.5 0.0 copy-start.4
  127.5 6.4 %home.1.h0 = bf16[64,1024]{1,0:T(8,128)(2,1)S(1)} custom-call(s32[2]{0:T(128)S(1)} %pad_add_fusion.ids, s32[64,64]{1,0:T(8,128)S(1)} %copy-done.2, bf16[64,16,128]{2,1,0:T(8,128)(2,1)S(1)} %all_to_all.11.back_ref, s32[1,1024]{1,0:T(1,128)S(1)} %copy-done.8), custom_call_target="tpu_custom_call" | custom-call | tf_op jit(solution)/shard_map/home/pallas_call | solution.py:293
  133.9 1.5 %collective-permute-start.13 = (bf16[64,1024]{1,0:T(8,128)(2,1)S(1)}, bf16[64,1024]{1,0:T(8,128)(2,1)S(1)}, u32[]{:S(2)}, u32[]{:S(2)}) collective-permute-start(bf16[64,1024]{1,0:T(8,128)(2,1)S(1)} %home.1.h0), channel_id=1, source_target_pairs={{3,0},{0,1},{1,2},{2,3},{7,4},{4,5},{5,6},{6,7},{11,8},{8,9},{9,10... | collective-permute-start | bytes 393224 | tf_op jit(solution)/shard_map/ppermute | solution.py:328
  135.4 2.4 %collective-permute-start.12 = (bf16[64,1024]{1,0:T(8,128)(2,1)S(1)}, bf16[64,1024]{1,0:T(8,128)(2,1)S(1)}, u32[]{:S(2)}, u32[]{:S(2)}) collective-permute-start(bf16[64,1024]{1,0:T(8,128)(2,1)S(1)} %home.1.h0), channel_id=1, source_target_pairs={{2,0},{3,1},{0,2},{1,3},{6,4},{7,5},{4,6},{5,7},{10,8},{11,9},{8,1... | collective-permute-start | bytes 393224 | tf_op jit(solution)/shard_map/ppermute | solution.py:328
  137.8 0.9 collective-permute-start.11
  138.7 2.2 %collective-permute-done.13.h3 = bf16[64,1024]{1,0:T(8,128)(2,1)S(1)} collective-permute-done((bf16[64,1024]{1,0:T(8,128)(2,1)S(1)}, bf16[64,1024]{1,0:T(8,128)(2,1)S(1)}, u32[]{:S(2)}, u32[]{:S(2)}) %collective-permute-start.13) | collective-permute-done | bytes 131104 | tf_op jit(solution)/shard_map/ppermute | solution.py:328
  141.0 3.1 %collective-permute-done.12.h2 = bf16[64,1024]{1,0:T(8,128)(2,1)S(1)} collective-permute-done((bf16[64,1024]{1,0:T(8,128)(2,1)S(1)}, bf16[64,1024]{1,0:T(8,128)(2,1)S(1)}, u32[]{:S(2)}, u32[]{:S(2)}) %collective-permute-start.12) | collective-permute-done | bytes 131104 | tf_op jit(solution)/shard_map/ppermute | solution.py:328
  144.1 0.0 collective-permute-done.11.h1
  144.1 0.0 copy-done.4
  144.1 1.6 %last.1 = bf16[64,1024]{1,0:T(8,128)(2,1)} custom-call(s32[2]{0:T(128)S(1)} %pad_add_fusion.ids, bf16[64,1024]{1,0:T(8,128)(2,1)S(1)} %get-tuple-element.7.mine_ref, bf16[64,1024]{1,0:T(8,128)(2,1)S(1)} %home.1.h0, bf16[64,1024]{1,0:T(8,128)(2,1)S(1)} %collective-permute-done.11.h1, bf16[64,1024]{1,0:T(8,128)(2,1)S(1)} %collective-permute-done.12.h2, ...), custom_call_target="tpu_custom_call" | custom-call | tf_op jit(solution)/shard_map/last/pallas_call | solution.py:315
Async XLA Ops:
  0.0 15.7 %copy-start.5 = (s32[27,1024]{1,0:T(8,128)S(1)}, s32[27,1024]{1,0:T(8,128)}, u32[]{:S(2)}) copy-start(s32[27,1024]{1,0:T(8,128)} %nb_ref.1) | copy-start | bytes 331780
  0.9 9.1 %collective-permute-start.1 = (bf16[128,256]{1,0:T(8,128)(2,1)S(1)}, bf16[128,256]{1,0:T(8,128)(2,1)S(1)}, u32[]{:S(2)}, u32[]{:S(2)}) collective-permute-start(bf16[128,256]{1,0:T(8,128)(2,1)S(1)} %get-tuple-element.9), channel_id=1, source_target_pairs={{4,0},{8,4},{12,8},{16,12},{20,16},{24,20},{28,24},{32,28},{36,32}... | collective-permute-start | bytes 196616 | tf_op jit(solution)/shard_map/ppermute | solution.py:341
  8.0 7.7 %collective-permute-start = (bf16[128,256]{1,0:T(8,128)(2,1)S(1)}, bf16[128,256]{1,0:T(8,128)(2,1)S(1)}, u32[]{:S(2)}, u32[]{:S(2)}) collective-permute-start(bf16[128,256]{1,0:T(8,128)(2,1)S(1)} %get-tuple-element.10), channel_id=1, source_target_pairs={{0,4},{4,8},{8,12},{12,16},{16,20},{20,24},{24,28},{28,32},{32,36}... | collective-permute-start | bytes 196616 | tf_op jit(solution)/shard_map/ppermute | solution.py:340
  15.7 1.2 copy-start
  16.9 1.0 copy-start.1
  17.9 18.3 %copy-start.6 = (bf16[256,3,64]{0,2,1:T(8,128)(2,1)S(1)}, bf16[256,3,64]{0,2,1:T(8,128)(2,1)}, u32[]{:S(2)}) copy-start(bf16[256,3,64]{0,2,1:T(8,128)(2,1)} %param.14) | copy-start | bytes 294916
  27.0 6.3 %collective-permute-start.4 = (bf16[64,1024]{1,0:T(8,128)(2,1)S(1)}, bf16[64,1024]{1,0:T(8,128)(2,1)S(1)}, u32[]{:S(2)}, u32[]{:S(2)}) collective-permute-start(bf16[64,1024]{1,0:T(8,128)(2,1)S(1)} %conv.1.x0), channel_id=1, source_target_pairs={{3,0},{0,1},{1,2},{2,3},{7,4},{4,5},{5,6},{6,7},{11,8},{8,9},{9,10... | collective-permute-start | bytes 393224 | tf_op jit(solution)/shard_map/ppermute | solution.py:328
  28.5 7.1 %collective-permute-start.3 = (bf16[64,1024]{1,0:T(8,128)(2,1)S(1)}, bf16[64,1024]{1,0:T(8,128)(2,1)S(1)}, u32[]{:S(2)}, u32[]{:S(2)}) collective-permute-start(bf16[64,1024]{1,0:T(8,128)(2,1)S(1)} %conv.1.x0), channel_id=1, source_target_pairs={{2,0},{3,1},{0,2},{1,3},{6,4},{7,5},{4,6},{5,7},{10,8},{11,9},{8,1... | collective-permute-start | bytes 393224 | tf_op jit(solution)/shard_map/ppermute | solution.py:328
  31.3 5.0 %collective-permute-start.2 = (bf16[64,1024]{1,0:T(8,128)(2,1)S(1)}, bf16[64,1024]{1,0:T(8,128)(2,1)S(1)}, u32[]{:S(2)}, u32[]{:S(2)}) collective-permute-start(bf16[64,1024]{1,0:T(8,128)(2,1)S(1)} %conv.1.x0), channel_id=1, source_target_pairs={{1,0},{2,1},{3,2},{0,3},{5,4},{6,5},{7,6},{4,7},{9,8},{10,9},{11,1... | collective-permute-start | bytes 393224 | tf_op jit(solution)/shard_map/ppermute | solution.py:328
  36.3 17.6 %copy-start.2 = (s32[64,64]{1,0:T(8,128)S(1)}, s32[64,64]{1,0:T(8,128)}, u32[]{:S(2)}) copy-start(s32[64,64]{1,0:T(8,128)} %counts_sm.3) | copy-start | bytes 49156
  36.3 17.6 %copy-start.3 = (bf16[256,256]{1,0:T(8,128)(2,1)S(1)}, bf16[256,256]{1,0:T(8,128)(2,1)}, u32[]{:S(2)}) copy-start(bf16[256,256]{1,0:T(8,128)(2,1)} %wo_ref.2) | copy-start | bytes 393220
  36.3 17.6 %copy-start.8 = (s32[1,1024]{1,0:T(1,128)S(1)}, s32[1,1024]{1,0:T(1,128)}, u32[]{:S(2)}) copy-start(s32[1,1024]{1,0:T(1,128)} %perm_ref.3) | copy-start | bytes 12292
  44.7 6.3 %collective-permute-start.7 = (bf16[64,1024]{1,0:T(8,128)(2,1)S(1)}, bf16[64,1024]{1,0:T(8,128)(2,1)S(1)}, u32[]{:S(2)}, u32[]{:S(2)}) collective-permute-start(bf16[64,1024]{1,0:T(8,128)(2,1)S(1)} %first.1.h0), channel_id=1, source_target_pairs={{3,0},{0,1},{1,2},{2,3},{7,4},{4,5},{5,6},{6,7},{11,8},{8,9},{9,10... | collective-permute-start | bytes 393224 | tf_op jit(solution)/shard_map/ppermute | solution.py:328
  46.0 7.2 %collective-permute-start.6 = (bf16[64,1024]{1,0:T(8,128)(2,1)S(1)}, bf16[64,1024]{1,0:T(8,128)(2,1)S(1)}, u32[]{:S(2)}, u32[]{:S(2)}) collective-permute-start(bf16[64,1024]{1,0:T(8,128)(2,1)S(1)} %first.1.h0), channel_id=1, source_target_pairs={{2,0},{3,1},{0,2},{1,3},{6,4},{7,5},{4,6},{5,7},{10,8},{11,9},{8,1... | collective-permute-start | bytes 393224 | tf_op jit(solution)/shard_map/ppermute | solution.py:328
  48.9 5.0 %collective-permute-start.5 = (bf16[64,1024]{1,0:T(8,128)(2,1)S(1)}, bf16[64,1024]{1,0:T(8,128)(2,1)S(1)}, u32[]{:S(2)}, u32[]{:S(2)}) collective-permute-start(bf16[64,1024]{1,0:T(8,128)(2,1)S(1)} %first.1.h0), channel_id=1, source_target_pairs={{1,0},{2,1},{3,2},{0,3},{5,4},{6,5},{7,6},{4,7},{9,8},{10,9},{11,1... | collective-permute-start | bytes 393224 | tf_op jit(solution)/shard_map/ppermute | solution.py:328
  55.8 34.6 %copy-start.7 = (bf16[256,3,64]{0,2,1:T(8,128)(2,1)S(1)}, bf16[256,3,64]{0,2,1:T(8,128)(2,1)}, u32[]{:S(2)}) copy-start(bf16[256,3,64]{0,2,1:T(8,128)(2,1)} %param.16) | copy-start | bytes 294916
  74.2 9.6 %collective-permute-start.10 = (bf16[64,8,256]{2,1,0:T(8,128)(2,1)S(1)}, bf16[64,8,256]{2,1,0:T(8,128)(2,1)S(1)}, u32[]{:S(2)}, u32[]{:S(2)}) collective-permute-start(bf16[64,8,256]{2,1,0:T(8,128)(2,1)S(1)} %all_to_all.10.a0), channel_id=1, source_target_pairs={{3,0},{0,1},{1,2},{2,3},{7,4},{4,5},{5,6},{6,7},{11,8},{8,9},{9,10... | collective-permute-start | bytes 786440 | tf_op jit(solution)/shard_map/ppermute | solution.py:328
  76.0 14.3 %collective-permute-start.9 = (bf16[64,8,256]{2,1,0:T(8,128)(2,1)S(1)}, bf16[64,8,256]{2,1,0:T(8,128)(2,1)S(1)}, u32[]{:S(2)}, u32[]{:S(2)}) collective-permute-start(bf16[64,8,256]{2,1,0:T(8,128)(2,1)S(1)} %all_to_all.10.a0), channel_id=1, source_target_pairs={{2,0},{3,1},{0,2},{1,3},{6,4},{7,5},{4,6},{5,7},{10,8},{11,9},{8,1... | collective-permute-start | bytes 786440 | tf_op jit(solution)/shard_map/ppermute | solution.py:328
  78.4 11.9 %collective-permute-start.8 = (bf16[64,8,256]{2,1,0:T(8,128)(2,1)S(1)}, bf16[64,8,256]{2,1,0:T(8,128)(2,1)S(1)}, u32[]{:S(2)}, u32[]{:S(2)}) collective-permute-start(bf16[64,8,256]{2,1,0:T(8,128)(2,1)S(1)} %all_to_all.10.a0), channel_id=1, source_target_pairs={{1,0},{2,1},{3,2},{0,3},{5,4},{6,5},{7,6},{4,7},{9,8},{10,9},{11,1... | collective-permute-start | bytes 786440 | tf_op jit(solution)/shard_map/ppermute | solution.py:328
  127.5 16.6 %copy-start.4 = (bf16[256,256]{1,0:T(8,128)(2,1)S(1)}, bf16[256,256]{1,0:T(8,128)(2,1)}, u32[]{:S(2)}) copy-start(bf16[256,256]{1,0:T(8,128)(2,1)} %wo_ref.3) | copy-start | bytes 393220
  133.9 7.1 %collective-permute-start.13 = (bf16[64,1024]{1,0:T(8,128)(2,1)S(1)}, bf16[64,1024]{1,0:T(8,128)(2,1)S(1)}, u32[]{:S(2)}, u32[]{:S(2)}) collective-permute-start(bf16[64,1024]{1,0:T(8,128)(2,1)S(1)} %home.1.h0), channel_id=1, source_target_pairs={{3,0},{0,1},{1,2},{2,3},{7,4},{4,5},{5,6},{6,7},{11,8},{8,9},{9,10... | collective-permute-start | bytes 393224 | tf_op jit(solution)/shard_map/ppermute | solution.py:328
  135.4 8.7 %collective-permute-start.12 = (bf16[64,1024]{1,0:T(8,128)(2,1)S(1)}, bf16[64,1024]{1,0:T(8,128)(2,1)S(1)}, u32[]{:S(2)}, u32[]{:S(2)}) collective-permute-start(bf16[64,1024]{1,0:T(8,128)(2,1)S(1)} %home.1.h0), channel_id=1, source_target_pairs={{2,0},{3,1},{0,2},{1,3},{6,4},{7,5},{4,6},{5,7},{10,8},{11,9},{8,1... | collective-permute-start | bytes 393224 | tf_op jit(solution)/shard_map/ppermute | solution.py:328
  137.8 6.3 %collective-permute-start.11 = (bf16[64,1024]{1,0:T(8,128)(2,1)S(1)}, bf16[64,1024]{1,0:T(8,128)(2,1)S(1)}, u32[]{:S(2)}, u32[]{:S(2)}) collective-permute-start(bf16[64,1024]{1,0:T(8,128)(2,1)S(1)} %home.1.h0), channel_id=1, source_target_pairs={{1,0},{2,1},{3,2},{0,3},{5,4},{6,5},{7,6},{4,7},{9,8},{10,9},{11,1... | collective-permute-start | bytes 393224 | tf_op jit(solution)/shard_map/ppermute | solution.py:328

commit v2 on v1

v2 whole, which is shorter than its diff:
```python
import jax
import jax.numpy as jnp
import numpy as np
from jax import lax
from jax.experimental import pallas as pl
from jax.experimental.pallas import tpu as pltpu
from jax.sharding import PartitionSpec as P

BF = jnp.bfloat16
F32 = jnp.float32
I32 = jnp.int32
HALO = 128
KOFF = 27
EPS = 1e-05
DEAD = -1e30
EXP_SCALE = float(16 ** (-0.5) * np.log2(np.e))
NT = (((1,), (1,)), ((), ()))
TN = (((0,), (0,)), ((), ()))
VM = pl.BlockSpec(memory_space=pltpu.VMEM)
SM = pl.BlockSpec(memory_space=pltpu.SMEM)
PARAMS = pltpu.CompilerParams(vmem_limit_bytes=50 << 20)


def cost(us):
    return pl.CostEstimate(flops=int(us * 500e6), bytes_accessed=1 << 20, transcendentals=0)


def iota(shape, dim):
    return lax.broadcasted_iota(I32, shape, dim)


def one_where(cond):
    return jnp.where(cond, 1.0, 0.0)


def norm_columns(x):
    centre = x - jnp.mean(x, axis=0, keepdims=True)
    spread = jnp.mean(centre * centre, axis=0, keepdims=True)
    return (centre * lax.rsqrt(spread + EPS)).astype(BF)


def in_eights(step, start):
    def eight(i, carry):
        for j in range(8):
            carry = step(i * 8 + j, carry)
        return carry

    return lax.fori_loop(0, 8, eight, start)


def place(pieces, ch, full_ref):
    size = pieces[0].shape[0]
    for j, piece in enumerate(pieces):
        owner = (ch + j) & 3
        full_ref[pl.ds(pl.multiple_of(owner * size, size), size), :] = piece[...]


def conv_kernel(ids, own_ref, nb_ref, w_ref, out_ref, y_ref, nbs_ref):
    base = ids[0] * 1024 - HALO
    ch = ids[1]
    for b in range(8):
        nbs_ref[b * 32 : b * 32 + KOFF, :] = nb_ref[:, b * 128 : (b + 1) * 128]
    chosen = one_where(iota((64, 256), 1) == iota((64, 256), 0) + ch * 64).astype(BF)
    out_ref[...] = lax.dot_general(chosen, own_ref[...], NT, preferred_element_type=F32)

    def transform(k, slot):
        w = w_ref[k]
        for j in range(4):
            y_ref[slot, :, j * 256 : (j + 1) * 256] = lax.dot_general(
                w, own_ref[j * 256 : (j + 1) * 256], NT, preferred_element_type=F32
            )

    def collect(k, slot):
        for b in range(8):
            target = nbs_ref[pl.ds(b * 32 + k, 8, stride=0), :]
            r = target - (base + b * 128)
            there = target >= 0
            if b == 0:
                there = there & (r >= 128)
            if b == 7:
                there = there & (r < 256)
            lane = r & 127
            first = r < 128
            second = r < 256
            for g in range(8):
                t = [
                    jnp.take_along_axis(
                        y_ref[slot, g * 8 : g * 8 + 8, (b + j - 1) * 128 : (b + j) * 128],
                        lane,
                        axis=1,
                        mode="promise_in_bounds",
                    )
                    if 0 <= b + j - 1 < 8
                    else None
                    for j in range(3)
                ]
                v = t[1] if t[2] is None else t[2]
                if t[2] is not None:
                    v = jnp.where(second, t[1], t[2])
                if t[0] is not None:
                    v = jnp.where(first, t[0], v)
                out_ref[g * 8 : g * 8 + 8, b * 128 : (b + 1) * 128] += jnp.where(there, v, 0.0)

    transform(0, 0)

    def body(i, carry):
        transform(2 * i + 1, 1)
        collect(2 * i, 0)
        transform(2 * i + 2, 0)
        collect(2 * i + 1, 1)
        return carry

    lax.fori_loop(0, KOFF // 2, body, 0)
    collect(KOFF - 1, 0)


def conv(ids, own, nb, w):
    return pl.pallas_call(
        conv_kernel,
        name="conv",
        out_shape=jax.ShapeDtypeStruct((64, 1024), F32),
        in_specs=[SM] + [VM] * 3,
        out_specs=VM,
        scratch_shapes=[pltpu.VMEM((2, 64, 1024), F32), pltpu.VMEM((264, 128), I32)],
        compiler_params=PARAMS,
        cost_estimate=cost(8),
    )(ids, own, nb, w)


def edge_kernel(ids, prev_ref, next_ref, nb_ref, w_ref, sum_ref, out_ref, y_ref, acc_ref, nbs_ref):
    base = ids[0] * 1024 - HALO
    for i, b in enumerate((0, 7)):
        nbs_ref[i * 32 : i * 32 + KOFF, :] = nb_ref[:, b * 128 : (b + 1) * 128]
        acc_ref[:, i * 128 : (i + 1) * 128] = sum_ref[:, b * 128 : (b + 1) * 128]
    ends = jnp.concatenate([prev_ref[...], next_ref[...]], 0)
    for i in range(3):
        w = w_ref[i * 9 : (i + 1) * 9].reshape(576, 256)
        y = lax.dot_general(w, ends, NT, preferred_element_type=F32)
        y_ref[i * 9 : (i + 1) * 9] = y.reshape(9, 64, 256)

    def collect(k):
        for i, b in enumerate((0, 7)):
            target = nbs_ref[pl.ds(i * 32 + k, 8, stride=0), :]
            r = target - (base + b * 128)
            there = (target >= 0) & ((r < 128) if b == 0 else (r >= 256))
            lane = r & 127
            for g in range(8):
                at = (slice(g * 8, g * 8 + 8), slice(i * 128, (i + 1) * 128))
                v = jnp.take_along_axis(
                    y_ref[k, at[0], at[1]], lane, axis=1, mode="promise_in_bounds"
                )
                acc_ref[at] += jnp.where(there, v, 0.0)

    def body(i, carry):
        for j in range(3):
            collect(i * 3 + j)
        return carry

    lax.fori_loop(0, 9, body, 0)
    out_ref[:, 128:896] = sum_ref[:, 128:896].astype(BF)
    for i, b in enumerate((0, 7)):
        out_ref[:, b * 128 : (b + 1) * 128] = acc_ref[:, i * 128 : (i + 1) * 128].astype(BF)


def edge(ids, prev, nxt, nb, w, total):
    return pl.pallas_call(
        edge_kernel,
        name="edge",
        out_shape=jax.ShapeDtypeStruct((64, 1024), BF),
        in_specs=[SM] + [VM] * 5,
        out_specs=VM,
        scratch_shapes=[
            pltpu.VMEM((KOFF, 64, 256), F32),
            pltpu.VMEM((64, 256), F32),
            pltpu.VMEM((72, 128), I32),
        ],
        compiler_params=PARAMS,
        cost_estimate=cost(2),
    )(ids, prev, nxt, nb, w, total)


def prep_kernel(ids, after_ref, wo_ref, perm_ref, counts_ref, pick_ref, home_ref, own_ref):
    seg = ids[0]
    ch = ids[1]
    counts = counts_ref[...].astype(F32)
    row = jnp.sum(jnp.where(iota((64, 64), 0) == seg, counts, 0.0), axis=0, keepdims=True)
    slot = iota((512, 64), 0)
    before = jnp.where(iota((512, 64), 1) < (slot >> 3), row, 0.0)
    position = jnp.sum(before, axis=1, keepdims=True).astype(I32)
    position = position + ch * 8 + (iota((512, 1), 0) & 7)
    perm = perm_ref[...].astype(F32)
    hit = iota((512, 1024), 1) == position
    source = jnp.sum(jnp.where(hit, perm, 0.0), axis=1, keepdims=True).astype(I32)
    pick_ref[...] = one_where(iota((512, 1024), 1) == source).astype(BF)
    home_ref[...] = one_where(iota((1024, 1024), 0) == perm_ref[...]).astype(BF)
    chosen = one_where(iota((64, 256), 1) == iota((64, 256), 0) + ch * 64).astype(BF)
    own = lax.dot_general(chosen, wo_ref[...], NT, preferred_element_type=F32)
    own_ref[...] = own.astype(BF)


def prep(ids, after, wo, perm, counts):
    return pl.pallas_call(
        prep_kernel,
        name="prep",
        out_shape=(
            jax.ShapeDtypeStruct((512, 1024), BF),
            jax.ShapeDtypeStruct((1024, 1024), BF),
            jax.ShapeDtypeStruct((64, 256), BF),
        ),
        in_specs=[SM, pl.BlockSpec(memory_space=pl.ANY)] + [VM] * 3,
        out_specs=(VM, VM, VM),
        compiler_params=PARAMS,
        cost_estimate=cost(3),
    )(ids, after, wo, perm, counts)


def stage_heads(qkv, bias, q_ref, k_ref, v_ref):
    rows = qkv.shape[1]
    qkv16 = qkv.astype(BF)
    ones = jnp.ones((16, rows), BF)
    values = jnp.concatenate([qkv16[128:192], jnp.ones((64, rows), BF)], 0).T
    owner = (iota((1, 128), 1) & 63) >> 4
    for h in range(4):
        mine = qkv16[h * 16 : (h + 1) * 16]
        k_ref[h, 0:16, :] = qkv16[64 + h * 16 : 80 + h * 16]
        if bias is not None:
            mine = jnp.concatenate([mine, ones], 0)
            k_ref[h, 16:32, :] = bias
        q_ref[h] = mine.T
        v_ref[h] = jnp.where(owner == h, values, jnp.zeros_like(values))


def attend(q_ref, k_ref, v_ref, patch, qb, block):
    start = patch * 1024
    if not isinstance(start, int):
        start = pl.multiple_of(start, 1024)
    rows = pl.ds(start + qb * block, block)
    keys = pl.ds(start, 1024)
    def score(h):
        return jnp.dot(q_ref[h, rows, :], k_ref[h, :, keys], preferred_element_type=F32)

    def weigh(s):
        peak = jnp.max(s, axis=1, keepdims=True)
        return jnp.exp2((s - peak) * EXP_SCALE).astype(BF)

    ss = [score(h) for h in range(4)]
    ps = [weigh(s) for s in ss]
    total = jnp.dot(jnp.concatenate(ps, 1), jnp.concatenate([v_ref[h, keys, :] for h in range(4)], 0), preferred_element_type=F32)
    return total / pltpu.roll(total, 64, 1)


def first_kernel(ids, x0, x1, x2, x3, w_ref, out_ref, full_ref, q_ref, k_ref, v_ref):
    place((x0, x1, x2, x3), ids[1], full_ref)
    normed = norm_columns(full_ref[...].astype(F32))
    qkv = jnp.dot(w_ref[...], normed, preferred_element_type=F32)
    stage_heads(qkv, None, q_ref, k_ref, v_ref)
    for qb in range(4):
        o = attend(q_ref, k_ref, v_ref, 0, qb, 256)
        out_ref[:, qb * 256 : (qb + 1) * 256] = o.T[:64].astype(BF)


def first(ids, pieces, w):
    return pl.pallas_call(
        first_kernel,
        name="first",
        out_shape=jax.ShapeDtypeStruct((64, 1024), BF),
        in_specs=[SM] + [VM] * 5,
        out_specs=VM,
        scratch_shapes=[
            pltpu.VMEM((256, 1024), BF),
            pltpu.VMEM((4, 1024, 16), BF),
            pltpu.VMEM((4, 16, 1024), BF),
            pltpu.VMEM((4, 1024, 128), BF),
        ],
        compiler_params=PARAMS,
    )(ids, *pieces, w)


def pick_kernel(ids, x0, x1, x2, x3, h0, h1, h2, h3, wo_ref, chosen_ref, send_ref, mine_ref, full_ref, heads_ref):
    ch = ids[1]
    place((x0, x1, x2, x3), ch, full_ref)
    place((h0, h1, h2, h3), ch, heads_ref)
    mixed = full_ref[...].astype(F32) + lax.dot_general(
        wo_ref[...], heads_ref[...], TN, preferred_element_type=F32
    )
    mixed16 = mixed.astype(BF)
    full_ref[...] = mixed16
    mine_ref[...] = full_ref[pl.ds(pl.multiple_of(ch * 64, 64), 64), :]
    normed = norm_columns(mixed16.astype(F32))
    rows = lax.dot_general(chosen_ref[...], normed, NT, preferred_element_type=F32)
    send_ref[...] = rows.astype(BF).reshape(64, 8, 256)


def pick(ids, mixed, heads, wo, chosen):
    return pl.pallas_call(
        pick_kernel,
        name="pick",
        out_shape=(
            jax.ShapeDtypeStruct((64, 8, 256), BF),
            jax.ShapeDtypeStruct((64, 1024), BF),
        ),
        in_specs=[SM] + [VM] * 10,
        out_specs=(VM, VM),
        scratch_shapes=[pltpu.VMEM((256, 1024), BF), pltpu.VMEM((256, 1024), BF)],
        compiler_params=PARAMS,
        cost_estimate=cost(2),
    )(ids, *mixed, *heads, wo, chosen)


def second_kernel(
    ids, counts_sm, a0, a1, a2, a3, w_ref, out_ref, lo_ref, hi_ref, q_ref, k_ref, v_ref, o_ref
):
    seg = ids[0]
    ch = ids[1]
    lo_ref[...] = jnp.zeros(lo_ref.shape, F32)
    hi_ref[...] = jnp.zeros(hi_ref.shape, F32)

    def compact(s, off):
        tiles = [piece[s].astype(F32) for piece in (a0, a1, a2, a3)]
        for j, tile in enumerate(tiles):
            dst = pl.ds(off + ((ch + j) & 3) * 8, 8)
            lo_ref[dst, :] = tile[:, :128]
            hi_ref[dst, :] = tile[:, 128:]
        return off + counts_sm[s, seg]

    live = in_eights(compact, 0)
    rows = jnp.concatenate([lo_ref[0:2048, :], hi_ref[0:2048, :]], 1).astype(BF)
    qkv = lax.dot_general(w_ref[...], rows, NT, preferred_element_type=F32)
    dead = (iota((16, 2048), 1) >= live) & (iota((16, 2048), 0) == 0)
    bias = jnp.where(dead, DEAD, 0.0).astype(BF)
    stage_heads(qkv, bias, q_ref, k_ref, v_ref)
    o_ref[2048:2080, :] = jnp.zeros((32, 128), F32)

    def block(i, carry):
        o = attend(q_ref, k_ref, v_ref, i >> 2, i & 3, 256)
        both = jnp.where(iota((1, 128), 1) < 64, o, pltpu.roll(o, 64, 1))
        o_ref[pl.ds(pl.multiple_of(i * 256, 256), 256), :] = both
        return carry

    lax.fori_loop(0, 8, block, 0)
    low = iota((16, 128), 1) < 64

    def give(s, off):
        top = o_ref[pl.ds(off, 16), :]
        end = o_ref[pl.ds(off + 16, 16), :]
        out_ref[s] = jnp.where(low, top, end).astype(BF)
        return off + counts_sm[s, seg]

    in_eights(give, 0)


def second(ids, counts, arrived, w):
    return pl.pallas_call(
        second_kernel,
        name="second",
        out_shape=jax.ShapeDtypeStruct((64, 16, 128), BF),
        in_specs=[SM, SM] + [VM] * 5,
        out_specs=VM,
        scratch_shapes=[
            pltpu.VMEM((2080, 128), F32),
            pltpu.VMEM((2080, 128), F32),
            pltpu.VMEM((4, 2048, 32), BF),
            pltpu.VMEM((4, 32, 2048), BF),
            pltpu.VMEM((4, 2048, 128), BF),
            pltpu.VMEM((2080, 128), F32),
        ],
        compiler_params=PARAMS,
    )(ids, counts, *arrived, w)


def home_kernel(ids, counts_sm, back_ref, chosen_ref, out_ref, sorted_ref):
    seg = ids[0]

    def put(t, off):
        tile = back_ref[t].astype(F32)
        sorted_ref[pl.ds(off, 16), :] = tile
        sorted_ref[pl.ds(off + 16, 16), :] = pltpu.roll(tile, 64, 1)
        return off + counts_sm[seg, t]

    in_eights(put, 0)
    rows = jnp.dot(chosen_ref[...], sorted_ref[0:1024, :].astype(BF), preferred_element_type=F32)
    out_ref[...] = rows.T[:64].astype(BF)


def home(ids, counts, back, chosen):
    return pl.pallas_call(
        home_kernel,
        name="home",
        out_shape=jax.ShapeDtypeStruct((64, 1024), BF),
        in_specs=[SM, SM, VM, VM],
        out_specs=VM,
        scratch_shapes=[pltpu.VMEM((1056, 128), F32)],
        compiler_params=PARAMS,
    )(ids, counts, back, chosen)


def last_kernel(ids, mine_ref, h0, h1, h2, h3, wo_ref, out_ref, heads_ref):
    place((h0, h1, h2, h3), ids[1], heads_ref)
    own = jnp.dot(wo_ref[...], heads_ref[...], preferred_element_type=F32)
    out_ref[...] = (mine_ref[...].astype(F32) + own).astype(BF)


def last(ids, mine, heads, wo):
    return pl.pallas_call(
        last_kernel,
        name="last",
        out_shape=jax.ShapeDtypeStruct((64, 1024), BF),
        in_specs=[SM] + [VM] * 6,
        out_specs=VM,
        scratch_shapes=[pltpu.VMEM((256, 1024), BF)],
        compiler_params=PARAMS,
    )(ids, mine, *heads, wo)


def spread(piece):
    def moved(step):
        return lax.ppermute(piece, "ch", [((i + step) % 4, i) for i in range(4)])

    return piece, moved(1), moved(2), moved(3)


def local(
    voxels, neighbours, send_perm, send_counts, conv_weight, qkv_first, out_first, qkv_second, out_second
):
    seg_count = lax.axis_size("seg")
    ids = jnp.stack([lax.axis_index("seg"), lax.axis_index("ch")]).astype(I32)
    up = [(i, i + 1) for i in range(seg_count - 1)]
    down = [(i + 1, i) for i in range(seg_count - 1)]
    prev = lax.ppermute(voxels[-HALO:], "seg", up)
    nxt = lax.ppermute(voxels[:HALO], "seg", down)
    conv_w = jnp.swapaxes(conv_weight, 1, 2)
    w_first = jnp.transpose(qkv_first, (1, 2, 0)).reshape(192, 256)
    w_second = jnp.transpose(qkv_second, (1, 2, 0)).reshape(192, 256)
    own_sum = conv(ids, voxels, neighbours, conv_w)
    mixed_part = edge(ids, prev, nxt, neighbours, conv_w, own_sum)
    mixed_a = spread(mixed_part)
    pick_rows, home_rows, own_out = prep(ids, mixed_part, out_second, send_perm, send_counts)
    heads_a = spread(first(ids, mixed_a, w_first))
    outgoing, mine = pick(ids, mixed_a, heads_a, out_first, pick_rows)
    arrived = lax.all_to_all(outgoing, "seg", split_axis=0, concat_axis=0, tiled=True)
    going = second(ids, send_counts, spread(arrived), w_second)
    back = lax.all_to_all(going, "seg", split_axis=0, concat_axis=0, tiled=True)
    heads_b = spread(home(ids, send_counts, back, home_rows))
    return jnp.swapaxes(last(ids, mine, heads_b, own_out), 0, 1)


def solution(mesh):
    placed = (
        P("seg", None),
        P(None, "seg"),
        P("seg", None),
        P(),
        P(None, None, "ch"),
        P(None, None, "ch"),
        P(),
        P(None, None, "ch"),
        P(),
    )
    return jax.shard_map(
        local, mesh=mesh, in_specs=placed, out_specs=P("seg", "ch"), check_vma=False
    )
```

time: 147 us -> 136 us (0.925)
  Pallas kernels: 46.9 us -> 38.7 us
  waiting for transfers between devices: 29.8 us -> 21.8 us
  blocking collectives: 36.1 us -> 39.6 us
    ppermute x1, waiting for transfers between devices: 5.68 us -> 0.01 us  [local(): prev = lax.ppermute(voxels[-HALO:], 'seg', up)]
    pallas_call x1, Pallas kernels: 19.5 us -> 14.7 us  [second(): pl.pallas_call(second_kernel, name='second', out_shape=jax.ShapeDtypeStru...]
    pallas_call x1, Pallas kernels: 6.41 us -> 2.47 us  [home(): pl.pallas_call(home_kernel, name='home', out_shape=jax.ShapeDtypeStruct((...]
    pallas_call x0 -> x2, Pallas kernels: none -> 3.91 us  [the longest x1 2.24 us: edge(): pl.pallas_call(edge_kernel, name='edge', out_shape=jax.ShapeDtypeStruct((...]
    all_to_all x1, blocking collectives: 18.5 us -> 22 us  [local(): lax.all_to_all(outgoing, 'seg', split_axis=0, concat_axis=0, tiled=True)]
    ppermute x12, waiting for transfers between devices: 24.1 us -> 21.8 us  [moved(): return lax.ppermute(piece, 'ch', [((i + step) % 4, i) for i in range(4)])]
    pallas_call x1, Pallas kernels: 8.41 us -> 6.23 us  [first(): pl.pallas_call(first_kernel, name='first', out_shape=jax.ShapeDtypeStruct...]
    unnamed x18 -> x20, local copies, waits for them, and re-layouts: 2.24 us -> 3.15 us
  transfers between devices with their start and end apart: 14 -> 14, of which waited for: 11 -> 9; matrix products, arithmetic and copies ran while one was open for 0% -> 0% of each run, Pallas kernels for 0% -> 7%
where the time goes in v2:
time: 136 us; the launch traced here: 135 us
  blocking collectives  39.6 us (29%)
  Pallas kernels  38.7 us (28%)
  starting transfers between devices  30.2 us (22%)
  waiting for transfers between devices  21.8 us (16%)
  local copies, waits for them, and re-layouts  4.03 us (3%)
    all_to_all x1, blocking collectives, local(): lax.all_to_all(outgoing, 'seg', split_axis=0, concat_axis=0, tiled=True)  22 us
    ppermute x12, waiting for transfers between devices, moved(): return lax.ppermute(piece, 'ch', [((i + step) % 4, i) for i in range(4)])  21.8 us
    ppermute x12, starting transfers between devices, moved(): return lax.ppermute(piece, 'ch', [((i + step) % 4, i) for i in range(4)])  21.2 us
    all_to_all x1, blocking collectives, local(): back = lax.all_to_all(going, 'seg', split_axis=0, concat_axis=0, tiled=True)  17.6 us
    pallas_call x1, Pallas kernels, second(): pl.pallas_call(second_kernel, name='second', out_shape=jax.ShapeDtypeStru...  14.7 us
    pallas_call x1, Pallas kernels, conv(): pl.pallas_call(conv_kernel, name='conv', out_shape=jax.ShapeDtypeStruct((...  8.35 us
    ppermute x1, starting transfers between devices, local(): nxt = lax.ppermute(voxels[:HALO], 'seg', down)  7.09 us
    pallas_call x1, Pallas kernels, first(): pl.pallas_call(first_kernel, name='first', out_shape=jax.ShapeDtypeStruct...  6.23 us
  transfers between devices with their start and end apart: 14, of which 9 were waited for; matrix products, arithmetic and copies ran while one was open for 0% of the time, Pallas kernels for 7%

profile of v2, /device:TPU:8, one launch (start us, length us, event | category | flops | bytes accessed | tf_op | source)
XLA Modules:
  0.0 134.6 jit_solution(5060967404768278486)
XLA Ops:
  0.0 0.9 fusion
  0.9 7.1 %collective-permute-start.1 = (bf16[128,256]{1,0:T(8,128)(2,1)S(1)}, bf16[128,256]{1,0:T(8,128)(2,1)S(1)}, u32[]{:S(2)}, u32[]{:S(2)}) collective-permute-start(bf16[128,256]{1,0:T(8,128)(2,1)S(1)} %get-tuple-element.15), channel_id=1, source_target_pairs={{4,0},{8,4},{12,8},{16,12},{20,16},{24,20},{28,24},{32,28},{36,32}... | collective-permute-start | bytes 196616 | tf_op jit(solution)/shard_map/ppermute | solution.py:430
  8.0 1.9 %collective-permute-start = (bf16[128,256]{1,0:T(8,128)(2,1)S(1)}, bf16[128,256]{1,0:T(8,128)(2,1)S(1)}, u32[]{:S(2)}, u32[]{:S(2)}) collective-permute-start(bf16[128,256]{1,0:T(8,128)(2,1)S(1)} %get-tuple-element.16), channel_id=1, source_target_pairs={{0,4},{4,8},{8,12},{12,16},{16,20},{20,24},{24,28},{28,32},{32,36}... | collective-permute-start | bytes 196616 | tf_op jit(solution)/shard_map/ppermute | solution.py:429
  9.9 0.1 pad_add_fusion.ids
  10.0 0.0 copy-start.3
  10.0 1.0 copy-done.3
  11.0 0.0 copy-start.4
  11.0 1.2 copy-done.4
  12.2 0.0 copy-start.6
  12.2 0.9 copy-done.6
  13.1 0.0 copy-start.5
  13.1 8.4 %conv.1.sum_ref = f32[64,1024]{1,0:T(8,128)S(1)} custom-call(s32[2]{0:T(128)S(1)} %pad_add_fusion.ids, bf16[1024,256]{1,0:T(8,128)(2,1)S(1)} %copy-done.3, s32[27,1024]{1,0:T(8,128)S(1)} %copy-done.6, bf16[27,64,256]{2,1,0:T(8,128)(2,1)S(1)} %bitcast.12), custom_call_target="tpu_custom_call" | custom-call | flops 4000000000 | bytes 1048576 | tf_op jit(solution)/shard_map/conv/pallas_call | solution.py:118
  21.5 0.0 copy-start.1
  21.5 0.0 copy-start
  21.5 0.0 copy-start.7
  21.5 0.0 copy-start.9
  21.5 0.0 collective-permute-done.1.next_ref
  21.5 0.0 collective-permute-done.prev_ref
  21.5 0.0 copy-done.5
  21.5 2.2 %edge.1.x0.after_ref = bf16[64,1024]{1,0:T(8,128)(2,1)S(1)} custom-call(s32[2]{0:T(128)S(1)} %pad_add_fusion.ids, bf16[128,256]{1,0:T(8,128)(2,1)S(1)} %collective-permute-done.prev_ref, bf16[128,256]{1,0:T(8,128)(2,1)S(1)} %collective-permute-done.1.next_ref, s32[27,1024]{1,0:T(8,128)S(1)} %copy-done.6, bf16[27,64,256]{2,1,0:T(8,128)(2,1)S(1)} %bitcast.13, ...), custom_call_target="tpu_custom_call" | custom-call | flops 1000000000 | bytes 1048576 | tf_op jit(solution)/shard_map/edge/pallas_call | solution.py:166
  23.8 1.6 %collective-permute-start.4 = (bf16[64,1024]{1,0:T(8,128)(2,1)S(1)}, bf16[64,1024]{1,0:T(8,128)(2,1)S(1)}, u32[]{:S(2)}, u32[]{:S(2)}) collective-permute-start(bf16[64,1024]{1,0:T(8,128)(2,1)S(1)} %edge.1.x0.after_ref), channel_id=1, source_target_pairs={{3,0},{0,1},{1,2},{2,3},{7,4},{4,5},{5,6},{6,7},{11,8},{8,9},{9,10... | collective-permute-start | bytes 393224 | tf_op jit(solution)/shard_map/ppermute | solution.py:417
  25.4 2.7 %collective-permute-start.3 = (bf16[64,1024]{1,0:T(8,128)(2,1)S(1)}, bf16[64,1024]{1,0:T(8,128)(2,1)S(1)}, u32[]{:S(2)}, u32[]{:S(2)}) collective-permute-start(bf16[64,1024]{1,0:T(8,128)(2,1)S(1)} %edge.1.x0.after_ref), channel_id=1, source_target_pairs={{2,0},{3,1},{0,2},{1,3},{6,4},{7,5},{4,6},{5,7},{10,8},{11,9},{8,1... | collective-permute-start | bytes 393224 | tf_op jit(solution)/shard_map/ppermute | solution.py:417
  28.1 1.4 %collective-permute-start.2 = (bf16[64,1024]{1,0:T(8,128)(2,1)S(1)}, bf16[64,1024]{1,0:T(8,128)(2,1)S(1)}, u32[]{:S(2)}, u32[]{:S(2)}) collective-permute-start(bf16[64,1024]{1,0:T(8,128)(2,1)S(1)} %edge.1.x0.after_ref), channel_id=1, source_target_pairs={{1,0},{2,1},{3,2},{0,3},{5,4},{6,5},{7,6},{4,7},{9,8},{10,9},{11,1... | collective-permute-start | bytes 393224 | tf_op jit(solution)/shard_map/ppermute | solution.py:417
  29.5 0.5 collective-permute-done.4.x3
  30.1 2.4 %collective-permute-done.3.x2 = bf16[64,1024]{1,0:T(8,128)(2,1)S(1)} collective-permute-done((bf16[64,1024]{1,0:T(8,128)(2,1)S(1)}, bf16[64,1024]{1,0:T(8,128)(2,1)S(1)}, u32[]{:S(2)}, u32[]{:S(2)}) %collective-permute-start.3) | collective-permute-done | bytes 131104 | tf_op jit(solution)/shard_map/ppermute | solution.py:417
  32.4 0.6 collective-permute-done.2.x1
  33.1 0.0 copy-done.1
  33.1 6.2 %first.1.h0 = bf16[64,1024]{1,0:T(8,128)(2,1)S(1)} custom-call(s32[2]{0:T(128)S(1)} %pad_add_fusion.ids, bf16[64,1024]{1,0:T(8,128)(2,1)S(1)} %edge.1.x0.after_ref, bf16[64,1024]{1,0:T(8,128)(2,1)S(1)} %collective-permute-done.2.x1, bf16[64,1024]{1,0:T(8,128)(2,1)S(1)} %collective-permute-done.3.x2, bf16[64,1024]{1,0:T(8,128)(2,1)S(1)} %collective-permute-done.4.x3, ...), custom_call_target="tpu_custom_call" | custom-call | tf_op jit(solution)/shard_map/first/pallas_call | solution.py:263
  39.3 0.0 copy-start.8
  39.3 1.4 %collective-permute-start.7 = (bf16[64,1024]{1,0:T(8,128)(2,1)S(1)}, bf16[64,1024]{1,0:T(8,128)(2,1)S(1)}, u32[]{:S(2)}, u32[]{:S(2)}) collective-permute-start(bf16[64,1024]{1,0:T(8,128)(2,1)S(1)} %first.1.h0), channel_id=1, source_target_pairs={{3,0},{0,1},{1,2},{2,3},{7,4},{4,5},{5,6},{6,7},{11,8},{8,9},{9,10... | collective-permute-start | bytes 393224 | tf_op jit(solution)/shard_map/ppermute | solution.py:417
  40.7 2.8 %collective-permute-start.6 = (bf16[64,1024]{1,0:T(8,128)(2,1)S(1)}, bf16[64,1024]{1,0:T(8,128)(2,1)S(1)}, u32[]{:S(2)}, u32[]{:S(2)}) collective-permute-start(bf16[64,1024]{1,0:T(8,128)(2,1)S(1)} %first.1.h0), channel_id=1, source_target_pairs={{2,0},{3,1},{0,2},{1,3},{6,4},{7,5},{4,6},{5,7},{10,8},{11,9},{8,1... | collective-permute-start | bytes 393224 | tf_op jit(solution)/shard_map/ppermute | solution.py:417
  43.5 0.8 collective-permute-start.5
  44.3 0.0 copy-done
  44.3 0.0 copy-done.7
  44.4 0.0 copy-done.9
  44.4 1.7 %prep.1 = (bf16[512,1024]{1,0:T(8,128)(2,1)S(1)}, bf16[1024,1024]{1,0:T(8,128)(2,1)S(1)}, bf16[64,256]{1,0:T(8,128)(2,1)S(1)}) custom-call(s32[2]{0:T(128)S(1)} %pad_add_fusion.ids, bf16[64,1024]{1,0:T(8,128)(2,1)S(1)} %edge.1.x0.after_ref, bf16[256,256]{1,0:T(8,128)(2,1)S(1)} %copy-done.7, s32[1,1024]{1,0:T(1,128)S(1)} %copy-done.9, s32[64,64]{1,0:T(8,128)S(1)} %copy-done), custom_call_target="tpu_custom_call" | custom-call | flops 1500000000 | bytes 1048576 | tf_op jit(solution)/shard_map/prep/pallas_call | solution.py:202
  46.0 0.0 collective-permute-done.7.h3
  46.0 1.8 %collective-permute-done.6.h2 = bf16[64,1024]{1,0:T(8,128)(2,1)S(1)} collective-permute-done((bf16[64,1024]{1,0:T(8,128)(2,1)S(1)}, bf16[64,1024]{1,0:T(8,128)(2,1)S(1)}, u32[]{:S(2)}, u32[]{:S(2)}) %collective-permute-start.6) | collective-permute-done | bytes 131104 | tf_op jit(solution)/shard_map/ppermute | solution.py:417
  47.8 0.6 collective-permute-done.5.h1
  48.5 0.0 copy-done.8
  48.5 0.0 copy-start.2
  48.5 1.6 %pick.1 = (bf16[64,8,256]{2,1,0:T(8,128)(2,1)S(1)}, bf16[64,1024]{1,0:T(8,128)(2,1)S(1)}) custom-call(s32[2]{0:T(128)S(1)} %pad_add_fusion.ids, bf16[64,1024]{1,0:T(8,128)(2,1)S(1)} %edge.1.x0.after_ref, bf16[64,1024]{1,0:T(8,128)(2,1)S(1)} %collective-permute-done.2.x1, bf16[64,1024]{1,0:T(8,128)(2,1)S(1)} %collective-permute-done.3.x2, ...), custom_call_target="tpu_custom_call" | custom-call | flops 1000000000 | bytes 1048576 | tf_op jit(solution)/shard_map/pick/pallas_call | solution.py:295
  50.1 22.0 %all_to_all.10.a0 = bf16[64,8,256]{2,1,0:T(8,128)(2,1)S(1)} all-to-all(bf16[64,8,256]{2,1,0:T(8,128)(2,1)S(1)} %get-tuple-element.12), channel_id=1, replica_groups=mesh['seg'=64,'ch'=4] {'seg'}, dimensions={0} | all-to-all | bytes 524288 | tf_op jit(solution)/shard_map/all_to_all | solution.py:440
  72.1 1.7 %collective-permute-start.10 = (bf16[64,8,256]{2,1,0:T(8,128)(2,1)S(1)}, bf16[64,8,256]{2,1,0:T(8,128)(2,1)S(1)}, u32[]{:S(2)}, u32[]{:S(2)}) collective-permute-start(bf16[64,8,256]{2,1,0:T(8,128)(2,1)S(1)} %all_to_all.10.a0), channel_id=1, source_target_pairs={{3,0},{0,1},{1,2},{2,3},{7,4},{4,5},{5,6},{6,7},{11,8},{8,9},{9,10... | collective-permute-start | bytes 786440 | tf_op jit(solution)/shard_map/ppermute | solution.py:417
  73.7 2.4 %collective-permute-start.9 = (bf16[64,8,256]{2,1,0:T(8,128)(2,1)S(1)}, bf16[64,8,256]{2,1,0:T(8,128)(2,1)S(1)}, u32[]{:S(2)}, u32[]{:S(2)}) collective-permute-start(bf16[64,8,256]{2,1,0:T(8,128)(2,1)S(1)} %all_to_all.10.a0), channel_id=1, source_target_pairs={{2,0},{3,1},{0,2},{1,3},{6,4},{7,5},{4,6},{5,7},{10,8},{11,9},{8,1... | collective-permute-start | bytes 786440 | tf_op jit(solution)/shard_map/ppermute | solution.py:417
  76.1 1.2 collective-permute-start.8
  77.3 4.3 %collective-permute-done.10.a3 = bf16[64,8,256]{2,1,0:T(8,128)(2,1)S(1)} collective-permute-done((bf16[64,8,256]{2,1,0:T(8,128)(2,1)S(1)}, bf16[64,8,256]{2,1,0:T(8,128)(2,1)S(1)}, u32[]{:S(2)}, u32[]{:S(2)}) %collective-permute-start.10) | collective-permute-done | bytes 262176 | tf_op jit(solution)/shard_map/ppermute | solution.py:417
  81.7 6.4 %collective-permute-done.9.a2 = bf16[64,8,256]{2,1,0:T(8,128)(2,1)S(1)} collective-permute-done((bf16[64,8,256]{2,1,0:T(8,128)(2,1)S(1)}, bf16[64,8,256]{2,1,0:T(8,128)(2,1)S(1)}, u32[]{:S(2)}, u32[]{:S(2)}) %collective-permute-start.9) | collective-permute-done | bytes 262176 | tf_op jit(solution)/shard_map/ppermute | solution.py:417
  88.1 0.0 collective-permute-done.8.a1
  88.1 0.0 copy-done.2
  88.1 14.7 %second.1 = bf16[64,16,128]{2,1,0:T(8,128)(2,1)S(1)} custom-call(s32[2]{0:T(128)S(1)} %pad_add_fusion.ids, s32[64,64]{1,0:T(8,128)S(1)} %copy-done, bf16[64,8,256]{2,1,0:T(8,128)(2,1)S(1)} %all_to_all.10.a0, bf16[64,8,256]{2,1,0:T(8,128)(2,1)S(1)} %collective-permute-done.8.a1, bf16[64,8,256]{2,1,0:T(8,128)(2,1)S(1)} %collective-permute-done.9.a2, ...), custom_call_target="tpu_custom_call" | custom-call | tf_op jit(solution)/shard_map/second/pallas_call | solution.py:353
  102.7 17.6 %all_to_all.11.back_ref = bf16[64,16,128]{2,1,0:T(8,128)(2,1)S(1)} all-to-all(bf16[64,16,128]{2,1,0:T(8,128)(2,1)S(1)} %second.1), channel_id=1, replica_groups=mesh['seg'=64,'ch'=4] {'seg'}, dimensions={0} | all-to-all | bytes 524288 | tf_op jit(solution)/shard_map/all_to_all | solution.py:442
  120.3 2.5 %home.1.h0 = bf16[64,1024]{1,0:T(8,128)(2,1)S(1)} custom-call(s32[2]{0:T(128)S(1)} %pad_add_fusion.ids, s32[64,64]{1,0:T(8,128)S(1)} %copy-done, bf16[64,16,128]{2,1,0:T(8,128)(2,1)S(1)} %all_to_all.11.back_ref, bf16[1024,1024]{1,0:T(8,128)(2,1)S(1)} %get-tuple-element.13.chosen_ref), custom_call_target="tpu_custom_call" | custom-call | tf_op jit(solution)/shard_map/home/pallas_call | solution.py:386
  122.8 1.6 %collective-permute-start.13 = (bf16[64,1024]{1,0:T(8,128)(2,1)S(1)}, bf16[64,1024]{1,0:T(8,128)(2,1)S(1)}, u32[]{:S(2)}, u32[]{:S(2)}) collective-permute-start(bf16[64,1024]{1,0:T(8,128)(2,1)S(1)} %home.1.h0), channel_id=1, source_target_pairs={{3,0},{0,1},{1,2},{2,3},{7,4},{4,5},{5,6},{6,7},{11,8},{8,9},{9,10... | collective-permute-start | bytes 393224 | tf_op jit(solution)/shard_map/ppermute | solution.py:417
  124.4 2.4 %collective-permute-start.12 = (bf16[64,1024]{1,0:T(8,128)(2,1)S(1)}, bf16[64,1024]{1,0:T(8,128)(2,1)S(1)}, u32[]{:S(2)}, u32[]{:S(2)}) collective-permute-start(bf16[64,1024]{1,0:T(8,128)(2,1)S(1)} %home.1.h0), channel_id=1, source_target_pairs={{2,0},{3,1},{0,2},{1,3},{6,4},{7,5},{4,6},{5,7},{10,8},{11,9},{8,1... | collective-permute-start | bytes 393224 | tf_op jit(solution)/shard_map/ppermute | solution.py:417
  126.8 1.2 collective-permute-start.11
  128.0 1.8 %collective-permute-done.13.h3 = bf16[64,1024]{1,0:T(8,128)(2,1)S(1)} collective-permute-done((bf16[64,1024]{1,0:T(8,128)(2,1)S(1)}, bf16[64,1024]{1,0:T(8,128)(2,1)S(1)}, u32[]{:S(2)}, u32[]{:S(2)}) %collective-permute-start.13) | collective-permute-done | bytes 131104 | tf_op jit(solution)/shard_map/ppermute | solution.py:417
  129.8 3.3 %collective-permute-done.12.h2 = bf16[64,1024]{1,0:T(8,128)(2,1)S(1)} collective-permute-done((bf16[64,1024]{1,0:T(8,128)(2,1)S(1)}, bf16[64,1024]{1,0:T(8,128)(2,1)S(1)}, u32[]{:S(2)}, u32[]{:S(2)}) %collective-permute-start.12) | collective-permute-done | bytes 131104 | tf_op jit(solution)/shard_map/ppermute | solution.py:417
  133.1 0.0 collective-permute-done.11.h1
  133.1 1.5 %last.1 = bf16[64,1024]{1,0:T(8,128)(2,1)} custom-call(s32[2]{0:T(128)S(1)} %pad_add_fusion.ids, bf16[64,1024]{1,0:T(8,128)(2,1)S(1)} %get-tuple-element.11.mine_ref, bf16[64,1024]{1,0:T(8,128)(2,1)S(1)} %home.1.h0, bf16[64,1024]{1,0:T(8,128)(2,1)S(1)} %collective-permute-done.11.h1, bf16[64,1024]{1,0:T(8,128)(2,1)S(1)} %collective-permute-done.12.h2, ...), custom_call_target="tpu_custom_call" | custom-call | tf_op jit(solution)/shard_map/last/pallas_call | solution.py:404
Async XLA Ops:
  0.9 20.6 %collective-permute-start.1 = (bf16[128,256]{1,0:T(8,128)(2,1)S(1)}, bf16[128,256]{1,0:T(8,128)(2,1)S(1)}, u32[]{:S(2)}, u32[]{:S(2)}) collective-permute-start(bf16[128,256]{1,0:T(8,128)(2,1)S(1)} %get-tuple-element.15), channel_id=1, source_target_pairs={{4,0},{8,4},{12,8},{16,12},{20,16},{24,20},{28,24},{32,28},{36,32}... | collective-permute-start | bytes 196616 | tf_op jit(solution)/shard_map/ppermute | solution.py:430
  8.0 13.5 %collective-permute-start = (bf16[128,256]{1,0:T(8,128)(2,1)S(1)}, bf16[128,256]{1,0:T(8,128)(2,1)S(1)}, u32[]{:S(2)}, u32[]{:S(2)}) collective-permute-start(bf16[128,256]{1,0:T(8,128)(2,1)S(1)} %get-tuple-element.16), channel_id=1, source_target_pairs={{0,4},{4,8},{8,12},{12,16},{16,20},{20,24},{24,28},{28,32},{32,36}... | collective-permute-start | bytes 196616 | tf_op jit(solution)/shard_map/ppermute | solution.py:429
  10.0 1.0 copy-start.3
  11.0 1.2 copy-start.4
  12.2 0.9 copy-start.6
  13.1 8.4 %copy-start.5 = (bf16[27,256,64]{1,2,0:T(8,128)(2,1)S(1)}, bf16[27,256,64]{1,2,0:T(8,128)(2,1)}, u32[]{:S(2)}) copy-start(bf16[27,256,64]{1,2,0:T(8,128)(2,1)} %param.13) | copy-start | bytes 2654212
  21.5 11.6 %copy-start.1 = (bf16[256,3,64]{0,2,1:T(8,128)(2,1)S(1)}, bf16[256,3,64]{0,2,1:T(8,128)(2,1)}, u32[]{:S(2)}) copy-start(bf16[256,3,64]{0,2,1:T(8,128)(2,1)} %param.14) | copy-start | bytes 294916
  21.5 22.9 %copy-start = (s32[64,64]{1,0:T(8,128)S(1)}, s32[64,64]{1,0:T(8,128)}, u32[]{:S(2)}) copy-start(s32[64,64]{1,0:T(8,128)} %counts_sm.3) | copy-start | bytes 49156
  21.5 22.9 %copy-start.7 = (bf16[256,256]{1,0:T(8,128)(2,1)S(1)}, bf16[256,256]{1,0:T(8,128)(2,1)}, u32[]{:S(2)}) copy-start(bf16[256,256]{1,0:T(8,128)(2,1)} %wo_ref.2) | copy-start | bytes 393220
  21.5 22.8 %copy-start.9 = (s32[1,1024]{1,0:T(1,128)S(1)}, s32[1,1024]{1,0:T(1,128)}, u32[]{:S(2)}) copy-start(s32[1,1024]{1,0:T(1,128)} %perm_ref.1) | copy-start | bytes 12292
  23.8 6.3 %collective-permute-start.4 = (bf16[64,1024]{1,0:T(8,128)(2,1)S(1)}, bf16[64,1024]{1,0:T(8,128)(2,1)S(1)}, u32[]{:S(2)}, u32[]{:S(2)}) collective-permute-start(bf16[64,1024]{1,0:T(8,128)(2,1)S(1)} %edge.1.x0.after_ref), channel_id=1, source_target_pairs={{3,0},{0,1},{1,2},{2,3},{7,4},{4,5},{5,6},{6,7},{11,8},{8,9},{9,10... | collective-permute-start | bytes 393224 | tf_op jit(solution)/shard_map/ppermute | solution.py:417
  25.4 7.1 %collective-permute-start.3 = (bf16[64,1024]{1,0:T(8,128)(2,1)S(1)}, bf16[64,1024]{1,0:T(8,128)(2,1)S(1)}, u32[]{:S(2)}, u32[]{:S(2)}) collective-permute-start(bf16[64,1024]{1,0:T(8,128)(2,1)S(1)} %edge.1.x0.after_ref), channel_id=1, source_target_pairs={{2,0},{3,1},{0,2},{1,3},{6,4},{7,5},{4,6},{5,7},{10,8},{11,9},{8,1... | collective-permute-start | bytes 393224 | tf_op jit(solution)/shard_map/ppermute | solution.py:417
  28.1 5.0 %collective-permute-start.2 = (bf16[64,1024]{1,0:T(8,128)(2,1)S(1)}, bf16[64,1024]{1,0:T(8,128)(2,1)S(1)}, u32[]{:S(2)}, u32[]{:S(2)}) collective-permute-start(bf16[64,1024]{1,0:T(8,128)(2,1)S(1)} %edge.1.x0.after_ref), channel_id=1, source_target_pairs={{1,0},{2,1},{3,2},{0,3},{5,4},{6,5},{7,6},{4,7},{9,8},{10,9},{11,1... | collective-permute-start | bytes 393224 | tf_op jit(solution)/shard_map/ppermute | solution.py:417
  39.3 9.2 %copy-start.8 = (bf16[256,256]{1,0:T(8,128)(2,1)S(1)}, bf16[256,256]{1,0:T(8,128)(2,1)}, u32[]{:S(2)}) copy-start(bf16[256,256]{1,0:T(8,128)(2,1)} %wo_ref.3) | copy-start | bytes 393220
  39.3 6.7 %collective-permute-start.7 = (bf16[64,1024]{1,0:T(8,128)(2,1)S(1)}, bf16[64,1024]{1,0:T(8,128)(2,1)S(1)}, u32[]{:S(2)}, u32[]{:S(2)}) collective-permute-start(bf16[64,1024]{1,0:T(8,128)(2,1)S(1)} %first.1.h0), channel_id=1, source_target_pairs={{3,0},{0,1},{1,2},{2,3},{7,4},{4,5},{5,6},{6,7},{11,8},{8,9},{9,10... | collective-permute-start | bytes 393224 | tf_op jit(solution)/shard_map/ppermute | solution.py:417
  40.7 7.2 %collective-permute-start.6 = (bf16[64,1024]{1,0:T(8,128)(2,1)S(1)}, bf16[64,1024]{1,0:T(8,128)(2,1)S(1)}, u32[]{:S(2)}, u32[]{:S(2)}) collective-permute-start(bf16[64,1024]{1,0:T(8,128)(2,1)S(1)} %first.1.h0), channel_id=1, source_target_pairs={{2,0},{3,1},{0,2},{1,3},{6,4},{7,5},{4,6},{5,7},{10,8},{11,9},{8,1... | collective-permute-start | bytes 393224 | tf_op jit(solution)/shard_map/ppermute | solution.py:417
  43.5 5.0 %collective-permute-start.5 = (bf16[64,1024]{1,0:T(8,128)(2,1)S(1)}, bf16[64,1024]{1,0:T(8,128)(2,1)S(1)}, u32[]{:S(2)}, u32[]{:S(2)}) collective-permute-start(bf16[64,1024]{1,0:T(8,128)(2,1)S(1)} %first.1.h0), channel_id=1, source_target_pairs={{1,0},{2,1},{3,2},{0,3},{5,4},{6,5},{7,6},{4,7},{9,8},{10,9},{11,1... | collective-permute-start | bytes 393224 | tf_op jit(solution)/shard_map/ppermute | solution.py:417
  48.5 39.6 %copy-start.2 = (bf16[256,3,64]{0,2,1:T(8,128)(2,1)S(1)}, bf16[256,3,64]{0,2,1:T(8,128)(2,1)}, u32[]{:S(2)}) copy-start(bf16[256,3,64]{0,2,1:T(8,128)(2,1)} %param.16) | copy-start | bytes 294916
  72.1 9.6 %collective-permute-start.10 = (bf16[64,8,256]{2,1,0:T(8,128)(2,1)S(1)}, bf16[64,8,256]{2,1,0:T(8,128)(2,1)S(1)}, u32[]{:S(2)}, u32[]{:S(2)}) collective-permute-start(bf16[64,8,256]{2,1,0:T(8,128)(2,1)S(1)} %all_to_all.10.a0), channel_id=1, source_target_pairs={{3,0},{0,1},{1,2},{2,3},{7,4},{4,5},{5,6},{6,7},{11,8},{8,9},{9,10... | collective-permute-start | bytes 786440 | tf_op jit(solution)/shard_map/ppermute | solution.py:417
  73.7 14.3 %collective-permute-start.9 = (bf16[64,8,256]{2,1,0:T(8,128)(2,1)S(1)}, bf16[64,8,256]{2,1,0:T(8,128)(2,1)S(1)}, u32[]{:S(2)}, u32[]{:S(2)}) collective-permute-start(bf16[64,8,256]{2,1,0:T(8,128)(2,1)S(1)} %all_to_all.10.a0), channel_id=1, source_target_pairs={{2,0},{3,1},{0,2},{1,3},{6,4},{7,5},{4,6},{5,7},{10,8},{11,9},{8,1... | collective-permute-start | bytes 786440 | tf_op jit(solution)/shard_map/ppermute | solution.py:417
  76.1 11.9 %collective-permute-start.8 = (bf16[64,8,256]{2,1,0:T(8,128)(2,1)S(1)}, bf16[64,8,256]{2,1,0:T(8,128)(2,1)S(1)}, u32[]{:S(2)}, u32[]{:S(2)}) collective-permute-start(bf16[64,8,256]{2,1,0:T(8,128)(2,1)S(1)} %all_to_all.10.a0), channel_id=1, source_target_pairs={{1,0},{2,1},{3,2},{0,3},{5,4},{6,5},{7,6},{4,7},{9,8},{10,9},{11,1... | collective-permute-start | bytes 786440 | tf_op jit(solution)/shard_map/ppermute | solution.py:417
  122.8 7.0 %collective-permute-start.13 = (bf16[64,1024]{1,0:T(8,128)(2,1)S(1)}, bf16[64,1024]{1,0:T(8,128)(2,1)S(1)}, u32[]{:S(2)}, u32[]{:S(2)}) collective-permute-start(bf16[64,1024]{1,0:T(8,128)(2,1)S(1)} %home.1.h0), channel_id=1, source_target_pairs={{3,0},{0,1},{1,2},{2,3},{7,4},{4,5},{5,6},{6,7},{11,8},{8,9},{9,10... | collective-permute-start | bytes 393224 | tf_op jit(solution)/shard_map/ppermute | solution.py:417
  124.4 8.7 %collective-permute-start.12 = (bf16[64,1024]{1,0:T(8,128)(2,1)S(1)}, bf16[64,1024]{1,0:T(8,128)(2,1)S(1)}, u32[]{:S(2)}, u32[]{:S(2)}) collective-permute-start(bf16[64,1024]{1,0:T(8,128)(2,1)S(1)} %home.1.h0), channel_id=1, source_target_pairs={{2,0},{3,1},{0,2},{1,3},{6,4},{7,5},{4,6},{5,7},{10,8},{11,9},{8,1... | collective-permute-start | bytes 393224 | tf_op jit(solution)/shard_map/ppermute | solution.py:417
  126.8 6.3 %collective-permute-start.11 = (bf16[64,1024]{1,0:T(8,128)(2,1)S(1)}, bf16[64,1024]{1,0:T(8,128)(2,1)S(1)}, u32[]{:S(2)}, u32[]{:S(2)}) collective-permute-start(bf16[64,1024]{1,0:T(8,128)(2,1)S(1)} %home.1.h0), channel_id=1, source_target_pairs={{1,0},{2,1},{3,2},{0,3},{5,4},{6,5},{7,6},{4,7},{9,8},{10,9},{11,1... | collective-permute-start | bytes 393224 | tf_op jit(solution)/shard_map/ppermute | solution.py:417

commit v3 on v2

--- a/solution.py
+++ b/solution.py
@@ -14,6 +14,8 @@
 EPS = 1e-05
 DEAD = -1e30
 EXP_SCALE = float(16 ** (-0.5) * np.log2(np.e))
+SAFE_BOUND = float((40.0 * 4) ** 2)
+TINY = 1e-30
 NT = (((1,), (1,)), ((), ()))
 TN = (((0,), (0,)), ((), ()))
 VM = pl.BlockSpec(memory_space=pltpu.VMEM)
@@ -218,45 +220,73 @@
     rows = qkv.shape[1]
     qkv16 = qkv.astype(BF)
     ones = jnp.ones((16, rows), BF)
-    values = jnp.concatenate([qkv16[128:192], jnp.ones((64, rows), BF)], 0).T
-    owner = (iota((1, 128), 1) & 63) >> 4
     for h in range(4):
-        mine = qkv16[h * 16 : (h + 1) * 16]
-        k_ref[h, 0:16, :] = qkv16[64 + h * 16 : 80 + h * 16]
+        key = qkv16[64 + h * 16 : 80 + h * 16]
+        q_ref[h, 0:16, :] = qkv16[h * 16 : (h + 1) * 16]
         if bias is not None:
-            mine = jnp.concatenate([mine, ones], 0)
-            k_ref[h, 16:32, :] = bias
-        q_ref[h] = mine.T
-        v_ref[h] = jnp.where(owner == h, values, jnp.zeros_like(values))
-
-
-def attend(q_ref, k_ref, v_ref, patch, qb, block):
-    start = patch * 1024
-    if not isinstance(start, int):
-        start = pl.multiple_of(start, 1024)
-    rows = pl.ds(start + qb * block, block)
-    keys = pl.ds(start, 1024)
-    def score(h):
-        return jnp.dot(q_ref[h, rows, :], k_ref[h, :, keys], preferred_element_type=F32)
-
-    def weigh(s):
-        peak = jnp.max(s, axis=1, keepdims=True)
-        return jnp.exp2((s - peak) * EXP_SCALE).astype(BF)
-
-    ss = [score(h) for h in range(4)]
-    ps = [weigh(s) for s in ss]
-    total = jnp.dot(jnp.concatenate(ps, 1), jnp.concatenate([v_ref[h, keys, :] for h in range(4)], 0), preferred_element_type=F32)
-    return total / pltpu.roll(total, 64, 1)
+            key = jnp.concatenate([key, bias], 0)
+            q_ref[h, 16:32, :] = ones
+        k_ref[h] = key.T
+        v_ref[h, 0:16, :] = qkv16[128 + h * 16 : 144 + h * 16]
+        v_ref[h, 16:32, :] = ones
+    square = qkv16[0:128].astype(F32)
+    square = square * square
+    longest = [
+        jnp.max(jnp.sum(square[i * 16 : (i + 1) * 16], axis=0, keepdims=True)) for i in range(8)
+    ]
+    bound = longest[0] * longest[4]
+    for h in range(1, 4):
+        bound = jnp.maximum(bound, longest[h] * longest[4 + h])
+    return bound <= SAFE_BOUND
+
+
+def attend(q_ref, k_ref, v_ref, out_ref, h, keys, cols, shifted):
+    s = jnp.dot(k_ref[h, keys, :], q_ref[h, :, cols], preferred_element_type=F32)
+    if shifted:
+        s = s - jnp.max(s, axis=0, keepdims=True)
+    p = jnp.exp2(s * EXP_SCALE).astype(BF)
+    o = jnp.dot(v_ref[h, :, keys], p, preferred_element_type=F32)
+    o = o[:16] / jnp.maximum(o[16:17], TINY)
+    at = h * 16 if isinstance(h, int) else pl.multiple_of(h * 16, 16)
+    out_ref[pl.ds(at, 16), cols] = o.astype(out_ref.dtype)
+
+
+def attend_all(safe, q_ref, k_ref, v_ref, out_ref, patches, block):
+    def window(start, size, aligned):
+        return pl.ds(start if isinstance(start, int) else pl.multiple_of(start, aligned), size)
+
+    @pl.when(safe)
+    def plain():
+        def patch(i, carry):
+            keys = window(i * 1024, 1024, 1024)
+            for qb in range(1024 // block):
+                cols = window(i * 1024 + qb * block, block, block)
+                for h in range(4):
+                    attend(q_ref, k_ref, v_ref, out_ref, h, keys, cols, False)
+            return carry
+
+        if patches == 1:
+            patch(0, 0)
+        else:
+            lax.fori_loop(0, patches, patch, 0)
+
+    @pl.when(jnp.logical_not(safe))
+    def with_peak():
+        def piece(i, carry):
+            keys = window((i >> 3) * 1024, 1024, 1024)
+            cols = window((i >> 3) * 1024 + (i & 1) * 512, 512, 512)
+            attend(q_ref, k_ref, v_ref, out_ref, (i >> 1) & 3, keys, cols, True)
+            return carry
+
+        lax.fori_loop(0, patches * 8, piece, 0)
 
 
 def first_kernel(ids, x0, x1, x2, x3, w_ref, out_ref, full_ref, q_ref, k_ref, v_ref):
     place((x0, x1, x2, x3), ids[1], full_ref)
     normed = norm_columns(full_ref[...].astype(F32))
     qkv = jnp.dot(w_ref[...], normed, preferred_element_type=F32)
-    stage_heads(qkv, None, q_ref, k_ref, v_ref)
-    for qb in range(4):
-        o = attend(q_ref, k_ref, v_ref, 0, qb, 256)
-        out_ref[:, qb * 256 : (qb + 1) * 256] = o.T[:64].astype(BF)
+    safe = stage_heads(qkv, None, q_ref, k_ref, v_ref)
+    attend_all(safe, q_ref, k_ref, v_ref, out_ref, 1, 512)
 
 
 def first(ids, pieces, w):
@@ -268,9 +298,9 @@
         out_specs=VM,
         scratch_shapes=[
             pltpu.VMEM((256, 1024), BF),
+            pltpu.VMEM((4, 16, 1024), BF),
             pltpu.VMEM((4, 1024, 16), BF),
-            pltpu.VMEM((4, 16, 1024), BF),
-            pltpu.VMEM((4, 1024, 128), BF),
+            pltpu.VMEM((4, 32, 1024), BF),
         ],
         compiler_params=PARAMS,
     )(ids, *pieces, w)
@@ -308,7 +338,7 @@
 
 
 def second_kernel(
-    ids, counts_sm, a0, a1, a2, a3, w_ref, out_ref, lo_ref, hi_ref, q_ref, k_ref, v_ref, o_ref
+    ids, counts_sm, a0, a1, a2, a3, w_ref, out_ref, lo_ref, hi_ref, q_ref, k_ref, v_ref, o_ref, heads_ref
 ):
     seg = ids[0]
     ch = ids[1]
@@ -328,16 +358,14 @@
     qkv = lax.dot_general(w_ref[...], rows, NT, preferred_element_type=F32)
     dead = (iota((16, 2048), 1) >= live) & (iota((16, 2048), 0) == 0)
     bias = jnp.where(dead, DEAD, 0.0).astype(BF)
-    stage_heads(qkv, bias, q_ref, k_ref, v_ref)
+    safe = stage_heads(qkv, bias, q_ref, k_ref, v_ref)
     o_ref[2048:2080, :] = jnp.zeros((32, 128), F32)
 
-    def block(i, carry):
-        o = attend(q_ref, k_ref, v_ref, i >> 2, i & 3, 256)
-        both = jnp.where(iota((1, 128), 1) < 64, o, pltpu.roll(o, 64, 1))
-        o_ref[pl.ds(pl.multiple_of(i * 256, 256), 256), :] = both
-        return carry
-
-    lax.fori_loop(0, 8, block, 0)
+    attend_all(safe, q_ref, k_ref, v_ref, heads_ref, 2, 1024)
+    for i in range(2):
+        rows = slice(i * 1024, (i + 1) * 1024)
+        o = heads_ref[:, rows]
+        o_ref[rows, :] = jnp.concatenate([o, o], 0).T
     low = iota((16, 128), 1) < 64
 
     def give(s, off):
@@ -359,10 +387,11 @@
         scratch_shapes=[
             pltpu.VMEM((2080, 128), F32),
             pltpu.VMEM((2080, 128), F32),
+            pltpu.VMEM((4, 32, 2048), BF),
             pltpu.VMEM((4, 2048, 32), BF),
             pltpu.VMEM((4, 32, 2048), BF),
-            pltpu.VMEM((4, 2048, 128), BF),
             pltpu.VMEM((2080, 128), F32),
+            pltpu.VMEM((64, 2048), F32),
         ],
         compiler_params=PARAMS,
     )(ids, counts, *arrived, w)

time: 136 us -> 144 us (1.059)
  Pallas kernels: 38.7 us -> 47.4 us
    pallas_call x1, Pallas kernels: 14.7 us -> 19.8 us  [second(): pl.pallas_call(second_kernel, name='second', out_shape=jax.ShapeDtypeStru...]
    pallas_call x1, Pallas kernels: 6.23 us -> 9.74 us  [first(): pl.pallas_call(first_kernel, name='first', out_shape=jax.ShapeDtypeStruct...]
where the time goes in v3:
time: 144 us; the launch traced here: 143 us
  Pallas kernels  47.4 us (33%)
  blocking collectives  39.7 us (28%)
  starting transfers between devices  30.2 us (21%)
  waiting for transfers between devices  21.8 us (15%)
  local copies, waits for them, and re-layouts  4.03 us (3%)
    all_to_all x1, blocking collectives, local(): lax.all_to_all(outgoing, 'seg', split_axis=0, concat_axis=0, tiled=True)  22 us
    ppermute x12, waiting for transfers between devices, moved(): return lax.ppermute(piece, 'ch', [((i + step) % 4, i) for i in range(4)])  21.8 us
    ppermute x12, starting transfers between devices, moved(): return lax.ppermute(piece, 'ch', [((i + step) % 4, i) for i in range(4)])  21.2 us
    pallas_call x1, Pallas kernels, second(): pl.pallas_call(second_kernel, name='second', out_shape=jax.ShapeDtypeStru...  19.8 us
    all_to_all x1, blocking collectives, local(): back = lax.all_to_all(going, 'seg', split_axis=0, concat_axis=0, tiled=True)  17.6 us
    pallas_call x1, Pallas kernels, first(): pl.pallas_call(first_kernel, name='first', out_shape=jax.ShapeDtypeStruct...  9.74 us
    pallas_call x1, Pallas kernels, conv(): pl.pallas_call(conv_kernel, name='conv', out_shape=jax.ShapeDtypeStruct((...  8.35 us
    ppermute x1, starting transfers between devices, local(): nxt = lax.ppermute(voxels[:HALO], 'seg', down)  7.09 us
  transfers between devices with their start and end apart: 14, of which 9 were waited for; matrix products, arithmetic and copies ran while one was open for 0% of the time, Pallas kernels for 7%

profile of v3, /device:TPU:8, one launch (start us, length us, event | category | flops | bytes accessed | tf_op | source)
XLA Modules:
  0.0 143.3 jit_solution(6733419590473104253)
XLA Ops:
  0.0 0.9 fusion
  0.9 7.1 %collective-permute-start.1 = (bf16[128,256]{1,0:T(8,128)(2,1)S(1)}, bf16[128,256]{1,0:T(8,128)(2,1)S(1)}, u32[]{:S(2)}, u32[]{:S(2)}) collective-permute-start(bf16[128,256]{1,0:T(8,128)(2,1)S(1)} %get-tuple-element.15), channel_id=1, source_target_pairs={{4,0},{8,4},{12,8},{16,12},{20,16},{24,20},{28,24},{32,28},{36,32}... | collective-permute-start | bytes 196616 | tf_op jit(solution)/shard_map/ppermute | solution.py:459
  8.0 1.9 %collective-permute-start = (bf16[128,256]{1,0:T(8,128)(2,1)S(1)}, bf16[128,256]{1,0:T(8,128)(2,1)S(1)}, u32[]{:S(2)}, u32[]{:S(2)}) collective-permute-start(bf16[128,256]{1,0:T(8,128)(2,1)S(1)} %get-tuple-element.16), channel_id=1, source_target_pairs={{0,4},{4,8},{8,12},{12,16},{16,20},{20,24},{24,28},{28,32},{32,36}... | collective-permute-start | bytes 196616 | tf_op jit(solution)/shard_map/ppermute | solution.py:458
  9.9 0.1 pad_add_fusion.ids
  10.0 0.0 copy-start.3
  10.0 1.0 copy-done.3
  11.0 0.0 copy-start.4
  11.0 1.2 copy-done.4
  12.2 0.0 copy-start.6
  12.2 0.9 copy-done.6
  13.1 0.0 copy-start.5
  13.1 8.4 %conv.1.sum_ref = f32[64,1024]{1,0:T(8,128)S(1)} custom-call(s32[2]{0:T(128)S(1)} %pad_add_fusion.ids, bf16[1024,256]{1,0:T(8,128)(2,1)S(1)} %copy-done.3, s32[27,1024]{1,0:T(8,128)S(1)} %copy-done.6, bf16[27,64,256]{2,1,0:T(8,128)(2,1)S(1)} %bitcast.12), custom_call_target="tpu_custom_call" | custom-call | flops 4000000000 | bytes 1048576 | tf_op jit(solution)/shard_map/conv/pallas_call | solution.py:120
  21.5 0.0 copy-start.1
  21.5 0.0 copy-start
  21.5 0.0 copy-start.7
  21.5 0.0 copy-start.9
  21.5 0.0 collective-permute-done.1.next_ref
  21.5 0.0 collective-permute-done.prev_ref
  21.5 0.0 copy-done.5
  21.5 2.2 %edge.1.x0.after_ref = bf16[64,1024]{1,0:T(8,128)(2,1)S(1)} custom-call(s32[2]{0:T(128)S(1)} %pad_add_fusion.ids, bf16[128,256]{1,0:T(8,128)(2,1)S(1)} %collective-permute-done.prev_ref, bf16[128,256]{1,0:T(8,128)(2,1)S(1)} %collective-permute-done.1.next_ref, s32[27,1024]{1,0:T(8,128)S(1)} %copy-done.6, bf16[27,64,256]{2,1,0:T(8,128)(2,1)S(1)} %bitcast.13, ...), custom_call_target="tpu_custom_call" | custom-call | flops 1000000000 | bytes 1048576 | tf_op jit(solution)/shard_map/edge/pallas_call | solution.py:168
  23.8 1.6 %collective-permute-start.4 = (bf16[64,1024]{1,0:T(8,128)(2,1)S(1)}, bf16[64,1024]{1,0:T(8,128)(2,1)S(1)}, u32[]{:S(2)}, u32[]{:S(2)}) collective-permute-start(bf16[64,1024]{1,0:T(8,128)(2,1)S(1)} %edge.1.x0.after_ref), channel_id=1, source_target_pairs={{3,0},{0,1},{1,2},{2,3},{7,4},{4,5},{5,6},{6,7},{11,8},{8,9},{9,10... | collective-permute-start | bytes 393224 | tf_op jit(solution)/shard_map/ppermute | solution.py:446
  25.4 2.7 %collective-permute-start.3 = (bf16[64,1024]{1,0:T(8,128)(2,1)S(1)}, bf16[64,1024]{1,0:T(8,128)(2,1)S(1)}, u32[]{:S(2)}, u32[]{:S(2)}) collective-permute-start(bf16[64,1024]{1,0:T(8,128)(2,1)S(1)} %edge.1.x0.after_ref), channel_id=1, source_target_pairs={{2,0},{3,1},{0,2},{1,3},{6,4},{7,5},{4,6},{5,7},{10,8},{11,9},{8,1... | collective-permute-start | bytes 393224 | tf_op jit(solution)/shard_map/ppermute | solution.py:446
  28.1 1.4 %collective-permute-start.2 = (bf16[64,1024]{1,0:T(8,128)(2,1)S(1)}, bf16[64,1024]{1,0:T(8,128)(2,1)S(1)}, u32[]{:S(2)}, u32[]{:S(2)}) collective-permute-start(bf16[64,1024]{1,0:T(8,128)(2,1)S(1)} %edge.1.x0.after_ref), channel_id=1, source_target_pairs={{1,0},{2,1},{3,2},{0,3},{5,4},{6,5},{7,6},{4,7},{9,8},{10,9},{11,1... | collective-permute-start | bytes 393224 | tf_op jit(solution)/shard_map/ppermute | solution.py:446
  29.5 0.5 collective-permute-done.4.x3
  30.1 2.4 %collective-permute-done.3.x2 = bf16[64,1024]{1,0:T(8,128)(2,1)S(1)} collective-permute-done((bf16[64,1024]{1,0:T(8,128)(2,1)S(1)}, bf16[64,1024]{1,0:T(8,128)(2,1)S(1)}, u32[]{:S(2)}, u32[]{:S(2)}) %collective-permute-start.3) | collective-permute-done | bytes 131104 | tf_op jit(solution)/shard_map/ppermute | solution.py:446
  32.4 0.6 collective-permute-done.2.x1
  33.1 0.0 copy-done.1
  33.1 9.7 %first.1.h0 = bf16[64,1024]{1,0:T(8,128)(2,1)S(1)} custom-call(s32[2]{0:T(128)S(1)} %pad_add_fusion.ids, bf16[64,1024]{1,0:T(8,128)(2,1)S(1)} %edge.1.x0.after_ref, bf16[64,1024]{1,0:T(8,128)(2,1)S(1)} %collective-permute-done.2.x1, bf16[64,1024]{1,0:T(8,128)(2,1)S(1)} %collective-permute-done.3.x2, bf16[64,1024]{1,0:T(8,128)(2,1)S(1)} %collective-permute-done.4.x3, ...), custom_call_target="tpu_custom_call" | custom-call | tf_op jit(solution)/shard_map/first/pallas_call | solution.py:293
  42.8 0.0 copy-start.8
  42.8 1.4 collective-permute-start.7
  44.2 2.8 %collective-permute-start.6 = (bf16[64,1024]{1,0:T(8,128)(2,1)S(1)}, bf16[64,1024]{1,0:T(8,128)(2,1)S(1)}, u32[]{:S(2)}, u32[]{:S(2)}) collective-permute-start(bf16[64,1024]{1,0:T(8,128)(2,1)S(1)} %first.1.h0), channel_id=1, source_target_pairs={{2,0},{3,1},{0,2},{1,3},{6,4},{7,5},{4,6},{5,7},{10,8},{11,9},{8,1... | collective-permute-start | bytes 393224 | tf_op jit(solution)/shard_map/ppermute | solution.py:446
  46.9 0.9 collective-permute-start.5
  47.9 0.0 copy-done
  47.9 0.0 copy-done.7
  47.9 0.0 copy-done.9
  47.9 1.7 %prep.1 = (bf16[512,1024]{1,0:T(8,128)(2,1)S(1)}, bf16[1024,1024]{1,0:T(8,128)(2,1)S(1)}, bf16[64,256]{1,0:T(8,128)(2,1)S(1)}) custom-call(s32[2]{0:T(128)S(1)} %pad_add_fusion.ids, bf16[64,1024]{1,0:T(8,128)(2,1)S(1)} %edge.1.x0.after_ref, bf16[256,256]{1,0:T(8,128)(2,1)S(1)} %copy-done.7, s32[1,1024]{1,0:T(1,128)S(1)} %copy-done.9, s32[64,64]{1,0:T(8,128)S(1)} %copy-done), custom_call_target="tpu_custom_call" | custom-call | flops 1500000000 | bytes 1048576 | tf_op jit(solution)/shard_map/prep/pallas_call | solution.py:204
  49.5 0.0 collective-permute-done.7.h3
  49.5 1.7 %collective-permute-done.6.h2 = bf16[64,1024]{1,0:T(8,128)(2,1)S(1)} collective-permute-done((bf16[64,1024]{1,0:T(8,128)(2,1)S(1)}, bf16[64,1024]{1,0:T(8,128)(2,1)S(1)}, u32[]{:S(2)}, u32[]{:S(2)}) %collective-permute-start.6) | collective-permute-done | bytes 131104 | tf_op jit(solution)/shard_map/ppermute | solution.py:446
  51.3 0.6 collective-permute-done.5.h1
  51.9 0.0 copy-done.8
  51.9 0.0 copy-start.2
  51.9 1.6 %pick.1 = (bf16[64,8,256]{2,1,0:T(8,128)(2,1)S(1)}, bf16[64,1024]{1,0:T(8,128)(2,1)S(1)}) custom-call(s32[2]{0:T(128)S(1)} %pad_add_fusion.ids, bf16[64,1024]{1,0:T(8,128)(2,1)S(1)} %edge.1.x0.after_ref, bf16[64,1024]{1,0:T(8,128)(2,1)S(1)} %collective-permute-done.2.x1, bf16[64,1024]{1,0:T(8,128)(2,1)S(1)} %collective-permute-done.3.x2, ...), custom_call_target="tpu_custom_call" | custom-call | flops 1000000000 | bytes 1048576 | tf_op jit(solution)/shard_map/pick/pallas_call | solution.py:325
  53.6 22.0 %all_to_all.10.a0 = bf16[64,8,256]{2,1,0:T(8,128)(2,1)S(1)} all-to-all(bf16[64,8,256]{2,1,0:T(8,128)(2,1)S(1)} %get-tuple-element.12), channel_id=1, replica_groups=mesh['seg'=64,'ch'=4] {'seg'}, dimensions={0} | all-to-all | bytes 524288 | tf_op jit(solution)/shard_map/all_to_all | solution.py:469
  75.6 1.7 %collective-permute-start.10 = (bf16[64,8,256]{2,1,0:T(8,128)(2,1)S(1)}, bf16[64,8,256]{2,1,0:T(8,128)(2,1)S(1)}, u32[]{:S(2)}, u32[]{:S(2)}) collective-permute-start(bf16[64,8,256]{2,1,0:T(8,128)(2,1)S(1)} %all_to_all.10.a0), channel_id=1, source_target_pairs={{3,0},{0,1},{1,2},{2,3},{7,4},{4,5},{5,6},{6,7},{11,8},{8,9},{9,10... | collective-permute-start | bytes 786440 | tf_op jit(solution)/shard_map/ppermute | solution.py:446
  77.2 2.4 %collective-permute-start.9 = (bf16[64,8,256]{2,1,0:T(8,128)(2,1)S(1)}, bf16[64,8,256]{2,1,0:T(8,128)(2,1)S(1)}, u32[]{:S(2)}, u32[]{:S(2)}) collective-permute-start(bf16[64,8,256]{2,1,0:T(8,128)(2,1)S(1)} %all_to_all.10.a0), channel_id=1, source_target_pairs={{2,0},{3,1},{0,2},{1,3},{6,4},{7,5},{4,6},{5,7},{10,8},{11,9},{8,1... | collective-permute-start | bytes 786440 | tf_op jit(solution)/shard_map/ppermute | solution.py:446
  79.6 1.2 collective-permute-start.8
  80.9 4.3 %collective-permute-done.10.a3 = bf16[64,8,256]{2,1,0:T(8,128)(2,1)S(1)} collective-permute-done((bf16[64,8,256]{2,1,0:T(8,128)(2,1)S(1)}, bf16[64,8,256]{2,1,0:T(8,128)(2,1)S(1)}, u32[]{:S(2)}, u32[]{:S(2)}) %collective-permute-start.10) | collective-permute-done | bytes 262176 | tf_op jit(solution)/shard_map/ppermute | solution.py:446
  85.2 6.4 %collective-permute-done.9.a2 = bf16[64,8,256]{2,1,0:T(8,128)(2,1)S(1)} collective-permute-done((bf16[64,8,256]{2,1,0:T(8,128)(2,1)S(1)}, bf16[64,8,256]{2,1,0:T(8,128)(2,1)S(1)}, u32[]{:S(2)}, u32[]{:S(2)}) %collective-permute-start.9) | collective-permute-done | bytes 262176 | tf_op jit(solution)/shard_map/ppermute | solution.py:446
  91.6 0.0 collective-permute-done.8.a1
  91.6 0.0 copy-done.2
  91.6 19.8 %second.1 = bf16[64,16,128]{2,1,0:T(8,128)(2,1)S(1)} custom-call(s32[2]{0:T(128)S(1)} %pad_add_fusion.ids, s32[64,64]{1,0:T(8,128)S(1)} %copy-done, bf16[64,8,256]{2,1,0:T(8,128)(2,1)S(1)} %all_to_all.10.a0, bf16[64,8,256]{2,1,0:T(8,128)(2,1)S(1)} %collective-permute-done.8.a1, bf16[64,8,256]{2,1,0:T(8,128)(2,1)S(1)} %collective-permute-done.9.a2, ...), custom_call_target="tpu_custom_call" | custom-call | tf_op jit(solution)/shard_map/second/pallas_call | solution.py:381
  111.4 17.6 %all_to_all.11.back_ref = bf16[64,16,128]{2,1,0:T(8,128)(2,1)S(1)} all-to-all(bf16[64,16,128]{2,1,0:T(8,128)(2,1)S(1)} %second.1), channel_id=1, replica_groups=mesh['seg'=64,'ch'=4] {'seg'}, dimensions={0} | all-to-all | bytes 524288 | tf_op jit(solution)/shard_map/all_to_all | solution.py:471
  129.0 2.5 %home.1.h0 = bf16[64,1024]{1,0:T(8,128)(2,1)S(1)} custom-call(s32[2]{0:T(128)S(1)} %pad_add_fusion.ids, s32[64,64]{1,0:T(8,128)S(1)} %copy-done, bf16[64,16,128]{2,1,0:T(8,128)(2,1)S(1)} %all_to_all.11.back_ref, bf16[1024,1024]{1,0:T(8,128)(2,1)S(1)} %get-tuple-element.13.chosen_ref), custom_call_target="tpu_custom_call" | custom-call | tf_op jit(solution)/shard_map/home/pallas_call | solution.py:415
  131.5 1.6 %collective-permute-start.13 = (bf16[64,1024]{1,0:T(8,128)(2,1)S(1)}, bf16[64,1024]{1,0:T(8,128)(2,1)S(1)}, u32[]{:S(2)}, u32[]{:S(2)}) collective-permute-start(bf16[64,1024]{1,0:T(8,128)(2,1)S(1)} %home.1.h0), channel_id=1, source_target_pairs={{3,0},{0,1},{1,2},{2,3},{7,4},{4,5},{5,6},{6,7},{11,8},{8,9},{9,10... | collective-permute-start | bytes 393224 | tf_op jit(solution)/shard_map/ppermute | solution.py:446
  133.1 2.4 %collective-permute-start.12 = (bf16[64,1024]{1,0:T(8,128)(2,1)S(1)}, bf16[64,1024]{1,0:T(8,128)(2,1)S(1)}, u32[]{:S(2)}, u32[]{:S(2)}) collective-permute-start(bf16[64,1024]{1,0:T(8,128)(2,1)S(1)} %home.1.h0), channel_id=1, source_target_pairs={{2,0},{3,1},{0,2},{1,3},{6,4},{7,5},{4,6},{5,7},{10,8},{11,9},{8,1... | collective-permute-start | bytes 393224 | tf_op jit(solution)/shard_map/ppermute | solution.py:446
  135.5 1.2 collective-permute-start.11
  136.7 1.8 %collective-permute-done.13.h3 = bf16[64,1024]{1,0:T(8,128)(2,1)S(1)} collective-permute-done((bf16[64,1024]{1,0:T(8,128)(2,1)S(1)}, bf16[64,1024]{1,0:T(8,128)(2,1)S(1)}, u32[]{:S(2)}, u32[]{:S(2)}) %collective-permute-start.13) | collective-permute-done | bytes 131104 | tf_op jit(solution)/shard_map/ppermute | solution.py:446
  138.5 3.3 %collective-permute-done.12.h2 = bf16[64,1024]{1,0:T(8,128)(2,1)S(1)} collective-permute-done((bf16[64,1024]{1,0:T(8,128)(2,1)S(1)}, bf16[64,1024]{1,0:T(8,128)(2,1)S(1)}, u32[]{:S(2)}, u32[]{:S(2)}) %collective-permute-start.12) | collective-permute-done | bytes 131104 | tf_op jit(solution)/shard_map/ppermute | solution.py:446
  141.8 0.0 collective-permute-done.11.h1
  141.8 1.5 %last.1 = bf16[64,1024]{1,0:T(8,128)(2,1)} custom-call(s32[2]{0:T(128)S(1)} %pad_add_fusion.ids, bf16[64,1024]{1,0:T(8,128)(2,1)S(1)} %get-tuple-element.11.mine_ref, bf16[64,1024]{1,0:T(8,128)(2,1)S(1)} %home.1.h0, bf16[64,1024]{1,0:T(8,128)(2,1)S(1)} %collective-permute-done.11.h1, bf16[64,1024]{1,0:T(8,128)(2,1)S(1)} %collective-permute-done.12.h2, ...), custom_call_target="tpu_custom_call" | custom-call | tf_op jit(solution)/shard_map/last/pallas_call | solution.py:433
Async XLA Ops:
  0.9 20.6 %collective-permute-start.1 = (bf16[128,256]{1,0:T(8,128)(2,1)S(1)}, bf16[128,256]{1,0:T(8,128)(2,1)S(1)}, u32[]{:S(2)}, u32[]{:S(2)}) collective-permute-start(bf16[128,256]{1,0:T(8,128)(2,1)S(1)} %get-tuple-element.15), channel_id=1, source_target_pairs={{4,0},{8,4},{12,8},{16,12},{20,16},{24,20},{28,24},{32,28},{36,32}... | collective-permute-start | bytes 196616 | tf_op jit(solution)/shard_map/ppermute | solution.py:459
  8.0 13.5 %collective-permute-start = (bf16[128,256]{1,0:T(8,128)(2,1)S(1)}, bf16[128,256]{1,0:T(8,128)(2,1)S(1)}, u32[]{:S(2)}, u32[]{:S(2)}) collective-permute-start(bf16[128,256]{1,0:T(8,128)(2,1)S(1)} %get-tuple-element.16), channel_id=1, source_target_pairs={{0,4},{4,8},{8,12},{12,16},{16,20},{20,24},{24,28},{28,32},{32,36}... | collective-permute-start | bytes 196616 | tf_op jit(solution)/shard_map/ppermute | solution.py:458
  10.0 1.0 copy-start.3
  11.0 1.2 copy-start.4
  12.2 0.9 copy-start.6
  13.1 8.4 %copy-start.5 = (bf16[27,256,64]{1,2,0:T(8,128)(2,1)S(1)}, bf16[27,256,64]{1,2,0:T(8,128)(2,1)}, u32[]{:S(2)}) copy-start(bf16[27,256,64]{1,2,0:T(8,128)(2,1)} %param.13) | copy-start | bytes 2654212
  21.5 11.6 %copy-start.1 = (bf16[256,3,64]{0,2,1:T(8,128)(2,1)S(1)}, bf16[256,3,64]{0,2,1:T(8,128)(2,1)}, u32[]{:S(2)}) copy-start(bf16[256,3,64]{0,2,1:T(8,128)(2,1)} %param.14) | copy-start | bytes 294916
  21.5 26.4 %copy-start = (s32[64,64]{1,0:T(8,128)S(1)}, s32[64,64]{1,0:T(8,128)}, u32[]{:S(2)}) copy-start(s32[64,64]{1,0:T(8,128)} %counts_sm.3) | copy-start | bytes 49156
  21.5 26.4 %copy-start.7 = (bf16[256,256]{1,0:T(8,128)(2,1)S(1)}, bf16[256,256]{1,0:T(8,128)(2,1)}, u32[]{:S(2)}) copy-start(bf16[256,256]{1,0:T(8,128)(2,1)} %wo_ref.2) | copy-start | bytes 393220
  21.5 26.4 %copy-start.9 = (s32[1,1024]{1,0:T(1,128)S(1)}, s32[1,1024]{1,0:T(1,128)}, u32[]{:S(2)}) copy-start(s32[1,1024]{1,0:T(1,128)} %perm_ref.1) | copy-start | bytes 12292
  23.8 6.3 %collective-permute-start.4 = (bf16[64,1024]{1,0:T(8,128)(2,1)S(1)}, bf16[64,1024]{1,0:T(8,128)(2,1)S(1)}, u32[]{:S(2)}, u32[]{:S(2)}) collective-permute-start(bf16[64,1024]{1,0:T(8,128)(2,1)S(1)} %edge.1.x0.after_ref), channel_id=1, source_target_pairs={{3,0},{0,1},{1,2},{2,3},{7,4},{4,5},{5,6},{6,7},{11,8},{8,9},{9,10... | collective-permute-start | bytes 393224 | tf_op jit(solution)/shard_map/ppermute | solution.py:446
  25.4 7.1 %collective-permute-start.3 = (bf16[64,1024]{1,0:T(8,128)(2,1)S(1)}, bf16[64,1024]{1,0:T(8,128)(2,1)S(1)}, u32[]{:S(2)}, u32[]{:S(2)}) collective-permute-start(bf16[64,1024]{1,0:T(8,128)(2,1)S(1)} %edge.1.x0.after_ref), channel_id=1, source_target_pairs={{2,0},{3,1},{0,2},{1,3},{6,4},{7,5},{4,6},{5,7},{10,8},{11,9},{8,1... | collective-permute-start | bytes 393224 | tf_op jit(solution)/shard_map/ppermute | solution.py:446
  28.1 5.0 %collective-permute-start.2 = (bf16[64,1024]{1,0:T(8,128)(2,1)S(1)}, bf16[64,1024]{1,0:T(8,128)(2,1)S(1)}, u32[]{:S(2)}, u32[]{:S(2)}) collective-permute-start(bf16[64,1024]{1,0:T(8,128)(2,1)S(1)} %edge.1.x0.after_ref), channel_id=1, source_target_pairs={{1,0},{2,1},{3,2},{0,3},{5,4},{6,5},{7,6},{4,7},{9,8},{10,9},{11,1... | collective-permute-start | bytes 393224 | tf_op jit(solution)/shard_map/ppermute | solution.py:446
  42.8 9.1 %copy-start.8 = (bf16[256,256]{1,0:T(8,128)(2,1)S(1)}, bf16[256,256]{1,0:T(8,128)(2,1)}, u32[]{:S(2)}) copy-start(bf16[256,256]{1,0:T(8,128)(2,1)} %wo_ref.3) | copy-start | bytes 393220
  42.8 6.7 %collective-permute-start.7 = (bf16[64,1024]{1,0:T(8,128)(2,1)S(1)}, bf16[64,1024]{1,0:T(8,128)(2,1)S(1)}, u32[]{:S(2)}, u32[]{:S(2)}) collective-permute-start(bf16[64,1024]{1,0:T(8,128)(2,1)S(1)} %first.1.h0), channel_id=1, source_target_pairs={{3,0},{0,1},{1,2},{2,3},{7,4},{4,5},{5,6},{6,7},{11,8},{8,9},{9,10... | collective-permute-start | bytes 393224 | tf_op jit(solution)/shard_map/ppermute | solution.py:446
  44.2 7.1 %collective-permute-start.6 = (bf16[64,1024]{1,0:T(8,128)(2,1)S(1)}, bf16[64,1024]{1,0:T(8,128)(2,1)S(1)}, u32[]{:S(2)}, u32[]{:S(2)}) collective-permute-start(bf16[64,1024]{1,0:T(8,128)(2,1)S(1)} %first.1.h0), channel_id=1, source_target_pairs={{2,0},{3,1},{0,2},{1,3},{6,4},{7,5},{4,6},{5,7},{10,8},{11,9},{8,1... | collective-permute-start | bytes 393224 | tf_op jit(solution)/shard_map/ppermute | solution.py:446
  46.9 5.0 %collective-permute-start.5 = (bf16[64,1024]{1,0:T(8,128)(2,1)S(1)}, bf16[64,1024]{1,0:T(8,128)(2,1)S(1)}, u32[]{:S(2)}, u32[]{:S(2)}) collective-permute-start(bf16[64,1024]{1,0:T(8,128)(2,1)S(1)} %first.1.h0), channel_id=1, source_target_pairs={{1,0},{2,1},{3,2},{0,3},{5,4},{6,5},{7,6},{4,7},{9,8},{10,9},{11,1... | collective-permute-start | bytes 393224 | tf_op jit(solution)/shard_map/ppermute | solution.py:446
  51.9 39.7 %copy-start.2 = (bf16[256,3,64]{0,2,1:T(8,128)(2,1)S(1)}, bf16[256,3,64]{0,2,1:T(8,128)(2,1)}, u32[]{:S(2)}) copy-start(bf16[256,3,64]{0,2,1:T(8,128)(2,1)} %param.16) | copy-start | bytes 294916
  75.6 9.6 %collective-permute-start.10 = (bf16[64,8,256]{2,1,0:T(8,128)(2,1)S(1)}, bf16[64,8,256]{2,1,0:T(8,128)(2,1)S(1)}, u32[]{:S(2)}, u32[]{:S(2)}) collective-permute-start(bf16[64,8,256]{2,1,0:T(8,128)(2,1)S(1)} %all_to_all.10.a0), channel_id=1, source_target_pairs={{3,0},{0,1},{1,2},{2,3},{7,4},{4,5},{5,6},{6,7},{11,8},{8,9},{9,10... | collective-permute-start | bytes 786440 | tf_op jit(solution)/shard_map/ppermute | solution.py:446
  77.2 14.3 %collective-permute-start.9 = (bf16[64,8,256]{2,1,0:T(8,128)(2,1)S(1)}, bf16[64,8,256]{2,1,0:T(8,128)(2,1)S(1)}, u32[]{:S(2)}, u32[]{:S(2)}) collective-permute-start(bf16[64,8,256]{2,1,0:T(8,128)(2,1)S(1)} %all_to_all.10.a0), channel_id=1, source_target_pairs={{2,0},{3,1},{0,2},{1,3},{6,4},{7,5},{4,6},{5,7},{10,8},{11,9},{8,1... | collective-permute-start | bytes 786440 | tf_op jit(solution)/shard_map/ppermute | solution.py:446
  79.6 11.9 %collective-permute-start.8 = (bf16[64,8,256]{2,1,0:T(8,128)(2,1)S(1)}, bf16[64,8,256]{2,1,0:T(8,128)(2,1)S(1)}, u32[]{:S(2)}, u32[]{:S(2)}) collective-permute-start(bf16[64,8,256]{2,1,0:T(8,128)(2,1)S(1)} %all_to_all.10.a0), channel_id=1, source_target_pairs={{1,0},{2,1},{3,2},{0,3},{5,4},{6,5},{7,6},{4,7},{9,8},{10,9},{11,1... | collective-permute-start | bytes 786440 | tf_op jit(solution)/shard_map/ppermute | solution.py:446
  131.5 7.0 %collective-permute-start.13 = (bf16[64,1024]{1,0:T(8,128)(2,1)S(1)}, bf16[64,1024]{1,0:T(8,128)(2,1)S(1)}, u32[]{:S(2)}, u32[]{:S(2)}) collective-permute-start(bf16[64,1024]{1,0:T(8,128)(2,1)S(1)} %home.1.h0), channel_id=1, source_target_pairs={{3,0},{0,1},{1,2},{2,3},{7,4},{4,5},{5,6},{6,7},{11,8},{8,9},{9,10... | collective-permute-start | bytes 393224 | tf_op jit(solution)/shard_map/ppermute | solution.py:446
  133.1 8.7 %collective-permute-start.12 = (bf16[64,1024]{1,0:T(8,128)(2,1)S(1)}, bf16[64,1024]{1,0:T(8,128)(2,1)S(1)}, u32[]{:S(2)}, u32[]{:S(2)}) collective-permute-start(bf16[64,1024]{1,0:T(8,128)(2,1)S(1)} %home.1.h0), channel_id=1, source_target_pairs={{2,0},{3,1},{0,2},{1,3},{6,4},{7,5},{4,6},{5,7},{10,8},{11,9},{8,1... | collective-permute-start | bytes 393224 | tf_op jit(solution)/shard_map/ppermute | solution.py:446
  135.5 6.3 %collective-permute-start.11 = (bf16[64,1024]{1,0:T(8,128)(2,1)S(1)}, bf16[64,1024]{1,0:T(8,128)(2,1)S(1)}, u32[]{:S(2)}, u32[]{:S(2)}) collective-permute-start(bf16[64,1024]{1,0:T(8,128)(2,1)S(1)} %home.1.h0), channel_id=1, source_target_pairs={{1,0},{2,1},{3,2},{0,3},{5,4},{6,5},{7,6},{4,7},{9,8},{10,9},{11,1... | collective-permute-start | bytes 393224 | tf_op jit(solution)/shard_map/ppermute | solution.py:446

commit v4 on v3

--- a/solution.py
+++ b/solution.py
@@ -57,13 +57,22 @@
         full_ref[pl.ds(pl.multiple_of(owner * size, size), size), :] = piece[...]
 
 
-def conv_kernel(ids, own_ref, nb_ref, w_ref, out_ref, y_ref, nbs_ref):
+def conv_kernel(
+    ids, own_hbm, nb_hbm, w_hbm, out_ref, own_ref, nb_ref, w_ref, y_ref, nbs_ref, sems
+):
     base = ids[0] * 1024 - HALO
     ch = ids[1]
+    pairs = ((nb_hbm, nb_ref), (own_hbm, own_ref), (w_hbm, w_ref))
+    copies = [pltpu.make_async_copy(a, b, sems.at[i]) for i, (a, b) in enumerate(pairs)]
+    for copy in copies:
+        copy.start()
+    copies[0].wait()
     for b in range(8):
         nbs_ref[b * 32 : b * 32 + KOFF, :] = nb_ref[:, b * 128 : (b + 1) * 128]
     chosen = one_where(iota((64, 256), 1) == iota((64, 256), 0) + ch * 64).astype(BF)
+    copies[1].wait()
     out_ref[...] = lax.dot_general(chosen, own_ref[...], NT, preferred_element_type=F32)
+    copies[2].wait()
 
     def transform(k, slot):
         w = w_ref[k]
@@ -117,16 +126,24 @@
 
 
 def conv(ids, own, nb, w):
+    stay = [pltpu.with_memory_space_constraint(x, pltpu.HBM) for x in (own, nb, w)]
     return pl.pallas_call(
         conv_kernel,
         name="conv",
         out_shape=jax.ShapeDtypeStruct((64, 1024), F32),
-        in_specs=[SM] + [VM] * 3,
+        in_specs=[SM] + [pl.BlockSpec(memory_space=pltpu.HBM)] * 3,
         out_specs=VM,
-        scratch_shapes=[pltpu.VMEM((2, 64, 1024), F32), pltpu.VMEM((264, 128), I32)],
+        scratch_shapes=[
+            pltpu.VMEM((1024, 256), BF),
+            pltpu.VMEM((KOFF, 1024), I32),
+            pltpu.VMEM((KOFF, 64, 256), BF),
+            pltpu.VMEM((2, 64, 1024), F32),
+            pltpu.VMEM((264, 128), I32),
+            pltpu.SemaphoreType.DMA((3,)),
+        ],
         compiler_params=PARAMS,
         cost_estimate=cost(8),
-    )(ids, own, nb, w)
+    )(ids, *stay)
 
 
 def edge_kernel(ids, prev_ref, next_ref, nb_ref, w_ref, sum_ref, out_ref, y_ref, acc_ref, nbs_ref):

time: 144 us -> 142 us (0.986)
  local copies, waits for them, and re-layouts: 4.03 us -> 0.92 us
    unnamed x20 -> x16, local copies, waits for them, and re-layouts: 3.15 us -> 0.04 us
  transfers between devices with their start and end apart: 14 -> 14, of which waited for: 9 -> 9; matrix products, arithmetic and copies ran while one was open for 0% -> 0% of each run, Pallas kernels for 7% -> 8%
where the time goes in v4:
time: 142 us; the launch traced here: 141 us
  Pallas kernels  48.5 us (34%)
  blocking collectives  39.6 us (28%)
  starting transfers between devices  30.3 us (21%)
  waiting for transfers between devices  21.8 us (15%)
    all_to_all x1, blocking collectives, local(): lax.all_to_all(outgoing, 'seg', split_axis=0, concat_axis=0, tiled=True)  22 us
    ppermute x12, waiting for transfers between devices, moved(): return lax.ppermute(piece, 'ch', [((i + step) % 4, i) for i in range(4)])  21.8 us
    ppermute x12, starting transfers between devices, moved(): return lax.ppermute(piece, 'ch', [((i + step) % 4, i) for i in range(4)])  21.3 us
    pallas_call x1, Pallas kernels, second(): pl.pallas_call(second_kernel, name='second', out_shape=jax.ShapeDtypeStru...  19.8 us
    all_to_all x1, blocking collectives, local(): back = lax.all_to_all(going, 'seg', split_axis=0, concat_axis=0, tiled=True)  17.6 us
    pallas_call x1, Pallas kernels, first(): pl.pallas_call(first_kernel, name='first', out_shape=jax.ShapeDtypeStruct...  9.67 us
    pallas_call x1, Pallas kernels, conv(): pl.pallas_call(conv_kernel, name='conv', out_shape=jax.ShapeDtypeStruct((...  9.56 us
    ppermute x1, starting transfers between devices, local(): nxt = lax.ppermute(voxels[:HALO], 'seg', down)  7.09 us
  transfers between devices with their start and end apart: 14, of which 9 were waited for; matrix products, arithmetic and copies ran while one was open for 0% of the time, Pallas kernels for 8%

profile of v4, /device:TPU:8, one launch (start us, length us, event | category | flops | bytes accessed | tf_op | source)
XLA Modules:
  0.0 141.3 jit_solution(17007957986051103449)
XLA Ops:
  0.0 0.9 fusion
  0.9 7.1 %collective-permute-start.1 = (bf16[128,256]{1,0:T(8,128)(2,1)S(1)}, bf16[128,256]{1,0:T(8,128)(2,1)S(1)}, u32[]{:S(2)}, u32[]{:S(2)}) collective-permute-start(bf16[128,256]{1,0:T(8,128)(2,1)S(1)} %get-tuple-element.15), channel_id=1, source_target_pairs={{4,0},{8,4},{12,8},{16,12},{20,16},{24,20},{28,24},{32,28},{36,32}... | collective-permute-start | bytes 196616 | tf_op jit(solution)/shard_map/ppermute | solution.py:476
  8.0 1.9 %collective-permute-start = (bf16[128,256]{1,0:T(8,128)(2,1)S(1)}, bf16[128,256]{1,0:T(8,128)(2,1)S(1)}, u32[]{:S(2)}, u32[]{:S(2)}) collective-permute-start(bf16[128,256]{1,0:T(8,128)(2,1)S(1)} %get-tuple-element.16), channel_id=1, source_target_pairs={{0,4},{4,8},{8,12},{12,16},{16,20},{20,24},{24,28},{28,32},{32,36}... | collective-permute-start | bytes 196616 | tf_op jit(solution)/shard_map/ppermute | solution.py:475
  9.9 0.1 pad_add_fusion.ids
  10.0 0.0 copy-start.3
  10.0 0.0 copy-start.4
  10.0 9.6 %conv.1.sum_ref = f32[64,1024]{1,0:T(8,128)S(1)} custom-call(s32[2]{0:T(128)S(1)} %pad_add_fusion.ids, bf16[1024,256]{1,0:T(8,128)(2,1)} %own_hbm.1, s32[27,1024]{1,0:T(8,128)} %nb_ref.1, bf16[27,64,256]{2,1,0:T(8,128)(2,1)} %bitcast.12), custom_call_target="tpu_custom_call" | custom-call | flops 4000000000 | bytes 1048576 | tf_op jit(solution)/shard_map/conv/pallas_call | solution.py:130
  19.6 0.0 copy-start.1
  19.6 0.0 copy-start
  19.6 0.0 copy-start.5
  19.6 0.0 copy-start.7
  19.6 0.0 collective-permute-done.1.next_ref
  19.6 0.0 collective-permute-done.prev_ref
  19.6 0.0 copy-done.3
  19.6 0.0 copy-done.4
  19.7 2.2 %edge.1.x0.after_ref = bf16[64,1024]{1,0:T(8,128)(2,1)S(1)} custom-call(s32[2]{0:T(128)S(1)} %pad_add_fusion.ids, bf16[128,256]{1,0:T(8,128)(2,1)S(1)} %collective-permute-done.prev_ref, bf16[128,256]{1,0:T(8,128)(2,1)S(1)} %collective-permute-done.1.next_ref, s32[27,1024]{1,0:T(8,128)S(1)} %copy-done.4, bf16[27,64,256]{2,1,0:T(8,128)(2,1)S(1)} %bitcast.13, ...), custom_call_target="tpu_custom_call" | custom-call | flops 1000000000 | bytes 1048576 | tf_op jit(solution)/shard_map/edge/pallas_call | solution.py:185
  21.9 1.6 %collective-permute-start.4 = (bf16[64,1024]{1,0:T(8,128)(2,1)S(1)}, bf16[64,1024]{1,0:T(8,128)(2,1)S(1)}, u32[]{:S(2)}, u32[]{:S(2)}) collective-permute-start(bf16[64,1024]{1,0:T(8,128)(2,1)S(1)} %edge.1.x0.after_ref), channel_id=1, source_target_pairs={{3,0},{0,1},{1,2},{2,3},{7,4},{4,5},{5,6},{6,7},{11,8},{8,9},{9,10... | collective-permute-start | bytes 393224 | tf_op jit(solution)/shard_map/ppermute | solution.py:463
  23.5 2.7 %collective-permute-start.3 = (bf16[64,1024]{1,0:T(8,128)(2,1)S(1)}, bf16[64,1024]{1,0:T(8,128)(2,1)S(1)}, u32[]{:S(2)}, u32[]{:S(2)}) collective-permute-start(bf16[64,1024]{1,0:T(8,128)(2,1)S(1)} %edge.1.x0.after_ref), channel_id=1, source_target_pairs={{2,0},{3,1},{0,2},{1,3},{6,4},{7,5},{4,6},{5,7},{10,8},{11,9},{8,1... | collective-permute-start | bytes 393224 | tf_op jit(solution)/shard_map/ppermute | solution.py:463
  26.2 1.4 %collective-permute-start.2 = (bf16[64,1024]{1,0:T(8,128)(2,1)S(1)}, bf16[64,1024]{1,0:T(8,128)(2,1)S(1)}, u32[]{:S(2)}, u32[]{:S(2)}) collective-permute-start(bf16[64,1024]{1,0:T(8,128)(2,1)S(1)} %edge.1.x0.after_ref), channel_id=1, source_target_pairs={{1,0},{2,1},{3,2},{0,3},{5,4},{6,5},{7,6},{4,7},{9,8},{10,9},{11,1... | collective-permute-start | bytes 393224 | tf_op jit(solution)/shard_map/ppermute | solution.py:463
  27.6 0.5 collective-permute-done.4.x3
  28.2 2.4 %collective-permute-done.3.x2 = bf16[64,1024]{1,0:T(8,128)(2,1)S(1)} collective-permute-done((bf16[64,1024]{1,0:T(8,128)(2,1)S(1)}, bf16[64,1024]{1,0:T(8,128)(2,1)S(1)}, u32[]{:S(2)}, u32[]{:S(2)}) %collective-permute-start.3) | collective-permute-done | bytes 131104 | tf_op jit(solution)/shard_map/ppermute | solution.py:463
  30.5 0.6 collective-permute-done.2.x1
  31.2 0.0 copy-done.1
  31.2 9.7 %first.1.h0 = bf16[64,1024]{1,0:T(8,128)(2,1)S(1)} custom-call(s32[2]{0:T(128)S(1)} %pad_add_fusion.ids, bf16[64,1024]{1,0:T(8,128)(2,1)S(1)} %edge.1.x0.after_ref, bf16[64,1024]{1,0:T(8,128)(2,1)S(1)} %collective-permute-done.2.x1, bf16[64,1024]{1,0:T(8,128)(2,1)S(1)} %collective-permute-done.3.x2, bf16[64,1024]{1,0:T(8,128)(2,1)S(1)} %collective-permute-done.4.x3, ...), custom_call_target="tpu_custom_call" | custom-call | tf_op jit(solution)/shard_map/first/pallas_call | solution.py:310
  40.8 0.0 copy-start.6
  40.9 1.4 collective-permute-start.7
  42.2 2.8 %collective-permute-start.6 = (bf16[64,1024]{1,0:T(8,128)(2,1)S(1)}, bf16[64,1024]{1,0:T(8,128)(2,1)S(1)}, u32[]{:S(2)}, u32[]{:S(2)}) collective-permute-start(bf16[64,1024]{1,0:T(8,128)(2,1)S(1)} %first.1.h0), channel_id=1, source_target_pairs={{2,0},{3,1},{0,2},{1,3},{6,4},{7,5},{4,6},{5,7},{10,8},{11,9},{8,1... | collective-permute-start | bytes 393224 | tf_op jit(solution)/shard_map/ppermute | solution.py:463
  45.0 0.9 collective-permute-start.5
  46.0 0.0 copy-done
  46.0 0.0 copy-done.5
  46.0 0.0 copy-done.7
  46.0 1.7 %prep.1 = (bf16[512,1024]{1,0:T(8,128)(2,1)S(1)}, bf16[1024,1024]{1,0:T(8,128)(2,1)S(1)}, bf16[64,256]{1,0:T(8,128)(2,1)S(1)}) custom-call(s32[2]{0:T(128)S(1)} %pad_add_fusion.ids, bf16[64,1024]{1,0:T(8,128)(2,1)S(1)} %edge.1.x0.after_ref, bf16[256,256]{1,0:T(8,128)(2,1)S(1)} %copy-done.5, s32[1,1024]{1,0:T(1,128)S(1)} %copy-done.7, s32[64,64]{1,0:T(8,128)S(1)} %copy-done), custom_call_target="tpu_custom_call" | custom-call | flops 1500000000 | bytes 1048576 | tf_op jit(solution)/shard_map/prep/pallas_call | solution.py:221
  47.6 0.0 collective-permute-done.7.h3
  47.7 1.7 %collective-permute-done.6.h2 = bf16[64,1024]{1,0:T(8,128)(2,1)S(1)} collective-permute-done((bf16[64,1024]{1,0:T(8,128)(2,1)S(1)}, bf16[64,1024]{1,0:T(8,128)(2,1)S(1)}, u32[]{:S(2)}, u32[]{:S(2)}) %collective-permute-start.6) | collective-permute-done | bytes 131104 | tf_op jit(solution)/shard_map/ppermute | solution.py:463
  49.4 0.6 collective-permute-done.5.h1
  50.0 0.0 copy-done.6
  50.0 0.0 copy-start.2
  50.0 1.6 %pick.1 = (bf16[64,8,256]{2,1,0:T(8,128)(2,1)S(1)}, bf16[64,1024]{1,0:T(8,128)(2,1)S(1)}) custom-call(s32[2]{0:T(128)S(1)} %pad_add_fusion.ids, bf16[64,1024]{1,0:T(8,128)(2,1)S(1)} %edge.1.x0.after_ref, bf16[64,1024]{1,0:T(8,128)(2,1)S(1)} %collective-permute-done.2.x1, bf16[64,1024]{1,0:T(8,128)(2,1)S(1)} %collective-permute-done.3.x2, ...), custom_call_target="tpu_custom_call" | custom-call | flops 1000000000 | bytes 1048576 | tf_op jit(solution)/shard_map/pick/pallas_call | solution.py:342
  51.7 22.0 %all_to_all.10.a0 = bf16[64,8,256]{2,1,0:T(8,128)(2,1)S(1)} all-to-all(bf16[64,8,256]{2,1,0:T(8,128)(2,1)S(1)} %get-tuple-element.12), channel_id=1, replica_groups=mesh['seg'=64,'ch'=4] {'seg'}, dimensions={0} | all-to-all | bytes 524288 | tf_op jit(solution)/shard_map/all_to_all | solution.py:486
  73.6 1.7 %collective-permute-start.10 = (bf16[64,8,256]{2,1,0:T(8,128)(2,1)S(1)}, bf16[64,8,256]{2,1,0:T(8,128)(2,1)S(1)}, u32[]{:S(2)}, u32[]{:S(2)}) collective-permute-start(bf16[64,8,256]{2,1,0:T(8,128)(2,1)S(1)} %all_to_all.10.a0), channel_id=1, source_target_pairs={{3,0},{0,1},{1,2},{2,3},{7,4},{4,5},{5,6},{6,7},{11,8},{8,9},{9,10... | collective-permute-start | bytes 786440 | tf_op jit(solution)/shard_map/ppermute | solution.py:463
  75.3 2.4 %collective-permute-start.9 = (bf16[64,8,256]{2,1,0:T(8,128)(2,1)S(1)}, bf16[64,8,256]{2,1,0:T(8,128)(2,1)S(1)}, u32[]{:S(2)}, u32[]{:S(2)}) collective-permute-start(bf16[64,8,256]{2,1,0:T(8,128)(2,1)S(1)} %all_to_all.10.a0), channel_id=1, source_target_pairs={{2,0},{3,1},{0,2},{1,3},{6,4},{7,5},{4,6},{5,7},{10,8},{11,9},{8,1... | collective-permute-start | bytes 786440 | tf_op jit(solution)/shard_map/ppermute | solution.py:463
  77.7 1.2 collective-permute-start.8
  78.9 4.3 %collective-permute-done.10.a3 = bf16[64,8,256]{2,1,0:T(8,128)(2,1)S(1)} collective-permute-done((bf16[64,8,256]{2,1,0:T(8,128)(2,1)S(1)}, bf16[64,8,256]{2,1,0:T(8,128)(2,1)S(1)}, u32[]{:S(2)}, u32[]{:S(2)}) %collective-permute-start.10) | collective-permute-done | bytes 262176 | tf_op jit(solution)/shard_map/ppermute | solution.py:463
  83.2 6.4 %collective-permute-done.9.a2 = bf16[64,8,256]{2,1,0:T(8,128)(2,1)S(1)} collective-permute-done((bf16[64,8,256]{2,1,0:T(8,128)(2,1)S(1)}, bf16[64,8,256]{2,1,0:T(8,128)(2,1)S(1)}, u32[]{:S(2)}, u32[]{:S(2)}) %collective-permute-start.9) | collective-permute-done | bytes 262176 | tf_op jit(solution)/shard_map/ppermute | solution.py:463
  89.6 0.0 collective-permute-done.8.a1
  89.6 0.0 copy-done.2
  89.6 19.8 %second.1 = bf16[64,16,128]{2,1,0:T(8,128)(2,1)S(1)} custom-call(s32[2]{0:T(128)S(1)} %pad_add_fusion.ids, s32[64,64]{1,0:T(8,128)S(1)} %copy-done, bf16[64,8,256]{2,1,0:T(8,128)(2,1)S(1)} %all_to_all.10.a0, bf16[64,8,256]{2,1,0:T(8,128)(2,1)S(1)} %collective-permute-done.8.a1, bf16[64,8,256]{2,1,0:T(8,128)(2,1)S(1)} %collective-permute-done.9.a2, ...), custom_call_target="tpu_custom_call" | custom-call | tf_op jit(solution)/shard_map/second/pallas_call | solution.py:398
  109.4 17.6 %all_to_all.11.back_ref = bf16[64,16,128]{2,1,0:T(8,128)(2,1)S(1)} all-to-all(bf16[64,16,128]{2,1,0:T(8,128)(2,1)S(1)} %second.1), channel_id=1, replica_groups=mesh['seg'=64,'ch'=4] {'seg'}, dimensions={0} | all-to-all | bytes 524288 | tf_op jit(solution)/shard_map/all_to_all | solution.py:488
  127.1 2.5 %home.1.h0 = bf16[64,1024]{1,0:T(8,128)(2,1)S(1)} custom-call(s32[2]{0:T(128)S(1)} %pad_add_fusion.ids, s32[64,64]{1,0:T(8,128)S(1)} %copy-done, bf16[64,16,128]{2,1,0:T(8,128)(2,1)S(1)} %all_to_all.11.back_ref, bf16[1024,1024]{1,0:T(8,128)(2,1)S(1)} %get-tuple-element.13.chosen_ref), custom_call_target="tpu_custom_call" | custom-call | tf_op jit(solution)/shard_map/home/pallas_call | solution.py:432
  129.5 1.6 %collective-permute-start.13 = (bf16[64,1024]{1,0:T(8,128)(2,1)S(1)}, bf16[64,1024]{1,0:T(8,128)(2,1)S(1)}, u32[]{:S(2)}, u32[]{:S(2)}) collective-permute-start(bf16[64,1024]{1,0:T(8,128)(2,1)S(1)} %home.1.h0), channel_id=1, source_target_pairs={{3,0},{0,1},{1,2},{2,3},{7,4},{4,5},{5,6},{6,7},{11,8},{8,9},{9,10... | collective-permute-start | bytes 393224 | tf_op jit(solution)/shard_map/ppermute | solution.py:463
  131.1 2.4 %collective-permute-start.12 = (bf16[64,1024]{1,0:T(8,128)(2,1)S(1)}, bf16[64,1024]{1,0:T(8,128)(2,1)S(1)}, u32[]{:S(2)}, u32[]{:S(2)}) collective-permute-start(bf16[64,1024]{1,0:T(8,128)(2,1)S(1)} %home.1.h0), channel_id=1, source_target_pairs={{2,0},{3,1},{0,2},{1,3},{6,4},{7,5},{4,6},{5,7},{10,8},{11,9},{8,1... | collective-permute-start | bytes 393224 | tf_op jit(solution)/shard_map/ppermute | solution.py:463
  133.5 1.2 collective-permute-start.11
  134.7 1.8 %collective-permute-done.13.h3 = bf16[64,1024]{1,0:T(8,128)(2,1)S(1)} collective-permute-done((bf16[64,1024]{1,0:T(8,128)(2,1)S(1)}, bf16[64,1024]{1,0:T(8,128)(2,1)S(1)}, u32[]{:S(2)}, u32[]{:S(2)}) %collective-permute-start.13) | collective-permute-done | bytes 131104 | tf_op jit(solution)/shard_map/ppermute | solution.py:463
  136.5 3.3 %collective-permute-done.12.h2 = bf16[64,1024]{1,0:T(8,128)(2,1)S(1)} collective-permute-done((bf16[64,1024]{1,0:T(8,128)(2,1)S(1)}, bf16[64,1024]{1,0:T(8,128)(2,1)S(1)}, u32[]{:S(2)}, u32[]{:S(2)}) %collective-permute-start.12) | collective-permute-done | bytes 131104 | tf_op jit(solution)/shard_map/ppermute | solution.py:463
  139.8 0.0 collective-permute-done.11.h1
  139.8 1.5 %last.1 = bf16[64,1024]{1,0:T(8,128)(2,1)} custom-call(s32[2]{0:T(128)S(1)} %pad_add_fusion.ids, bf16[64,1024]{1,0:T(8,128)(2,1)S(1)} %get-tuple-element.11.mine_ref, bf16[64,1024]{1,0:T(8,128)(2,1)S(1)} %home.1.h0, bf16[64,1024]{1,0:T(8,128)(2,1)S(1)} %collective-permute-done.11.h1, bf16[64,1024]{1,0:T(8,128)(2,1)S(1)} %collective-permute-done.12.h2, ...), custom_call_target="tpu_custom_call" | custom-call | tf_op jit(solution)/shard_map/last/pallas_call | solution.py:450
Async XLA Ops:
  0.9 18.7 %collective-permute-start.1 = (bf16[128,256]{1,0:T(8,128)(2,1)S(1)}, bf16[128,256]{1,0:T(8,128)(2,1)S(1)}, u32[]{:S(2)}, u32[]{:S(2)}) collective-permute-start(bf16[128,256]{1,0:T(8,128)(2,1)S(1)} %get-tuple-element.15), channel_id=1, source_target_pairs={{4,0},{8,4},{12,8},{16,12},{20,16},{24,20},{28,24},{32,28},{36,32}... | collective-permute-start | bytes 196616 | tf_op jit(solution)/shard_map/ppermute | solution.py:476
  8.0 11.6 %collective-permute-start = (bf16[128,256]{1,0:T(8,128)(2,1)S(1)}, bf16[128,256]{1,0:T(8,128)(2,1)S(1)}, u32[]{:S(2)}, u32[]{:S(2)}) collective-permute-start(bf16[128,256]{1,0:T(8,128)(2,1)S(1)} %get-tuple-element.16), channel_id=1, source_target_pairs={{0,4},{4,8},{8,12},{12,16},{16,20},{20,24},{24,28},{28,32},{32,36}... | collective-permute-start | bytes 196616 | tf_op jit(solution)/shard_map/ppermute | solution.py:475
  10.0 9.6 %copy-start.3 = (bf16[27,256,64]{1,2,0:T(8,128)(2,1)S(1)}, bf16[27,256,64]{1,2,0:T(8,128)(2,1)}, u32[]{:S(2)}) copy-start(bf16[27,256,64]{1,2,0:T(8,128)(2,1)} %param.13) | copy-start | bytes 2654212
  10.0 9.7 %copy-start.4 = (s32[27,1024]{1,0:T(8,128)S(1)}, s32[27,1024]{1,0:T(8,128)}, u32[]{:S(2)}) copy-start(s32[27,1024]{1,0:T(8,128)} %nb_ref.1) | copy-start | bytes 331780
  19.6 11.6 %copy-start.1 = (bf16[256,3,64]{0,2,1:T(8,128)(2,1)S(1)}, bf16[256,3,64]{0,2,1:T(8,128)(2,1)}, u32[]{:S(2)}) copy-start(bf16[256,3,64]{0,2,1:T(8,128)(2,1)} %param.14) | copy-start | bytes 294916
  19.6 26.4 %copy-start = (s32[64,64]{1,0:T(8,128)S(1)}, s32[64,64]{1,0:T(8,128)}, u32[]{:S(2)}) copy-start(s32[64,64]{1,0:T(8,128)} %counts_sm.3) | copy-start | bytes 49156
  19.6 26.4 %copy-start.5 = (bf16[256,256]{1,0:T(8,128)(2,1)S(1)}, bf16[256,256]{1,0:T(8,128)(2,1)}, u32[]{:S(2)}) copy-start(bf16[256,256]{1,0:T(8,128)(2,1)} %wo_ref.2) | copy-start | bytes 393220
  19.6 26.4 %copy-start.7 = (s32[1,1024]{1,0:T(1,128)S(1)}, s32[1,1024]{1,0:T(1,128)}, u32[]{:S(2)}) copy-start(s32[1,1024]{1,0:T(1,128)} %perm_ref.1) | copy-start | bytes 12292
  21.9 6.3 %collective-permute-start.4 = (bf16[64,1024]{1,0:T(8,128)(2,1)S(1)}, bf16[64,1024]{1,0:T(8,128)(2,1)S(1)}, u32[]{:S(2)}, u32[]{:S(2)}) collective-permute-start(bf16[64,1024]{1,0:T(8,128)(2,1)S(1)} %edge.1.x0.after_ref), channel_id=1, source_target_pairs={{3,0},{0,1},{1,2},{2,3},{7,4},{4,5},{5,6},{6,7},{11,8},{8,9},{9,10... | collective-permute-start | bytes 393224 | tf_op jit(solution)/shard_map/ppermute | solution.py:463
  23.5 7.1 %collective-permute-start.3 = (bf16[64,1024]{1,0:T(8,128)(2,1)S(1)}, bf16[64,1024]{1,0:T(8,128)(2,1)S(1)}, u32[]{:S(2)}, u32[]{:S(2)}) collective-permute-start(bf16[64,1024]{1,0:T(8,128)(2,1)S(1)} %edge.1.x0.after_ref), channel_id=1, source_target_pairs={{2,0},{3,1},{0,2},{1,3},{6,4},{7,5},{4,6},{5,7},{10,8},{11,9},{8,1... | collective-permute-start | bytes 393224 | tf_op jit(solution)/shard_map/ppermute | solution.py:463
  26.2 5.0 %collective-permute-start.2 = (bf16[64,1024]{1,0:T(8,128)(2,1)S(1)}, bf16[64,1024]{1,0:T(8,128)(2,1)S(1)}, u32[]{:S(2)}, u32[]{:S(2)}) collective-permute-start(bf16[64,1024]{1,0:T(8,128)(2,1)S(1)} %edge.1.x0.after_ref), channel_id=1, source_target_pairs={{1,0},{2,1},{3,2},{0,3},{5,4},{6,5},{7,6},{4,7},{9,8},{10,9},{11,1... | collective-permute-start | bytes 393224 | tf_op jit(solution)/shard_map/ppermute | solution.py:463
  40.8 9.2 %copy-start.6 = (bf16[256,256]{1,0:T(8,128)(2,1)S(1)}, bf16[256,256]{1,0:T(8,128)(2,1)}, u32[]{:S(2)}) copy-start(bf16[256,256]{1,0:T(8,128)(2,1)} %wo_ref.3) | copy-start | bytes 393220
  40.9 6.8 %collective-permute-start.7 = (bf16[64,1024]{1,0:T(8,128)(2,1)S(1)}, bf16[64,1024]{1,0:T(8,128)(2,1)S(1)}, u32[]{:S(2)}, u32[]{:S(2)}) collective-permute-start(bf16[64,1024]{1,0:T(8,128)(2,1)S(1)} %first.1.h0), channel_id=1, source_target_pairs={{3,0},{0,1},{1,2},{2,3},{7,4},{4,5},{5,6},{6,7},{11,8},{8,9},{9,10... | collective-permute-start | bytes 393224 | tf_op jit(solution)/shard_map/ppermute | solution.py:463
  42.2 7.2 %collective-permute-start.6 = (bf16[64,1024]{1,0:T(8,128)(2,1)S(1)}, bf16[64,1024]{1,0:T(8,128)(2,1)S(1)}, u32[]{:S(2)}, u32[]{:S(2)}) collective-permute-start(bf16[64,1024]{1,0:T(8,128)(2,1)S(1)} %first.1.h0), channel_id=1, source_target_pairs={{2,0},{3,1},{0,2},{1,3},{6,4},{7,5},{4,6},{5,7},{10,8},{11,9},{8,1... | collective-permute-start | bytes 393224 | tf_op jit(solution)/shard_map/ppermute | solution.py:463
  45.0 5.0 %collective-permute-start.5 = (bf16[64,1024]{1,0:T(8,128)(2,1)S(1)}, bf16[64,1024]{1,0:T(8,128)(2,1)S(1)}, u32[]{:S(2)}, u32[]{:S(2)}) collective-permute-start(bf16[64,1024]{1,0:T(8,128)(2,1)S(1)} %first.1.h0), channel_id=1, source_target_pairs={{1,0},{2,1},{3,2},{0,3},{5,4},{6,5},{7,6},{4,7},{9,8},{10,9},{11,1... | collective-permute-start | bytes 393224 | tf_op jit(solution)/shard_map/ppermute | solution.py:463
  50.0 39.6 %copy-start.2 = (bf16[256,3,64]{0,2,1:T(8,128)(2,1)S(1)}, bf16[256,3,64]{0,2,1:T(8,128)(2,1)}, u32[]{:S(2)}) copy-start(bf16[256,3,64]{0,2,1:T(8,128)(2,1)} %param.16) | copy-start | bytes 294916
  73.6 9.6 %collective-permute-start.10 = (bf16[64,8,256]{2,1,0:T(8,128)(2,1)S(1)}, bf16[64,8,256]{2,1,0:T(8,128)(2,1)S(1)}, u32[]{:S(2)}, u32[]{:S(2)}) collective-permute-start(bf16[64,8,256]{2,1,0:T(8,128)(2,1)S(1)} %all_to_all.10.a0), channel_id=1, source_target_pairs={{3,0},{0,1},{1,2},{2,3},{7,4},{4,5},{5,6},{6,7},{11,8},{8,9},{9,10... | collective-permute-start | bytes 786440 | tf_op jit(solution)/shard_map/ppermute | solution.py:463
  75.3 14.3 %collective-permute-start.9 = (bf16[64,8,256]{2,1,0:T(8,128)(2,1)S(1)}, bf16[64,8,256]{2,1,0:T(8,128)(2,1)S(1)}, u32[]{:S(2)}, u32[]{:S(2)}) collective-permute-start(bf16[64,8,256]{2,1,0:T(8,128)(2,1)S(1)} %all_to_all.10.a0), channel_id=1, source_target_pairs={{2,0},{3,1},{0,2},{1,3},{6,4},{7,5},{4,6},{5,7},{10,8},{11,9},{8,1... | collective-permute-start | bytes 786440 | tf_op jit(solution)/shard_map/ppermute | solution.py:463
  77.7 11.9 %collective-permute-start.8 = (bf16[64,8,256]{2,1,0:T(8,128)(2,1)S(1)}, bf16[64,8,256]{2,1,0:T(8,128)(2,1)S(1)}, u32[]{:S(2)}, u32[]{:S(2)}) collective-permute-start(bf16[64,8,256]{2,1,0:T(8,128)(2,1)S(1)} %all_to_all.10.a0), channel_id=1, source_target_pairs={{1,0},{2,1},{3,2},{0,3},{5,4},{6,5},{7,6},{4,7},{9,8},{10,9},{11,1... | collective-permute-start | bytes 786440 | tf_op jit(solution)/shard_map/ppermute | solution.py:463
  129.5 7.0 %collective-permute-start.13 = (bf16[64,1024]{1,0:T(8,128)(2,1)S(1)}, bf16[64,1024]{1,0:T(8,128)(2,1)S(1)}, u32[]{:S(2)}, u32[]{:S(2)}) collective-permute-start(bf16[64,1024]{1,0:T(8,128)(2,1)S(1)} %home.1.h0), channel_id=1, source_target_pairs={{3,0},{0,1},{1,2},{2,3},{7,4},{4,5},{5,6},{6,7},{11,8},{8,9},{9,10... | collective-permute-start | bytes 393224 | tf_op jit(solution)/shard_map/ppermute | solution.py:463
  131.1 8.7 %collective-permute-start.12 = (bf16[64,1024]{1,0:T(8,128)(2,1)S(1)}, bf16[64,1024]{1,0:T(8,128)(2,1)S(1)}, u32[]{:S(2)}, u32[]{:S(2)}) collective-permute-start(bf16[64,1024]{1,0:T(8,128)(2,1)S(1)} %home.1.h0), channel_id=1, source_target_pairs={{2,0},{3,1},{0,2},{1,3},{6,4},{7,5},{4,6},{5,7},{10,8},{11,9},{8,1... | collective-permute-start | bytes 393224 | tf_op jit(solution)/shard_map/ppermute | solution.py:463
  133.5 6.3 %collective-permute-start.11 = (bf16[64,1024]{1,0:T(8,128)(2,1)S(1)}, bf16[64,1024]{1,0:T(8,128)(2,1)S(1)}, u32[]{:S(2)}, u32[]{:S(2)}) collective-permute-start(bf16[64,1024]{1,0:T(8,128)(2,1)S(1)} %home.1.h0), channel_id=1, source_target_pairs={{1,0},{2,1},{3,2},{0,3},{5,4},{6,5},{7,6},{4,7},{9,8},{10,9},{11,1... | collective-permute-start | bytes 393224 | tf_op jit(solution)/shard_map/ppermute | solution.py:463

commit v5 on v4

--- a/solution.py
+++ b/solution.py
@@ -18,6 +18,7 @@
 TINY = 1e-30
 NT = (((1,), (1,)), ((), ()))
 TN = (((0,), (0,)), ((), ()))
+DN = lax.GatherDimensionNumbers((), (1,), (1,), (0,), (0,))
 VM = pl.BlockSpec(memory_space=pltpu.VMEM)
 SM = pl.BlockSpec(memory_space=pltpu.SMEM)
 PARAMS = pltpu.CompilerParams(vmem_limit_bytes=50 << 20)
@@ -74,43 +75,50 @@
     out_ref[...] = lax.dot_general(chosen, own_ref[...], NT, preferred_element_type=F32)
     copies[2].wait()
 
-    def transform(k, slot):
-        w = w_ref[k]
+    def transform(group, slot):
+        w = w_ref[pl.ds(group * 3, 3)].reshape(192, 256)
         for j in range(4):
             y_ref[slot, :, j * 256 : (j + 1) * 256] = lax.dot_general(
                 w, own_ref[j * 256 : (j + 1) * 256], NT, preferred_element_type=F32
-            )
-
-    def collect(k, slot):
+            ).astype(BF)
+
+    def collect(group, slot):
+        for kk in range(3):
+            collect_one(group * 3 + kk, slot, kk * 64)
+
+    def collect_one(k, slot, top):
         for b in range(8):
-            target = nbs_ref[pl.ds(b * 32 + k, 8, stride=0), :]
+            target = nbs_ref[pl.ds(b * 32 + k, 16, stride=0), :]
             r = target - (base + b * 128)
             there = target >= 0
             if b == 0:
                 there = there & (r >= 128)
             if b == 7:
                 there = there & (r < 256)
-            lane = r & 127
-            first = r < 128
-            second = r < 256
-            for g in range(8):
+            place16 = jnp.where(there, r, 512).astype(jnp.int16)
+            lane16 = place16 & jnp.int16(127)
+            first = place16 < jnp.int16(128)
+            second = place16 < jnp.int16(256)
+            third = place16 < jnp.int16(384)
+            for g in range(4):
                 t = [
-                    jnp.take_along_axis(
-                        y_ref[slot, g * 8 : g * 8 + 8, (b + j - 1) * 128 : (b + j) * 128],
-                        lane,
-                        axis=1,
-                        mode="promise_in_bounds",
+                    lax.gather(
+                        y_ref[slot, top + g * 16 : top + g * 16 + 16, (b + j - 1) * 128 : (b + j) * 128],
+                        lane16[..., None],
+                        DN,
+                        (1, 1),
+                        mode=lax.GatherScatterMode.PROMISE_IN_BOUNDS,
                     )
                     if 0 <= b + j - 1 < 8
                     else None
                     for j in range(3)
                 ]
-                v = t[1] if t[2] is None else t[2]
-                if t[2] is not None:
-                    v = jnp.where(second, t[1], t[2])
+                none = jnp.zeros((16, 128), BF)
+                v = none if t[2] is None else jnp.where(third, t[2], none)
+                v = jnp.where(second, t[1], v)
                 if t[0] is not None:
                     v = jnp.where(first, t[0], v)
-                out_ref[g * 8 : g * 8 + 8, b * 128 : (b + 1) * 128] += jnp.where(there, v, 0.0)
+                out_ref[g * 16 : g * 16 + 16, b * 128 : (b + 1) * 128] += v.astype(F32)
 
     transform(0, 0)
 
@@ -121,8 +129,8 @@
         collect(2 * i + 1, 1)
         return carry
 
-    lax.fori_loop(0, KOFF // 2, body, 0)
-    collect(KOFF - 1, 0)
+    lax.fori_loop(0, 4, body, 0)
+    collect(8, 0)
 
 
 def conv(ids, own, nb, w):
@@ -137,8 +145,8 @@
             pltpu.VMEM((1024, 256), BF),
             pltpu.VMEM((KOFF, 1024), I32),
             pltpu.VMEM((KOFF, 64, 256), BF),
-            pltpu.VMEM((2, 64, 1024), F32),
-            pltpu.VMEM((264, 128), I32),
+            pltpu.VMEM((2, 192, 1024), BF),
+            pltpu.VMEM((272, 128), I32),
             pltpu.SemaphoreType.DMA((3,)),
         ],
         compiler_params=PARAMS,

time: 142 us -> 139 us (0.979)
  Pallas kernels: 48.5 us -> 45.2 us
    pallas_call x1, Pallas kernels: 9.56 us -> 6.21 us  [conv(): pl.pallas_call(conv_kernel, name='conv', out_shape=jax.ShapeDtypeStruct((...]
  transfers between devices with their start and end apart: 14 -> 14, of which waited for: 9 -> 9; matrix products, arithmetic and copies ran while one was open for 0% -> 0% of each run, Pallas kernels for 8% -> 6%
where the time goes in v5:
time: 139 us; the launch traced here: 138 us
  Pallas kernels  45.2 us (33%)
  blocking collectives  39.6 us (28%)
  starting transfers between devices  30.3 us (22%)
  waiting for transfers between devices  21.7 us (16%)
    all_to_all x1, blocking collectives, local(): lax.all_to_all(outgoing, 'seg', split_axis=0, concat_axis=0, tiled=True)  22 us
    ppermute x12, waiting for transfers between devices, moved(): return lax.ppermute(piece, 'ch', [((i + step) % 4, i) for i in range(4)])  21.7 us
    ppermute x12, starting transfers between devices, moved(): return lax.ppermute(piece, 'ch', [((i + step) % 4, i) for i in range(4)])  21.3 us
    pallas_call x1, Pallas kernels, second(): pl.pallas_call(second_kernel, name='second', out_shape=jax.ShapeDtypeStru...  19.8 us
    all_to_all x1, blocking collectives, local(): back = lax.all_to_all(going, 'seg', split_axis=0, concat_axis=0, tiled=True)  17.6 us
    pallas_call x1, Pallas kernels, first(): pl.pallas_call(first_kernel, name='first', out_shape=jax.ShapeDtypeStruct...  9.74 us
    ppermute x1, starting transfers between devices, local(): nxt = lax.ppermute(voxels[:HALO], 'seg', down)  7.09 us
    pallas_call x1, Pallas kernels, conv(): pl.pallas_call(conv_kernel, name='conv', out_shape=jax.ShapeDtypeStruct((...  6.21 us
  transfers between devices with their start and end apart: 14, of which 9 were waited for; matrix products, arithmetic and copies ran while one was open for 0% of the time, Pallas kernels for 6%

profile of v5, /device:TPU:8, one launch (start us, length us, event | category | flops | bytes accessed | tf_op | source)
XLA Modules:
  0.0 137.9 jit_solution(7655916207429738836)
XLA Ops:
  0.0 0.9 fusion
  0.9 7.1 %collective-permute-start.1 = (bf16[128,256]{1,0:T(8,128)(2,1)S(1)}, bf16[128,256]{1,0:T(8,128)(2,1)S(1)}, u32[]{:S(2)}, u32[]{:S(2)}) collective-permute-start(bf16[128,256]{1,0:T(8,128)(2,1)S(1)} %get-tuple-element.15), channel_id=1, source_target_pairs={{4,0},{8,4},{12,8},{16,12},{20,16},{24,20},{28,24},{32,28},{36,32}... | collective-permute-start | bytes 196616 | tf_op jit(solution)/shard_map/ppermute | solution.py:484
  8.0 1.9 %collective-permute-start = (bf16[128,256]{1,0:T(8,128)(2,1)S(1)}, bf16[128,256]{1,0:T(8,128)(2,1)S(1)}, u32[]{:S(2)}, u32[]{:S(2)}) collective-permute-start(bf16[128,256]{1,0:T(8,128)(2,1)S(1)} %get-tuple-element.16), channel_id=1, source_target_pairs={{0,4},{4,8},{8,12},{12,16},{16,20},{20,24},{24,28},{28,32},{32,36}... | collective-permute-start | bytes 196616 | tf_op jit(solution)/shard_map/ppermute | solution.py:483
  9.9 0.1 pad_add_fusion.ids
  10.0 0.0 copy-start.3
  10.0 0.0 copy-start.4
  10.0 6.2 %conv.1.sum_ref = f32[64,1024]{1,0:T(8,128)S(1)} custom-call(s32[2]{0:T(128)S(1)} %pad_add_fusion.ids, bf16[1024,256]{1,0:T(8,128)(2,1)} %own_hbm.1, s32[27,1024]{1,0:T(8,128)} %nb_ref.1, bf16[27,64,256]{2,1,0:T(8,128)(2,1)} %bitcast.12), custom_call_target="tpu_custom_call" | custom-call | flops 4000000000 | bytes 1048576 | tf_op jit(solution)/shard_map/conv/pallas_call | solution.py:138
  16.2 0.0 copy-start.1
  16.2 0.0 copy-start
  16.2 0.0 copy-start.5
  16.3 0.0 copy-start.7
  16.3 0.0 collective-permute-done.1.next_ref
  16.3 0.0 collective-permute-done.prev_ref
  16.3 0.0 copy-done.3
  16.3 0.0 copy-done.4
  16.3 2.2 %edge.1.x0.after_ref = bf16[64,1024]{1,0:T(8,128)(2,1)S(1)} custom-call(s32[2]{0:T(128)S(1)} %pad_add_fusion.ids, bf16[128,256]{1,0:T(8,128)(2,1)S(1)} %collective-permute-done.prev_ref, bf16[128,256]{1,0:T(8,128)(2,1)S(1)} %collective-permute-done.1.next_ref, s32[27,1024]{1,0:T(8,128)S(1)} %copy-done.4, bf16[27,64,256]{2,1,0:T(8,128)(2,1)S(1)} %bitcast.13, ...), custom_call_target="tpu_custom_call" | custom-call | flops 1000000000 | bytes 1048576 | tf_op jit(solution)/shard_map/edge/pallas_call | solution.py:193
  18.6 1.6 %collective-permute-start.4 = (bf16[64,1024]{1,0:T(8,128)(2,1)S(1)}, bf16[64,1024]{1,0:T(8,128)(2,1)S(1)}, u32[]{:S(2)}, u32[]{:S(2)}) collective-permute-start(bf16[64,1024]{1,0:T(8,128)(2,1)S(1)} %edge.1.x0.after_ref), channel_id=1, source_target_pairs={{3,0},{0,1},{1,2},{2,3},{7,4},{4,5},{5,6},{6,7},{11,8},{8,9},{9,10... | collective-permute-start | bytes 393224 | tf_op jit(solution)/shard_map/ppermute | solution.py:471
  20.1 2.7 %collective-permute-start.3 = (bf16[64,1024]{1,0:T(8,128)(2,1)S(1)}, bf16[64,1024]{1,0:T(8,128)(2,1)S(1)}, u32[]{:S(2)}, u32[]{:S(2)}) collective-permute-start(bf16[64,1024]{1,0:T(8,128)(2,1)S(1)} %edge.1.x0.after_ref), channel_id=1, source_target_pairs={{2,0},{3,1},{0,2},{1,3},{6,4},{7,5},{4,6},{5,7},{10,8},{11,9},{8,1... | collective-permute-start | bytes 393224 | tf_op jit(solution)/shard_map/ppermute | solution.py:471
  22.8 1.4 %collective-permute-start.2 = (bf16[64,1024]{1,0:T(8,128)(2,1)S(1)}, bf16[64,1024]{1,0:T(8,128)(2,1)S(1)}, u32[]{:S(2)}, u32[]{:S(2)}) collective-permute-start(bf16[64,1024]{1,0:T(8,128)(2,1)S(1)} %edge.1.x0.after_ref), channel_id=1, source_target_pairs={{1,0},{2,1},{3,2},{0,3},{5,4},{6,5},{7,6},{4,7},{9,8},{10,9},{11,1... | collective-permute-start | bytes 393224 | tf_op jit(solution)/shard_map/ppermute | solution.py:471
  24.3 0.5 collective-permute-done.4.x3
  24.8 2.4 %collective-permute-done.3.x2 = bf16[64,1024]{1,0:T(8,128)(2,1)S(1)} collective-permute-done((bf16[64,1024]{1,0:T(8,128)(2,1)S(1)}, bf16[64,1024]{1,0:T(8,128)(2,1)S(1)}, u32[]{:S(2)}, u32[]{:S(2)}) %collective-permute-start.3) | collective-permute-done | bytes 131104 | tf_op jit(solution)/shard_map/ppermute | solution.py:471
  27.2 0.6 collective-permute-done.2.x1
  27.8 0.0 copy-done.1
  27.8 9.7 %first.1.h0 = bf16[64,1024]{1,0:T(8,128)(2,1)S(1)} custom-call(s32[2]{0:T(128)S(1)} %pad_add_fusion.ids, bf16[64,1024]{1,0:T(8,128)(2,1)S(1)} %edge.1.x0.after_ref, bf16[64,1024]{1,0:T(8,128)(2,1)S(1)} %collective-permute-done.2.x1, bf16[64,1024]{1,0:T(8,128)(2,1)S(1)} %collective-permute-done.3.x2, bf16[64,1024]{1,0:T(8,128)(2,1)S(1)} %collective-permute-done.4.x3, ...), custom_call_target="tpu_custom_call" | custom-call | tf_op jit(solution)/shard_map/first/pallas_call | solution.py:318
  37.6 0.0 copy-start.6
  37.6 1.4 collective-permute-start.7
  38.9 2.8 %collective-permute-start.6 = (bf16[64,1024]{1,0:T(8,128)(2,1)S(1)}, bf16[64,1024]{1,0:T(8,128)(2,1)S(1)}, u32[]{:S(2)}, u32[]{:S(2)}) collective-permute-start(bf16[64,1024]{1,0:T(8,128)(2,1)S(1)} %first.1.h0), channel_id=1, source_target_pairs={{2,0},{3,1},{0,2},{1,3},{6,4},{7,5},{4,6},{5,7},{10,8},{11,9},{8,1... | collective-permute-start | bytes 393224 | tf_op jit(solution)/shard_map/ppermute | solution.py:471
  41.7 0.9 collective-permute-start.5
  42.6 0.0 copy-done
  42.6 0.0 copy-done.5
  42.6 0.0 copy-done.7
  42.6 1.7 %prep.1 = (bf16[512,1024]{1,0:T(8,128)(2,1)S(1)}, bf16[1024,1024]{1,0:T(8,128)(2,1)S(1)}, bf16[64,256]{1,0:T(8,128)(2,1)S(1)}) custom-call(s32[2]{0:T(128)S(1)} %pad_add_fusion.ids, bf16[64,1024]{1,0:T(8,128)(2,1)S(1)} %edge.1.x0.after_ref, bf16[256,256]{1,0:T(8,128)(2,1)S(1)} %copy-done.5, s32[1,1024]{1,0:T(1,128)S(1)} %copy-done.7, s32[64,64]{1,0:T(8,128)S(1)} %copy-done), custom_call_target="tpu_custom_call" | custom-call | flops 1500000000 | bytes 1048576 | tf_op jit(solution)/shard_map/prep/pallas_call | solution.py:229
  44.3 0.0 collective-permute-done.7.h3
  44.3 1.7 %collective-permute-done.6.h2 = bf16[64,1024]{1,0:T(8,128)(2,1)S(1)} collective-permute-done((bf16[64,1024]{1,0:T(8,128)(2,1)S(1)}, bf16[64,1024]{1,0:T(8,128)(2,1)S(1)}, u32[]{:S(2)}, u32[]{:S(2)}) %collective-permute-start.6) | collective-permute-done | bytes 131104 | tf_op jit(solution)/shard_map/ppermute | solution.py:471
  46.0 0.6 collective-permute-done.5.h1
  46.7 0.0 copy-done.6
  46.7 0.0 copy-start.2
  46.7 1.6 %pick.1 = (bf16[64,8,256]{2,1,0:T(8,128)(2,1)S(1)}, bf16[64,1024]{1,0:T(8,128)(2,1)S(1)}) custom-call(s32[2]{0:T(128)S(1)} %pad_add_fusion.ids, bf16[64,1024]{1,0:T(8,128)(2,1)S(1)} %edge.1.x0.after_ref, bf16[64,1024]{1,0:T(8,128)(2,1)S(1)} %collective-permute-done.2.x1, bf16[64,1024]{1,0:T(8,128)(2,1)S(1)} %collective-permute-done.3.x2, ...), custom_call_target="tpu_custom_call" | custom-call | flops 1000000000 | bytes 1048576 | tf_op jit(solution)/shard_map/pick/pallas_call | solution.py:350
  48.3 22.0 %all_to_all.10.a0 = bf16[64,8,256]{2,1,0:T(8,128)(2,1)S(1)} all-to-all(bf16[64,8,256]{2,1,0:T(8,128)(2,1)S(1)} %get-tuple-element.12), channel_id=1, replica_groups=mesh['seg'=64,'ch'=4] {'seg'}, dimensions={0} | all-to-all | bytes 524288 | tf_op jit(solution)/shard_map/all_to_all | solution.py:494
  70.3 1.7 %collective-permute-start.10 = (bf16[64,8,256]{2,1,0:T(8,128)(2,1)S(1)}, bf16[64,8,256]{2,1,0:T(8,128)(2,1)S(1)}, u32[]{:S(2)}, u32[]{:S(2)}) collective-permute-start(bf16[64,8,256]{2,1,0:T(8,128)(2,1)S(1)} %all_to_all.10.a0), channel_id=1, source_target_pairs={{3,0},{0,1},{1,2},{2,3},{7,4},{4,5},{5,6},{6,7},{11,8},{8,9},{9,10... | collective-permute-start | bytes 786440 | tf_op jit(solution)/shard_map/ppermute | solution.py:471
  72.0 2.4 %collective-permute-start.9 = (bf16[64,8,256]{2,1,0:T(8,128)(2,1)S(1)}, bf16[64,8,256]{2,1,0:T(8,128)(2,1)S(1)}, u32[]{:S(2)}, u32[]{:S(2)}) collective-permute-start(bf16[64,8,256]{2,1,0:T(8,128)(2,1)S(1)} %all_to_all.10.a0), channel_id=1, source_target_pairs={{2,0},{3,1},{0,2},{1,3},{6,4},{7,5},{4,6},{5,7},{10,8},{11,9},{8,1... | collective-permute-start | bytes 786440 | tf_op jit(solution)/shard_map/ppermute | solution.py:471
  74.4 1.2 collective-permute-start.8
  75.6 4.2 %collective-permute-done.10.a3 = bf16[64,8,256]{2,1,0:T(8,128)(2,1)S(1)} collective-permute-done((bf16[64,8,256]{2,1,0:T(8,128)(2,1)S(1)}, bf16[64,8,256]{2,1,0:T(8,128)(2,1)S(1)}, u32[]{:S(2)}, u32[]{:S(2)}) %collective-permute-start.10) | collective-permute-done | bytes 262176 | tf_op jit(solution)/shard_map/ppermute | solution.py:471
  79.8 6.5 %collective-permute-done.9.a2 = bf16[64,8,256]{2,1,0:T(8,128)(2,1)S(1)} collective-permute-done((bf16[64,8,256]{2,1,0:T(8,128)(2,1)S(1)}, bf16[64,8,256]{2,1,0:T(8,128)(2,1)S(1)}, u32[]{:S(2)}, u32[]{:S(2)}) %collective-permute-start.9) | collective-permute-done | bytes 262176 | tf_op jit(solution)/shard_map/ppermute | solution.py:471
  86.3 0.0 collective-permute-done.8.a1
  86.3 0.0 copy-done.2
  86.3 19.8 %second.1 = bf16[64,16,128]{2,1,0:T(8,128)(2,1)S(1)} custom-call(s32[2]{0:T(128)S(1)} %pad_add_fusion.ids, s32[64,64]{1,0:T(8,128)S(1)} %copy-done, bf16[64,8,256]{2,1,0:T(8,128)(2,1)S(1)} %all_to_all.10.a0, bf16[64,8,256]{2,1,0:T(8,128)(2,1)S(1)} %collective-permute-done.8.a1, bf16[64,8,256]{2,1,0:T(8,128)(2,1)S(1)} %collective-permute-done.9.a2, ...), custom_call_target="tpu_custom_call" | custom-call | tf_op jit(solution)/shard_map/second/pallas_call | solution.py:406
  106.1 17.6 %all_to_all.11.back_ref = bf16[64,16,128]{2,1,0:T(8,128)(2,1)S(1)} all-to-all(bf16[64,16,128]{2,1,0:T(8,128)(2,1)S(1)} %second.1), channel_id=1, replica_groups=mesh['seg'=64,'ch'=4] {'seg'}, dimensions={0} | all-to-all | bytes 524288 | tf_op jit(solution)/shard_map/all_to_all | solution.py:496
  123.8 2.5 %home.1.h0 = bf16[64,1024]{1,0:T(8,128)(2,1)S(1)} custom-call(s32[2]{0:T(128)S(1)} %pad_add_fusion.ids, s32[64,64]{1,0:T(8,128)S(1)} %copy-done, bf16[64,16,128]{2,1,0:T(8,128)(2,1)S(1)} %all_to_all.11.back_ref, bf16[1024,1024]{1,0:T(8,128)(2,1)S(1)} %get-tuple-element.13.chosen_ref), custom_call_target="tpu_custom_call" | custom-call | tf_op jit(solution)/shard_map/home/pallas_call | solution.py:440
  126.2 1.5 %collective-permute-start.13 = (bf16[64,1024]{1,0:T(8,128)(2,1)S(1)}, bf16[64,1024]{1,0:T(8,128)(2,1)S(1)}, u32[]{:S(2)}, u32[]{:S(2)}) collective-permute-start(bf16[64,1024]{1,0:T(8,128)(2,1)S(1)} %home.1.h0), channel_id=1, source_target_pairs={{3,0},{0,1},{1,2},{2,3},{7,4},{4,5},{5,6},{6,7},{11,8},{8,9},{9,10... | collective-permute-start | bytes 393224 | tf_op jit(solution)/shard_map/ppermute | solution.py:471
  127.8 2.4 %collective-permute-start.12 = (bf16[64,1024]{1,0:T(8,128)(2,1)S(1)}, bf16[64,1024]{1,0:T(8,128)(2,1)S(1)}, u32[]{:S(2)}, u32[]{:S(2)}) collective-permute-start(bf16[64,1024]{1,0:T(8,128)(2,1)S(1)} %home.1.h0), channel_id=1, source_target_pairs={{2,0},{3,1},{0,2},{1,3},{6,4},{7,5},{4,6},{5,7},{10,8},{11,9},{8,1... | collective-permute-start | bytes 393224 | tf_op jit(solution)/shard_map/ppermute | solution.py:471
  130.2 1.2 collective-permute-start.11
  131.4 1.9 %collective-permute-done.13.h3 = bf16[64,1024]{1,0:T(8,128)(2,1)S(1)} collective-permute-done((bf16[64,1024]{1,0:T(8,128)(2,1)S(1)}, bf16[64,1024]{1,0:T(8,128)(2,1)S(1)}, u32[]{:S(2)}, u32[]{:S(2)}) %collective-permute-start.13) | collective-permute-done | bytes 131104 | tf_op jit(solution)/shard_map/ppermute | solution.py:471
  133.3 3.2 %collective-permute-done.12.h2 = bf16[64,1024]{1,0:T(8,128)(2,1)S(1)} collective-permute-done((bf16[64,1024]{1,0:T(8,128)(2,1)S(1)}, bf16[64,1024]{1,0:T(8,128)(2,1)S(1)}, u32[]{:S(2)}, u32[]{:S(2)}) %collective-permute-start.12) | collective-permute-done | bytes 131104 | tf_op jit(solution)/shard_map/ppermute | solution.py:471
  136.5 0.0 collective-permute-done.11.h1
  136.5 1.5 %last.1 = bf16[64,1024]{1,0:T(8,128)(2,1)} custom-call(s32[2]{0:T(128)S(1)} %pad_add_fusion.ids, bf16[64,1024]{1,0:T(8,128)(2,1)S(1)} %get-tuple-element.11.mine_ref, bf16[64,1024]{1,0:T(8,128)(2,1)S(1)} %home.1.h0, bf16[64,1024]{1,0:T(8,128)(2,1)S(1)} %collective-permute-done.11.h1, bf16[64,1024]{1,0:T(8,128)(2,1)S(1)} %collective-permute-done.12.h2, ...), custom_call_target="tpu_custom_call" | custom-call | tf_op jit(solution)/shard_map/last/pallas_call | solution.py:458
Async XLA Ops:
  0.9 15.4 %collective-permute-start.1 = (bf16[128,256]{1,0:T(8,128)(2,1)S(1)}, bf16[128,256]{1,0:T(8,128)(2,1)S(1)}, u32[]{:S(2)}, u32[]{:S(2)}) collective-permute-start(bf16[128,256]{1,0:T(8,128)(2,1)S(1)} %get-tuple-element.15), channel_id=1, source_target_pairs={{4,0},{8,4},{12,8},{16,12},{20,16},{24,20},{28,24},{32,28},{36,32}... | collective-permute-start | bytes 196616 | tf_op jit(solution)/shard_map/ppermute | solution.py:484
  8.0 8.3 %collective-permute-start = (bf16[128,256]{1,0:T(8,128)(2,1)S(1)}, bf16[128,256]{1,0:T(8,128)(2,1)S(1)}, u32[]{:S(2)}, u32[]{:S(2)}) collective-permute-start(bf16[128,256]{1,0:T(8,128)(2,1)S(1)} %get-tuple-element.16), channel_id=1, source_target_pairs={{0,4},{4,8},{8,12},{12,16},{16,20},{20,24},{24,28},{28,32},{32,36}... | collective-permute-start | bytes 196616 | tf_op jit(solution)/shard_map/ppermute | solution.py:483
  10.0 6.3 %copy-start.3 = (bf16[27,256,64]{1,2,0:T(8,128)(2,1)S(1)}, bf16[27,256,64]{1,2,0:T(8,128)(2,1)}, u32[]{:S(2)}) copy-start(bf16[27,256,64]{1,2,0:T(8,128)(2,1)} %param.13) | copy-start | bytes 2654212
  10.0 6.3 %copy-start.4 = (s32[27,1024]{1,0:T(8,128)S(1)}, s32[27,1024]{1,0:T(8,128)}, u32[]{:S(2)}) copy-start(s32[27,1024]{1,0:T(8,128)} %nb_ref.1) | copy-start | bytes 331780
  16.2 11.6 %copy-start.1 = (bf16[256,3,64]{0,2,1:T(8,128)(2,1)S(1)}, bf16[256,3,64]{0,2,1:T(8,128)(2,1)}, u32[]{:S(2)}) copy-start(bf16[256,3,64]{0,2,1:T(8,128)(2,1)} %param.14) | copy-start | bytes 294916
  16.2 26.4 %copy-start = (s32[64,64]{1,0:T(8,128)S(1)}, s32[64,64]{1,0:T(8,128)}, u32[]{:S(2)}) copy-start(s32[64,64]{1,0:T(8,128)} %counts_sm.3) | copy-start | bytes 49156
  16.2 26.4 %copy-start.5 = (bf16[256,256]{1,0:T(8,128)(2,1)S(1)}, bf16[256,256]{1,0:T(8,128)(2,1)}, u32[]{:S(2)}) copy-start(bf16[256,256]{1,0:T(8,128)(2,1)} %wo_ref.2) | copy-start | bytes 393220
  16.3 26.4 %copy-start.7 = (s32[1,1024]{1,0:T(1,128)S(1)}, s32[1,1024]{1,0:T(1,128)}, u32[]{:S(2)}) copy-start(s32[1,1024]{1,0:T(1,128)} %perm_ref.1) | copy-start | bytes 12292
  18.6 6.3 %collective-permute-start.4 = (bf16[64,1024]{1,0:T(8,128)(2,1)S(1)}, bf16[64,1024]{1,0:T(8,128)(2,1)S(1)}, u32[]{:S(2)}, u32[]{:S(2)}) collective-permute-start(bf16[64,1024]{1,0:T(8,128)(2,1)S(1)} %edge.1.x0.after_ref), channel_id=1, source_target_pairs={{3,0},{0,1},{1,2},{2,3},{7,4},{4,5},{5,6},{6,7},{11,8},{8,9},{9,10... | collective-permute-start | bytes 393224 | tf_op jit(solution)/shard_map/ppermute | solution.py:471
  20.1 7.1 %collective-permute-start.3 = (bf16[64,1024]{1,0:T(8,128)(2,1)S(1)}, bf16[64,1024]{1,0:T(8,128)(2,1)S(1)}, u32[]{:S(2)}, u32[]{:S(2)}) collective-permute-start(bf16[64,1024]{1,0:T(8,128)(2,1)S(1)} %edge.1.x0.after_ref), channel_id=1, source_target_pairs={{2,0},{3,1},{0,2},{1,3},{6,4},{7,5},{4,6},{5,7},{10,8},{11,9},{8,1... | collective-permute-start | bytes 393224 | tf_op jit(solution)/shard_map/ppermute | solution.py:471
  22.8 5.0 %collective-permute-start.2 = (bf16[64,1024]{1,0:T(8,128)(2,1)S(1)}, bf16[64,1024]{1,0:T(8,128)(2,1)S(1)}, u32[]{:S(2)}, u32[]{:S(2)}) collective-permute-start(bf16[64,1024]{1,0:T(8,128)(2,1)S(1)} %edge.1.x0.after_ref), channel_id=1, source_target_pairs={{1,0},{2,1},{3,2},{0,3},{5,4},{6,5},{7,6},{4,7},{9,8},{10,9},{11,1... | collective-permute-start | bytes 393224 | tf_op jit(solution)/shard_map/ppermute | solution.py:471
  37.6 9.1 %copy-start.6 = (bf16[256,256]{1,0:T(8,128)(2,1)S(1)}, bf16[256,256]{1,0:T(8,128)(2,1)}, u32[]{:S(2)}) copy-start(bf16[256,256]{1,0:T(8,128)(2,1)} %wo_ref.3) | copy-start | bytes 393220
  37.6 6.7 %collective-permute-start.7 = (bf16[64,1024]{1,0:T(8,128)(2,1)S(1)}, bf16[64,1024]{1,0:T(8,128)(2,1)S(1)}, u32[]{:S(2)}, u32[]{:S(2)}) collective-permute-start(bf16[64,1024]{1,0:T(8,128)(2,1)S(1)} %first.1.h0), channel_id=1, source_target_pairs={{3,0},{0,1},{1,2},{2,3},{7,4},{4,5},{5,6},{6,7},{11,8},{8,9},{9,10... | collective-permute-start | bytes 393224 | tf_op jit(solution)/shard_map/ppermute | solution.py:471
  38.9 7.1 %collective-permute-start.6 = (bf16[64,1024]{1,0:T(8,128)(2,1)S(1)}, bf16[64,1024]{1,0:T(8,128)(2,1)S(1)}, u32[]{:S(2)}, u32[]{:S(2)}) collective-permute-start(bf16[64,1024]{1,0:T(8,128)(2,1)S(1)} %first.1.h0), channel_id=1, source_target_pairs={{2,0},{3,1},{0,2},{1,3},{6,4},{7,5},{4,6},{5,7},{10,8},{11,9},{8,1... | collective-permute-start | bytes 393224 | tf_op jit(solution)/shard_map/ppermute | solution.py:471
  41.7 5.0 %collective-permute-start.5 = (bf16[64,1024]{1,0:T(8,128)(2,1)S(1)}, bf16[64,1024]{1,0:T(8,128)(2,1)S(1)}, u32[]{:S(2)}, u32[]{:S(2)}) collective-permute-start(bf16[64,1024]{1,0:T(8,128)(2,1)S(1)} %first.1.h0), channel_id=1, source_target_pairs={{1,0},{2,1},{3,2},{0,3},{5,4},{6,5},{7,6},{4,7},{9,8},{10,9},{11,1... | collective-permute-start | bytes 393224 | tf_op jit(solution)/shard_map/ppermute | solution.py:471
  46.7 39.6 %copy-start.2 = (bf16[256,3,64]{0,2,1:T(8,128)(2,1)S(1)}, bf16[256,3,64]{0,2,1:T(8,128)(2,1)}, u32[]{:S(2)}) copy-start(bf16[256,3,64]{0,2,1:T(8,128)(2,1)} %param.16) | copy-start | bytes 294916
  70.3 9.6 %collective-permute-start.10 = (bf16[64,8,256]{2,1,0:T(8,128)(2,1)S(1)}, bf16[64,8,256]{2,1,0:T(8,128)(2,1)S(1)}, u32[]{:S(2)}, u32[]{:S(2)}) collective-permute-start(bf16[64,8,256]{2,1,0:T(8,128)(2,1)S(1)} %all_to_all.10.a0), channel_id=1, source_target_pairs={{3,0},{0,1},{1,2},{2,3},{7,4},{4,5},{5,6},{6,7},{11,8},{8,9},{9,10... | collective-permute-start | bytes 786440 | tf_op jit(solution)/shard_map/ppermute | solution.py:471
  72.0 14.3 %collective-permute-start.9 = (bf16[64,8,256]{2,1,0:T(8,128)(2,1)S(1)}, bf16[64,8,256]{2,1,0:T(8,128)(2,1)S(1)}, u32[]{:S(2)}, u32[]{:S(2)}) collective-permute-start(bf16[64,8,256]{2,1,0:T(8,128)(2,1)S(1)} %all_to_all.10.a0), channel_id=1, source_target_pairs={{2,0},{3,1},{0,2},{1,3},{6,4},{7,5},{4,6},{5,7},{10,8},{11,9},{8,1... | collective-permute-start | bytes 786440 | tf_op jit(solution)/shard_map/ppermute | solution.py:471
  74.4 11.9 %collective-permute-start.8 = (bf16[64,8,256]{2,1,0:T(8,128)(2,1)S(1)}, bf16[64,8,256]{2,1,0:T(8,128)(2,1)S(1)}, u32[]{:S(2)}, u32[]{:S(2)}) collective-permute-start(bf16[64,8,256]{2,1,0:T(8,128)(2,1)S(1)} %all_to_all.10.a0), channel_id=1, source_target_pairs={{1,0},{2,1},{3,2},{0,3},{5,4},{6,5},{7,6},{4,7},{9,8},{10,9},{11,1... | collective-permute-start | bytes 786440 | tf_op jit(solution)/shard_map/ppermute | solution.py:471
  126.2 7.0 %collective-permute-start.13 = (bf16[64,1024]{1,0:T(8,128)(2,1)S(1)}, bf16[64,1024]{1,0:T(8,128)(2,1)S(1)}, u32[]{:S(2)}, u32[]{:S(2)}) collective-permute-start(bf16[64,1024]{1,0:T(8,128)(2,1)S(1)} %home.1.h0), channel_id=1, source_target_pairs={{3,0},{0,1},{1,2},{2,3},{7,4},{4,5},{5,6},{6,7},{11,8},{8,9},{9,10... | collective-permute-start | bytes 393224 | tf_op jit(solution)/shard_map/ppermute | solution.py:471
  127.8 8.7 %collective-permute-start.12 = (bf16[64,1024]{1,0:T(8,128)(2,1)S(1)}, bf16[64,1024]{1,0:T(8,128)(2,1)S(1)}, u32[]{:S(2)}, u32[]{:S(2)}) collective-permute-start(bf16[64,1024]{1,0:T(8,128)(2,1)S(1)} %home.1.h0), channel_id=1, source_target_pairs={{2,0},{3,1},{0,2},{1,3},{6,4},{7,5},{4,6},{5,7},{10,8},{11,9},{8,1... | collective-permute-start | bytes 393224 | tf_op jit(solution)/shard_map/ppermute | solution.py:471
  130.2 6.3 %collective-permute-start.11 = (bf16[64,1024]{1,0:T(8,128)(2,1)S(1)}, bf16[64,1024]{1,0:T(8,128)(2,1)S(1)}, u32[]{:S(2)}, u32[]{:S(2)}) collective-permute-start(bf16[64,1024]{1,0:T(8,128)(2,1)S(1)} %home.1.h0), channel_id=1, source_target_pairs={{1,0},{2,1},{3,2},{0,3},{5,4},{6,5},{7,6},{4,7},{9,8},{10,9},{11,1... | collective-permute-start | bytes 393224 | tf_op jit(solution)/shard_map/ppermute | solution.py:471

commit v6 on v5

--- a/solution.py
+++ b/solution.py
@@ -19,6 +19,7 @@
 NT = (((1,), (1,)), ((), ()))
 TN = (((0,), (0,)), ((), ()))
 DN = lax.GatherDimensionNumbers((), (1,), (1,), (0,), (0,))
+STEPS = (0, 1, 3, 2)
 VM = pl.BlockSpec(memory_space=pltpu.VMEM)
 SM = pl.BlockSpec(memory_space=pltpu.SMEM)
 PARAMS = pltpu.CompilerParams(vmem_limit_bytes=50 << 20)
@@ -53,7 +54,7 @@
 
 def place(pieces, ch, full_ref):
     size = pieces[0].shape[0]
-    for j, piece in enumerate(pieces):
+    for j, piece in zip(STEPS, pieces):
         owner = (ch + j) & 3
         full_ref[pl.ds(pl.multiple_of(owner * size, size), size), :] = piece[...]
 
@@ -372,7 +373,7 @@
 
     def compact(s, off):
         tiles = [piece[s].astype(F32) for piece in (a0, a1, a2, a3)]
-        for j, tile in enumerate(tiles):
+        for j, tile in zip(STEPS, tiles):
             dst = pl.ds(off + ((ch + j) & 3) * 8, 8)
             lo_ref[dst, :] = tile[:, :128]
             hi_ref[dst, :] = tile[:, 128:]
@@ -470,7 +471,7 @@
     def moved(step):
         return lax.ppermute(piece, "ch", [((i + step) % 4, i) for i in range(4)])
 
-    return piece, moved(1), moved(2), moved(3)
+    return piece, moved(1), moved(3), moved(2)
 
 
 def local(

time: 139 us -> 138 us (level)
  transfers between devices with their start and end apart: 14 -> 14, of which waited for: 9 -> 10; matrix products, arithmetic and copies ran while one was open for 0% -> 0% of each run, Pallas kernels for 6% -> 6%
where the time goes in v6:
time: 138 us; the launch traced here: 136 us
  Pallas kernels  45.2 us (33%)
  blocking collectives  38.6 us (28%)
  starting transfers between devices  30.9 us (22%)
  waiting for transfers between devices  20.4 us (15%)
    ppermute x12, starting transfers between devices, moved(): return lax.ppermute(piece, 'ch', [((i + step) % 4, i) for i in range(4)])  21.8 us
    all_to_all x1, blocking collectives, local(): lax.all_to_all(outgoing, 'seg', split_axis=0, concat_axis=0, tiled=True)  21 us
    ppermute x12, waiting for transfers between devices, moved(): return lax.ppermute(piece, 'ch', [((i + step) % 4, i) for i in range(4)])  20.4 us
    pallas_call x1, Pallas kernels, second(): pl.pallas_call(second_kernel, name='second', out_shape=jax.ShapeDtypeStru...  19.8 us
    all_to_all x1, blocking collectives, local(): back = lax.all_to_all(going, 'seg', split_axis=0, concat_axis=0, tiled=True)  17.6 us
    pallas_call x1, Pallas kernels, first(): pl.pallas_call(first_kernel, name='first', out_shape=jax.ShapeDtypeStruct...  9.67 us
    ppermute x1, starting transfers between devices, local(): nxt = lax.ppermute(voxels[:HALO], 'seg', down)  7.09 us
    pallas_call x1, Pallas kernels, conv(): pl.pallas_call(conv_kernel, name='conv', out_shape=jax.ShapeDtypeStruct((...  6.21 us
  transfers between devices with their start and end apart: 14, of which 10 were waited for; matrix products, arithmetic and copies ran while one was open for 0% of the time, Pallas kernels for 6%

profile of v6, /device:TPU:8, one launch (start us, length us, event | category | flops | bytes accessed | tf_op | source)
XLA Modules:
  0.0 136.2 jit_solution(15603864486354677730)
XLA Ops:
  0.0 0.9 fusion
  0.9 7.1 %collective-permute-start.1 = (bf16[128,256]{1,0:T(8,128)(2,1)S(1)}, bf16[128,256]{1,0:T(8,128)(2,1)S(1)}, u32[]{:S(2)}, u32[]{:S(2)}) collective-permute-start(bf16[128,256]{1,0:T(8,128)(2,1)S(1)} %get-tuple-element.15), channel_id=1, source_target_pairs={{4,0},{8,4},{12,8},{16,12},{20,16},{24,20},{28,24},{32,28},{36,32}... | collective-permute-start | bytes 196616 | tf_op jit(solution)/shard_map/ppermute | solution.py:485
  8.0 1.9 %collective-permute-start = (bf16[128,256]{1,0:T(8,128)(2,1)S(1)}, bf16[128,256]{1,0:T(8,128)(2,1)S(1)}, u32[]{:S(2)}, u32[]{:S(2)}) collective-permute-start(bf16[128,256]{1,0:T(8,128)(2,1)S(1)} %get-tuple-element.16), channel_id=1, source_target_pairs={{0,4},{4,8},{8,12},{12,16},{16,20},{20,24},{24,28},{28,32},{32,36}... | collective-permute-start | bytes 196616 | tf_op jit(solution)/shard_map/ppermute | solution.py:484
  9.9 0.1 pad_add_fusion.ids
  10.0 0.0 copy-start.3
  10.0 0.0 copy-start.4
  10.0 6.2 %conv.1.sum_ref = f32[64,1024]{1,0:T(8,128)S(1)} custom-call(s32[2]{0:T(128)S(1)} %pad_add_fusion.ids, bf16[1024,256]{1,0:T(8,128)(2,1)} %own_hbm.1, s32[27,1024]{1,0:T(8,128)} %nb_ref.1, bf16[27,64,256]{2,1,0:T(8,128)(2,1)} %bitcast.12), custom_call_target="tpu_custom_call" | custom-call | flops 4000000000 | bytes 1048576 | tf_op jit(solution)/shard_map/conv/pallas_call | solution.py:139
  16.2 0.0 copy-start.1
  16.2 0.0 copy-start
  16.2 0.0 copy-start.5
  16.3 0.0 copy-start.7
  16.3 0.0 collective-permute-done.1.next_ref
  16.3 0.0 collective-permute-done.prev_ref
  16.3 0.0 copy-done.3
  16.3 0.0 copy-done.4
  16.3 2.2 %edge.1.x0.after_ref = bf16[64,1024]{1,0:T(8,128)(2,1)S(1)} custom-call(s32[2]{0:T(128)S(1)} %pad_add_fusion.ids, bf16[128,256]{1,0:T(8,128)(2,1)S(1)} %collective-permute-done.prev_ref, bf16[128,256]{1,0:T(8,128)(2,1)S(1)} %collective-permute-done.1.next_ref, s32[27,1024]{1,0:T(8,128)S(1)} %copy-done.4, bf16[27,64,256]{2,1,0:T(8,128)(2,1)S(1)} %bitcast.13, ...), custom_call_target="tpu_custom_call" | custom-call | flops 1000000000 | bytes 1048576 | tf_op jit(solution)/shard_map/edge/pallas_call | solution.py:194
  18.6 3.1 %collective-permute-start.4 = (bf16[64,1024]{1,0:T(8,128)(2,1)S(1)}, bf16[64,1024]{1,0:T(8,128)(2,1)S(1)}, u32[]{:S(2)}, u32[]{:S(2)}) collective-permute-start(bf16[64,1024]{1,0:T(8,128)(2,1)S(1)} %edge.1.x0.after_ref), channel_id=1, source_target_pairs={{2,0},{3,1},{0,2},{1,3},{6,4},{7,5},{4,6},{5,7},{10,8},{11,9},{8,1... | collective-permute-start | bytes 393224 | tf_op jit(solution)/shard_map/ppermute | solution.py:472
  21.7 0.6 collective-permute-start.3
  22.2 2.7 %collective-permute-start.2 = (bf16[64,1024]{1,0:T(8,128)(2,1)S(1)}, bf16[64,1024]{1,0:T(8,128)(2,1)S(1)}, u32[]{:S(2)}, u32[]{:S(2)}) collective-permute-start(bf16[64,1024]{1,0:T(8,128)(2,1)S(1)} %edge.1.x0.after_ref), channel_id=1, source_target_pairs={{1,0},{2,1},{3,2},{0,3},{5,4},{6,5},{7,6},{4,7},{9,8},{10,9},{11,1... | collective-permute-start | bytes 393224 | tf_op jit(solution)/shard_map/ppermute | solution.py:472
  24.9 0.2 collective-permute-done.4.x3
  25.1 2.7 %collective-permute-done.3.x2 = bf16[64,1024]{1,0:T(8,128)(2,1)S(1)} collective-permute-done((bf16[64,1024]{1,0:T(8,128)(2,1)S(1)}, bf16[64,1024]{1,0:T(8,128)(2,1)S(1)}, u32[]{:S(2)}, u32[]{:S(2)}) %collective-permute-start.3) | collective-permute-done | bytes 131104 | tf_op jit(solution)/shard_map/ppermute | solution.py:472
  27.8 0.0 collective-permute-done.2.x1
  27.8 0.0 copy-done.1
  27.8 9.7 %first.1.h0 = bf16[64,1024]{1,0:T(8,128)(2,1)S(1)} custom-call(s32[2]{0:T(128)S(1)} %pad_add_fusion.ids, bf16[64,1024]{1,0:T(8,128)(2,1)S(1)} %edge.1.x0.after_ref, bf16[64,1024]{1,0:T(8,128)(2,1)S(1)} %collective-permute-done.2.x1, bf16[64,1024]{1,0:T(8,128)(2,1)S(1)} %collective-permute-done.3.x2, bf16[64,1024]{1,0:T(8,128)(2,1)S(1)} %collective-permute-done.4.x3, ...), custom_call_target="tpu_custom_call" | custom-call | tf_op jit(solution)/shard_map/first/pallas_call | solution.py:319
  37.5 0.0 copy-start.6
  37.5 1.5 %collective-permute-start.7 = (bf16[64,1024]{1,0:T(8,128)(2,1)S(1)}, bf16[64,1024]{1,0:T(8,128)(2,1)S(1)}, u32[]{:S(2)}, u32[]{:S(2)}) collective-permute-start(bf16[64,1024]{1,0:T(8,128)(2,1)S(1)} %first.1.h0), channel_id=1, source_target_pairs={{2,0},{3,1},{0,2},{1,3},{6,4},{7,5},{4,6},{5,7},{10,8},{11,9},{8,1... | collective-permute-start | bytes 393224 | tf_op jit(solution)/shard_map/ppermute | solution.py:472
  39.1 2.6 %collective-permute-start.6 = (bf16[64,1024]{1,0:T(8,128)(2,1)S(1)}, bf16[64,1024]{1,0:T(8,128)(2,1)S(1)}, u32[]{:S(2)}, u32[]{:S(2)}) collective-permute-start(bf16[64,1024]{1,0:T(8,128)(2,1)S(1)} %first.1.h0), channel_id=1, source_target_pairs={{3,0},{0,1},{1,2},{2,3},{7,4},{4,5},{5,6},{6,7},{11,8},{8,9},{9,10... | collective-permute-start | bytes 393224 | tf_op jit(solution)/shard_map/ppermute | solution.py:472
  41.7 0.6 collective-permute-start.5
  42.3 0.0 copy-done
  42.3 0.0 copy-done.5
  42.3 0.0 copy-done.7
  42.3 1.7 %prep.1 = (bf16[512,1024]{1,0:T(8,128)(2,1)S(1)}, bf16[1024,1024]{1,0:T(8,128)(2,1)S(1)}, bf16[64,256]{1,0:T(8,128)(2,1)S(1)}) custom-call(s32[2]{0:T(128)S(1)} %pad_add_fusion.ids, bf16[64,1024]{1,0:T(8,128)(2,1)S(1)} %edge.1.x0.after_ref, bf16[256,256]{1,0:T(8,128)(2,1)S(1)} %copy-done.5, s32[1,1024]{1,0:T(1,128)S(1)} %copy-done.7, s32[64,64]{1,0:T(8,128)S(1)} %copy-done), custom_call_target="tpu_custom_call" | custom-call | flops 1500000000 | bytes 1048576 | tf_op jit(solution)/shard_map/prep/pallas_call | solution.py:230
  44.0 0.1 collective-permute-done.7.h3
  44.1 1.4 %collective-permute-done.6.h2 = bf16[64,1024]{1,0:T(8,128)(2,1)S(1)} collective-permute-done((bf16[64,1024]{1,0:T(8,128)(2,1)S(1)}, bf16[64,1024]{1,0:T(8,128)(2,1)S(1)}, u32[]{:S(2)}, u32[]{:S(2)}) %collective-permute-start.6) | collective-permute-done | bytes 131104 | tf_op jit(solution)/shard_map/ppermute | solution.py:472
  45.5 1.2 collective-permute-done.5.h1
  46.7 0.0 copy-done.6
  46.7 0.0 copy-start.2
  46.7 1.6 %pick.1 = (bf16[64,8,256]{2,1,0:T(8,128)(2,1)S(1)}, bf16[64,1024]{1,0:T(8,128)(2,1)S(1)}) custom-call(s32[2]{0:T(128)S(1)} %pad_add_fusion.ids, bf16[64,1024]{1,0:T(8,128)(2,1)S(1)} %edge.1.x0.after_ref, bf16[64,1024]{1,0:T(8,128)(2,1)S(1)} %collective-permute-done.2.x1, bf16[64,1024]{1,0:T(8,128)(2,1)S(1)} %collective-permute-done.3.x2, ...), custom_call_target="tpu_custom_call" | custom-call | flops 1000000000 | bytes 1048576 | tf_op jit(solution)/shard_map/pick/pallas_call | solution.py:351
  48.3 21.0 %all_to_all.10.a0 = bf16[64,8,256]{2,1,0:T(8,128)(2,1)S(1)} all-to-all(bf16[64,8,256]{2,1,0:T(8,128)(2,1)S(1)} %get-tuple-element.12), channel_id=1, replica_groups=mesh['seg'=64,'ch'=4] {'seg'}, dimensions={0} | all-to-all | bytes 524288 | tf_op jit(solution)/shard_map/all_to_all | solution.py:495
  69.4 2.1 %collective-permute-start.10 = (bf16[64,8,256]{2,1,0:T(8,128)(2,1)S(1)}, bf16[64,8,256]{2,1,0:T(8,128)(2,1)S(1)}, u32[]{:S(2)}, u32[]{:S(2)}) collective-permute-start(bf16[64,8,256]{2,1,0:T(8,128)(2,1)S(1)} %all_to_all.10.a0), channel_id=1, source_target_pairs={{2,0},{3,1},{0,2},{1,3},{6,4},{7,5},{4,6},{5,7},{10,8},{11,9},{8,1... | collective-permute-start | bytes 786440 | tf_op jit(solution)/shard_map/ppermute | solution.py:472
  71.5 1.4 %collective-permute-start.9 = (bf16[64,8,256]{2,1,0:T(8,128)(2,1)S(1)}, bf16[64,8,256]{2,1,0:T(8,128)(2,1)S(1)}, u32[]{:S(2)}, u32[]{:S(2)}) collective-permute-start(bf16[64,8,256]{2,1,0:T(8,128)(2,1)S(1)} %all_to_all.10.a0), channel_id=1, source_target_pairs={{3,0},{0,1},{1,2},{2,3},{7,4},{4,5},{5,6},{6,7},{11,8},{8,9},{9,10... | collective-permute-start | bytes 786440 | tf_op jit(solution)/shard_map/ppermute | solution.py:472
  72.9 1.8 %collective-permute-start.8 = (bf16[64,8,256]{2,1,0:T(8,128)(2,1)S(1)}, bf16[64,8,256]{2,1,0:T(8,128)(2,1)S(1)}, u32[]{:S(2)}, u32[]{:S(2)}) collective-permute-start(bf16[64,8,256]{2,1,0:T(8,128)(2,1)S(1)} %all_to_all.10.a0), channel_id=1, source_target_pairs={{1,0},{2,1},{3,2},{0,3},{5,4},{6,5},{7,6},{4,7},{9,8},{10,9},{11,1... | collective-permute-start | bytes 786440 | tf_op jit(solution)/shard_map/ppermute | solution.py:472
  74.7 5.4 %collective-permute-done.10.a3 = bf16[64,8,256]{2,1,0:T(8,128)(2,1)S(1)} collective-permute-done((bf16[64,8,256]{2,1,0:T(8,128)(2,1)S(1)}, bf16[64,8,256]{2,1,0:T(8,128)(2,1)S(1)}, u32[]{:S(2)}, u32[]{:S(2)}) %collective-permute-start.10) | collective-permute-done | bytes 262176 | tf_op jit(solution)/shard_map/ppermute | solution.py:472
  80.1 4.7 %collective-permute-done.9.a2 = bf16[64,8,256]{2,1,0:T(8,128)(2,1)S(1)} collective-permute-done((bf16[64,8,256]{2,1,0:T(8,128)(2,1)S(1)}, bf16[64,8,256]{2,1,0:T(8,128)(2,1)S(1)}, u32[]{:S(2)}, u32[]{:S(2)}) %collective-permute-start.9) | collective-permute-done | bytes 262176 | tf_op jit(solution)/shard_map/ppermute | solution.py:472
  84.8 0.1 collective-permute-done.8.a1
  84.9 0.0 copy-done.2
  84.9 19.8 %second.1 = bf16[64,16,128]{2,1,0:T(8,128)(2,1)S(1)} custom-call(s32[2]{0:T(128)S(1)} %pad_add_fusion.ids, s32[64,64]{1,0:T(8,128)S(1)} %copy-done, bf16[64,8,256]{2,1,0:T(8,128)(2,1)S(1)} %all_to_all.10.a0, bf16[64,8,256]{2,1,0:T(8,128)(2,1)S(1)} %collective-permute-done.8.a1, bf16[64,8,256]{2,1,0:T(8,128)(2,1)S(1)} %collective-permute-done.9.a2, ...), custom_call_target="tpu_custom_call" | custom-call | tf_op jit(solution)/shard_map/second/pallas_call | solution.py:407
  104.7 17.6 %all_to_all.11.back_ref = bf16[64,16,128]{2,1,0:T(8,128)(2,1)S(1)} all-to-all(bf16[64,16,128]{2,1,0:T(8,128)(2,1)S(1)} %second.1), channel_id=1, replica_groups=mesh['seg'=64,'ch'=4] {'seg'}, dimensions={0} | all-to-all | bytes 524288 | tf_op jit(solution)/shard_map/all_to_all | solution.py:497
  122.3 2.5 %home.1.h0 = bf16[64,1024]{1,0:T(8,128)(2,1)S(1)} custom-call(s32[2]{0:T(128)S(1)} %pad_add_fusion.ids, s32[64,64]{1,0:T(8,128)S(1)} %copy-done, bf16[64,16,128]{2,1,0:T(8,128)(2,1)S(1)} %all_to_all.11.back_ref, bf16[1024,1024]{1,0:T(8,128)(2,1)S(1)} %get-tuple-element.13.chosen_ref), custom_call_target="tpu_custom_call" | custom-call | tf_op jit(solution)/shard_map/home/pallas_call | solution.py:441
  124.8 2.1 %collective-permute-start.13 = (bf16[64,1024]{1,0:T(8,128)(2,1)S(1)}, bf16[64,1024]{1,0:T(8,128)(2,1)S(1)}, u32[]{:S(2)}, u32[]{:S(2)}) collective-permute-start(bf16[64,1024]{1,0:T(8,128)(2,1)S(1)} %home.1.h0), channel_id=1, source_target_pairs={{2,0},{3,1},{0,2},{1,3},{6,4},{7,5},{4,6},{5,7},{10,8},{11,9},{8,1... | collective-permute-start | bytes 393224 | tf_op jit(solution)/shard_map/ppermute | solution.py:472
  126.9 1.4 %collective-permute-start.12 = (bf16[64,1024]{1,0:T(8,128)(2,1)S(1)}, bf16[64,1024]{1,0:T(8,128)(2,1)S(1)}, u32[]{:S(2)}, u32[]{:S(2)}) collective-permute-start(bf16[64,1024]{1,0:T(8,128)(2,1)S(1)} %home.1.h0), channel_id=1, source_target_pairs={{3,0},{0,1},{1,2},{2,3},{7,4},{4,5},{5,6},{6,7},{11,8},{8,9},{9,10... | collective-permute-start | bytes 393224 | tf_op jit(solution)/shard_map/ppermute | solution.py:472
  128.4 1.8 %collective-permute-start.11 = (bf16[64,1024]{1,0:T(8,128)(2,1)S(1)}, bf16[64,1024]{1,0:T(8,128)(2,1)S(1)}, u32[]{:S(2)}, u32[]{:S(2)}) collective-permute-start(bf16[64,1024]{1,0:T(8,128)(2,1)S(1)} %home.1.h0), channel_id=1, source_target_pairs={{1,0},{2,1},{3,2},{0,3},{5,4},{6,5},{7,6},{4,7},{9,8},{10,9},{11,1... | collective-permute-start | bytes 393224 | tf_op jit(solution)/shard_map/ppermute | solution.py:472
  130.2 2.6 %collective-permute-done.13.h3 = bf16[64,1024]{1,0:T(8,128)(2,1)S(1)} collective-permute-done((bf16[64,1024]{1,0:T(8,128)(2,1)S(1)}, bf16[64,1024]{1,0:T(8,128)(2,1)S(1)}, u32[]{:S(2)}, u32[]{:S(2)}) %collective-permute-start.13) | collective-permute-done | bytes 131104 | tf_op jit(solution)/shard_map/ppermute | solution.py:472
  132.8 2.0 %collective-permute-done.12.h2 = bf16[64,1024]{1,0:T(8,128)(2,1)S(1)} collective-permute-done((bf16[64,1024]{1,0:T(8,128)(2,1)S(1)}, bf16[64,1024]{1,0:T(8,128)(2,1)S(1)}, u32[]{:S(2)}, u32[]{:S(2)}) %collective-permute-start.12) | collective-permute-done | bytes 131104 | tf_op jit(solution)/shard_map/ppermute | solution.py:472
  134.7 0.0 collective-permute-done.11.h1
  134.7 1.5 %last.1 = bf16[64,1024]{1,0:T(8,128)(2,1)} custom-call(s32[2]{0:T(128)S(1)} %pad_add_fusion.ids, bf16[64,1024]{1,0:T(8,128)(2,1)S(1)} %get-tuple-element.11.mine_ref, bf16[64,1024]{1,0:T(8,128)(2,1)S(1)} %home.1.h0, bf16[64,1024]{1,0:T(8,128)(2,1)S(1)} %collective-permute-done.11.h1, bf16[64,1024]{1,0:T(8,128)(2,1)S(1)} %collective-permute-done.12.h2, ...), custom_call_target="tpu_custom_call" | custom-call | tf_op jit(solution)/shard_map/last/pallas_call | solution.py:459
Async XLA Ops:
  0.9 15.4 %collective-permute-start.1 = (bf16[128,256]{1,0:T(8,128)(2,1)S(1)}, bf16[128,256]{1,0:T(8,128)(2,1)S(1)}, u32[]{:S(2)}, u32[]{:S(2)}) collective-permute-start(bf16[128,256]{1,0:T(8,128)(2,1)S(1)} %get-tuple-element.15), channel_id=1, source_target_pairs={{4,0},{8,4},{12,8},{16,12},{20,16},{24,20},{28,24},{32,28},{36,32}... | collective-permute-start | bytes 196616 | tf_op jit(solution)/shard_map/ppermute | solution.py:485
  8.0 8.3 %collective-permute-start = (bf16[128,256]{1,0:T(8,128)(2,1)S(1)}, bf16[128,256]{1,0:T(8,128)(2,1)S(1)}, u32[]{:S(2)}, u32[]{:S(2)}) collective-permute-start(bf16[128,256]{1,0:T(8,128)(2,1)S(1)} %get-tuple-element.16), channel_id=1, source_target_pairs={{0,4},{4,8},{8,12},{12,16},{16,20},{20,24},{24,28},{28,32},{32,36}... | collective-permute-start | bytes 196616 | tf_op jit(solution)/shard_map/ppermute | solution.py:484
  10.0 6.3 %copy-start.3 = (bf16[27,256,64]{1,2,0:T(8,128)(2,1)S(1)}, bf16[27,256,64]{1,2,0:T(8,128)(2,1)}, u32[]{:S(2)}) copy-start(bf16[27,256,64]{1,2,0:T(8,128)(2,1)} %param.13) | copy-start | bytes 2654212
  10.0 6.3 %copy-start.4 = (s32[27,1024]{1,0:T(8,128)S(1)}, s32[27,1024]{1,0:T(8,128)}, u32[]{:S(2)}) copy-start(s32[27,1024]{1,0:T(8,128)} %nb_ref.1) | copy-start | bytes 331780
  16.2 11.6 %copy-start.1 = (bf16[256,3,64]{0,2,1:T(8,128)(2,1)S(1)}, bf16[256,3,64]{0,2,1:T(8,128)(2,1)}, u32[]{:S(2)}) copy-start(bf16[256,3,64]{0,2,1:T(8,128)(2,1)} %param.14) | copy-start | bytes 294916
  16.2 26.1 %copy-start = (s32[64,64]{1,0:T(8,128)S(1)}, s32[64,64]{1,0:T(8,128)}, u32[]{:S(2)}) copy-start(s32[64,64]{1,0:T(8,128)} %counts_sm.3) | copy-start | bytes 49156
  16.2 26.1 %copy-start.5 = (bf16[256,256]{1,0:T(8,128)(2,1)S(1)}, bf16[256,256]{1,0:T(8,128)(2,1)}, u32[]{:S(2)}) copy-start(bf16[256,256]{1,0:T(8,128)(2,1)} %wo_ref.2) | copy-start | bytes 393220
  16.3 26.1 %copy-start.7 = (s32[1,1024]{1,0:T(1,128)S(1)}, s32[1,1024]{1,0:T(1,128)}, u32[]{:S(2)}) copy-start(s32[1,1024]{1,0:T(1,128)} %perm_ref.1) | copy-start | bytes 12292
  18.6 6.6 %collective-permute-start.4 = (bf16[64,1024]{1,0:T(8,128)(2,1)S(1)}, bf16[64,1024]{1,0:T(8,128)(2,1)S(1)}, u32[]{:S(2)}, u32[]{:S(2)}) collective-permute-start(bf16[64,1024]{1,0:T(8,128)(2,1)S(1)} %edge.1.x0.after_ref), channel_id=1, source_target_pairs={{2,0},{3,1},{0,2},{1,3},{6,4},{7,5},{4,6},{5,7},{10,8},{11,9},{8,1... | collective-permute-start | bytes 393224 | tf_op jit(solution)/shard_map/ppermute | solution.py:472
  21.7 6.2 %collective-permute-start.3 = (bf16[64,1024]{1,0:T(8,128)(2,1)S(1)}, bf16[64,1024]{1,0:T(8,128)(2,1)S(1)}, u32[]{:S(2)}, u32[]{:S(2)}) collective-permute-start(bf16[64,1024]{1,0:T(8,128)(2,1)S(1)} %edge.1.x0.after_ref), channel_id=1, source_target_pairs={{3,0},{0,1},{1,2},{2,3},{7,4},{4,5},{5,6},{6,7},{11,8},{8,9},{9,10... | collective-permute-start | bytes 393224 | tf_op jit(solution)/shard_map/ppermute | solution.py:472
  22.2 5.6 %collective-permute-start.2 = (bf16[64,1024]{1,0:T(8,128)(2,1)S(1)}, bf16[64,1024]{1,0:T(8,128)(2,1)S(1)}, u32[]{:S(2)}, u32[]{:S(2)}) collective-permute-start(bf16[64,1024]{1,0:T(8,128)(2,1)S(1)} %edge.1.x0.after_ref), channel_id=1, source_target_pairs={{1,0},{2,1},{3,2},{0,3},{5,4},{6,5},{7,6},{4,7},{9,8},{10,9},{11,1... | collective-permute-start | bytes 393224 | tf_op jit(solution)/shard_map/ppermute | solution.py:472
  37.5 9.2 %copy-start.6 = (bf16[256,256]{1,0:T(8,128)(2,1)S(1)}, bf16[256,256]{1,0:T(8,128)(2,1)}, u32[]{:S(2)}) copy-start(bf16[256,256]{1,0:T(8,128)(2,1)} %wo_ref.3) | copy-start | bytes 393220
  37.5 6.6 %collective-permute-start.7 = (bf16[64,1024]{1,0:T(8,128)(2,1)S(1)}, bf16[64,1024]{1,0:T(8,128)(2,1)S(1)}, u32[]{:S(2)}, u32[]{:S(2)}) collective-permute-start(bf16[64,1024]{1,0:T(8,128)(2,1)S(1)} %first.1.h0), channel_id=1, source_target_pairs={{2,0},{3,1},{0,2},{1,3},{6,4},{7,5},{4,6},{5,7},{10,8},{11,9},{8,1... | collective-permute-start | bytes 393224 | tf_op jit(solution)/shard_map/ppermute | solution.py:472
  39.1 6.4 %collective-permute-start.6 = (bf16[64,1024]{1,0:T(8,128)(2,1)S(1)}, bf16[64,1024]{1,0:T(8,128)(2,1)S(1)}, u32[]{:S(2)}, u32[]{:S(2)}) collective-permute-start(bf16[64,1024]{1,0:T(8,128)(2,1)S(1)} %first.1.h0), channel_id=1, source_target_pairs={{3,0},{0,1},{1,2},{2,3},{7,4},{4,5},{5,6},{6,7},{11,8},{8,9},{9,10... | collective-permute-start | bytes 393224 | tf_op jit(solution)/shard_map/ppermute | solution.py:472
  41.7 5.0 %collective-permute-start.5 = (bf16[64,1024]{1,0:T(8,128)(2,1)S(1)}, bf16[64,1024]{1,0:T(8,128)(2,1)S(1)}, u32[]{:S(2)}, u32[]{:S(2)}) collective-permute-start(bf16[64,1024]{1,0:T(8,128)(2,1)S(1)} %first.1.h0), channel_id=1, source_target_pairs={{1,0},{2,1},{3,2},{0,3},{5,4},{6,5},{7,6},{4,7},{9,8},{10,9},{11,1... | collective-permute-start | bytes 393224 | tf_op jit(solution)/shard_map/ppermute | solution.py:472
  46.7 38.2 %copy-start.2 = (bf16[256,3,64]{0,2,1:T(8,128)(2,1)S(1)}, bf16[256,3,64]{0,2,1:T(8,128)(2,1)}, u32[]{:S(2)}) copy-start(bf16[256,3,64]{0,2,1:T(8,128)(2,1)} %param.16) | copy-start | bytes 294916
  69.4 10.7 %collective-permute-start.10 = (bf16[64,8,256]{2,1,0:T(8,128)(2,1)S(1)}, bf16[64,8,256]{2,1,0:T(8,128)(2,1)S(1)}, u32[]{:S(2)}, u32[]{:S(2)}) collective-permute-start(bf16[64,8,256]{2,1,0:T(8,128)(2,1)S(1)} %all_to_all.10.a0), channel_id=1, source_target_pairs={{2,0},{3,1},{0,2},{1,3},{6,4},{7,5},{4,6},{5,7},{10,8},{11,9},{8,1... | collective-permute-start | bytes 786440 | tf_op jit(solution)/shard_map/ppermute | solution.py:472
  71.5 13.4 %collective-permute-start.9 = (bf16[64,8,256]{2,1,0:T(8,128)(2,1)S(1)}, bf16[64,8,256]{2,1,0:T(8,128)(2,1)S(1)}, u32[]{:S(2)}, u32[]{:S(2)}) collective-permute-start(bf16[64,8,256]{2,1,0:T(8,128)(2,1)S(1)} %all_to_all.10.a0), channel_id=1, source_target_pairs={{3,0},{0,1},{1,2},{2,3},{7,4},{4,5},{5,6},{6,7},{11,8},{8,9},{9,10... | collective-permute-start | bytes 786440 | tf_op jit(solution)/shard_map/ppermute | solution.py:472
  72.9 12.0 %collective-permute-start.8 = (bf16[64,8,256]{2,1,0:T(8,128)(2,1)S(1)}, bf16[64,8,256]{2,1,0:T(8,128)(2,1)S(1)}, u32[]{:S(2)}, u32[]{:S(2)}) collective-permute-start(bf16[64,8,256]{2,1,0:T(8,128)(2,1)S(1)} %all_to_all.10.a0), channel_id=1, source_target_pairs={{1,0},{2,1},{3,2},{0,3},{5,4},{6,5},{7,6},{4,7},{9,8},{10,9},{11,1... | collective-permute-start | bytes 786440 | tf_op jit(solution)/shard_map/ppermute | solution.py:472
  124.8 8.0 %collective-permute-start.13 = (bf16[64,1024]{1,0:T(8,128)(2,1)S(1)}, bf16[64,1024]{1,0:T(8,128)(2,1)S(1)}, u32[]{:S(2)}, u32[]{:S(2)}) collective-permute-start(bf16[64,1024]{1,0:T(8,128)(2,1)S(1)} %home.1.h0), channel_id=1, source_target_pairs={{2,0},{3,1},{0,2},{1,3},{6,4},{7,5},{4,6},{5,7},{10,8},{11,9},{8,1... | collective-permute-start | bytes 393224 | tf_op jit(solution)/shard_map/ppermute | solution.py:472
  126.9 7.8 %collective-permute-start.12 = (bf16[64,1024]{1,0:T(8,128)(2,1)S(1)}, bf16[64,1024]{1,0:T(8,128)(2,1)S(1)}, u32[]{:S(2)}, u32[]{:S(2)}) collective-permute-start(bf16[64,1024]{1,0:T(8,128)(2,1)S(1)} %home.1.h0), channel_id=1, source_target_pairs={{3,0},{0,1},{1,2},{2,3},{7,4},{4,5},{5,6},{6,7},{11,8},{8,9},{9,10... | collective-permute-start | bytes 393224 | tf_op jit(solution)/shard_map/ppermute | solution.py:472
  128.4 6.4 %collective-permute-start.11 = (bf16[64,1024]{1,0:T(8,128)(2,1)S(1)}, bf16[64,1024]{1,0:T(8,128)(2,1)S(1)}, u32[]{:S(2)}, u32[]{:S(2)}) collective-permute-start(bf16[64,1024]{1,0:T(8,128)(2,1)S(1)} %home.1.h0), channel_id=1, source_target_pairs={{1,0},{2,1},{3,2},{0,3},{5,4},{6,5},{7,6},{4,7},{9,8},{10,9},{11,1... | collective-permute-start | bytes 393224 | tf_op jit(solution)/shard_map/ppermute | solution.py:472
